TPU v7x, 32 devices: a whole 2x2x4 slice. The times are simulated.
32 devices in a mesh: dp: 2 (over x), row: 4 (over y, core), col: 4 (over z).
Axes of the slice: x: 2, y: 2, z: 4, core: 2. Of those that a mesh axis runs over, the one named last changes fastest.
Arguments:
- tokens_in: bfloat16 [16384, 1024], P(('dp', 'col'), 'row'), may hold values from -6 to 6
- cotangent: bfloat16 [16384, 1024], P(('dp', 'col'), 'row'), may hold values from -6 to 6
- doc_lengths: int32 [8, 6], P(('dp', 'row')), may hold values from 1 to 1024, 2048 in all within a row
- mixer_gain: bfloat16 [1024], P('row'), may hold values from 0.099609375 to 1.8984375
- w_query: bfloat16 [1024, 512], P('row', 'col'), may hold values from -0.1875 to 0.1875
- w_key: bfloat16 [1024, 512], P('row', 'col'), may hold values from -0.1875 to 0.1875
- w_value: bfloat16 [1024, 1024], P('row', 'col'), may hold values from -0.1875 to 0.1875
- w_outgate: bfloat16 [1024, 1024], P('row', 'col'), may hold values from -0.1875 to 0.1875
- w_rank_in: bfloat16 [1024, 16], P('row'), may hold values from -0.1875 to 0.1875
- w_rank_out: bfloat16 [16, 512], P(None, 'col'), may hold values from -1.5 to 1.5
- decay_bias: bfloat16 [512], P('col'), may hold values from -1 to 6
- head_gain: bfloat16 [256], replicated, may hold values from 0.099609375 to 1.8984375
- w_output: bfloat16 [1024, 1024], P('col', 'row'), may hold values from -0.1875 to 0.1875
- ffn_gain: bfloat16 [1024], P('row'), may hold values from 0.099609375 to 1.8984375
- w_gate: bfloat16 [1024, 2816], P('row', 'col'), may hold values from -0.1875 to 0.1875
- w_up: bfloat16 [1024, 2816], P('row', 'col'), may hold values from -0.1875 to 0.1875
- w_down: bfloat16 [2816, 1024], P('col', 'row'), may hold values from -0.109375 to 0.109375
Outputs:
- output_rows: bfloat16 [16384, 1024], P(('dp', 'col'), 'row')
- grad_tokens: float32 [16384, 1024], P(('dp', 'col'), 'row')
- grad_mixer_gain: float32 [1024], P('row')
- grad_w_query: float32 [1024, 512], P('row', 'col')
- grad_w_key: float32 [1024, 512], P('row', 'col')
- grad_w_value: float32 [1024, 1024], P('row', 'col')
- grad_w_outgate: float32 [1024, 1024], P('row', 'col')
- grad_w_rank_in: float32 [1024, 16], P('row')
- grad_w_rank_out: float32 [16, 512], P(None, 'col')
- grad_decay_bias: float32 [512], P('col')
- grad_head_gain: float32 [256], replicated
- grad_w_output: float32 [1024, 1024], P('col', 'row')
- grad_ffn_gain: float32 [1024], P('row')
- grad_w_gate: float32 [1024, 2816], P('row', 'col')
- grad_w_up: float32 [1024, 2816], P('row', 'col')
- grad_w_down: float32 [2816, 1024], P('col', 'row')
Inputs may be any that keep to these rules, and one draw needn't show every extreme that they name: `doc_lengths`: each row sums to 2048.
All inputs are finite; a program needn't handle non-finite values.
Results may differ from a plain program's by a relative error of at most 0.015.
Values may be sent and summed in bfloat16 or wider, within the bound.
No kernel may reach another device: no remote copies, remote signals or barrier semaphores. Data moves between devices by JAX's collectives and lax.ppermute only.
A program may use at most 256 MiB of HBM per device.

v0:
```python
from functools import partial

import jax
import jax.numpy as jnp
from jax import lax
from jax.sharding import PartitionSpec as P

D = 1024
DK = 512
SEQ_LEN = 2048
SPAN = 64
HK = 128
HV = 256


exact_mode = lax.Precision.HIGHEST
norm_eps = 1e-05
head_eps = 1.0
contract_rows = (((0,), (0,)), ((), ()))
contract_cols = (((1,), (1,)), ((), ()))


def product(left, right):
    return jnp.dot(left, right, preferred_element_type=jnp.float32)


def gram_of(left, right):
    return lax.dot_general(left, right, contract_rows, preferred_element_type=jnp.float32)


def times_transpose(left, weight):
    return lax.dot_general(left, weight, contract_cols, preferred_element_type=jnp.float32)


def feature_sum(vector):
    return lax.psum(vector, "row")


def col_tokens(block):
    return lax.all_gather(block, "col", axis=0, tiled=True)


def col_parts(partial_sum):
    return lax.psum_scatter(partial_sum, "col", scatter_dimension=0, tiled=True)


def data_sum(group):
    return (
        lax.psum(group[0].astype(jnp.bfloat16), "dp").astype(jnp.float32),
        lax.psum(group[1].astype(jnp.bfloat16), "dp").astype(jnp.float32),
        lax.psum(group[2].astype(jnp.bfloat16), "dp").astype(jnp.float32),
        lax.psum(group[3].astype(jnp.bfloat16), "dp").astype(jnp.float32),
        lax.psum(group[4].astype(jnp.bfloat16), "dp").astype(jnp.float32),
        lax.psum(group[5].astype(jnp.bfloat16), "dp").astype(jnp.float32),
        lax.psum(group[6].astype(jnp.bfloat16), "dp").astype(jnp.float32),
        lax.psum(group[7].astype(jnp.bfloat16), "dp").astype(jnp.float32),
    )


def segment_ids(doc_lengths, length):
    starts = jnp.cumsum(doc_lengths, axis=-1, dtype=jnp.int32) - doc_lengths
    places = jnp.arange(length, dtype=jnp.int32)
    inside = (starts[:, None, :] <= places[None, :, None]).astype(jnp.int32)
    return jnp.sum(inside, axis=-1) - 1


def span_attend(queries, key_rows, value_rows, log_decay, segments):
    batch, length, head_count, key_dim = queries.shape
    value_dim = value_rows.shape[-1]
    spans = length // SPAN
    queries = queries.reshape(batch, spans, SPAN, head_count, key_dim)
    key_rows = key_rows.reshape(batch, spans, SPAN, head_count, key_dim)
    value_rows = value_rows.reshape(batch, spans, SPAN, head_count, value_dim)
    log_decay = log_decay.reshape(batch, spans, SPAN, head_count, key_dim)
    segments = segments.reshape(batch, spans, SPAN)
    cumulative = jnp.cumsum(log_decay, axis=2)
    final_log = cumulative[:, :, -1:]
    q_scaled = queries * jnp.exp(cumulative)
    k_scaled = key_rows * jnp.exp(-cumulative)
    k_to_end = key_rows * jnp.exp(final_log - cumulative)
    places = jnp.arange(SPAN, dtype=jnp.int32)
    causal = places[:, None] >= places[None, :]
    allowed = ((segments[..., :, None] == segments[..., None, :]) & causal).astype(jnp.float32)
    scores = (
        jnp.einsum("bnihk,bnjhk->bnhij", q_scaled, k_scaled, precision=exact_mode)
        * allowed[:, :, None]
    )
    within = jnp.einsum("bnhij,bnjhv->bnihv", scores, value_rows, precision=exact_mode)
    seg_last = segments[:, :, -1]
    tail_mask = (segments == seg_last[..., None]).astype(jnp.float32)
    update = jnp.einsum(
        "bnjhk,bnjhv->bnhkv",
        k_to_end * tail_mask[..., None, None],
        value_rows,
        precision=exact_mode,
    )
    seg_prev = jnp.concatenate([jnp.full((batch, 1), -1, jnp.int32), seg_last[:, :-1]], axis=1)
    carry_on = (seg_last == seg_prev).astype(jnp.float32)
    fade_out = jnp.exp(final_log[:, :, 0])

    def advance(carried, inputs):
        fade_now, keep_now, update_now = inputs
        before = carried
        carried = carried * (fade_now * keep_now[:, None, None])[..., None] + update_now
        return (carried, before)

    start_state = jnp.zeros((batch, head_count, key_dim, value_dim), jnp.float32)
    _, states = lax.scan(
        advance,
        start_state,
        (jnp.moveaxis(fade_out, 1, 0), jnp.moveaxis(carry_on, 1, 0), jnp.moveaxis(update, 1, 0)),
    )
    states = jnp.moveaxis(states, 0, 1)
    reads_old = (segments == seg_prev[..., None]).astype(jnp.float32)
    across = jnp.einsum(
        "bnihk,bnhkv->bnihv", q_scaled * reads_old[..., None, None], states, precision=exact_mode
    )
    return (within + across).reshape(batch, length, head_count, value_dim)


def local_mixer(segments, queries, key_rows, value_rows, gate_rows, decay_pre, gain_head):
    row_count = queries.shape[0]
    head_count = queries.shape[1] // HK
    seq_count = row_count // SEQ_LEN
    log_decay = jax.nn.log_sigmoid(decay_pre) / 16.0
    attended = span_attend(
        (queries * HK ** (-0.5)).reshape(seq_count, SEQ_LEN, head_count, HK),
        key_rows.reshape(seq_count, SEQ_LEN, head_count, HK),
        value_rows.reshape(seq_count, SEQ_LEN, head_count, HV),
        log_decay.reshape(seq_count, SEQ_LEN, head_count, HK),
        segments,
    )
    attended = attended.reshape(row_count, head_count, HV)
    normed = (
        attended
        * lax.rsqrt(jnp.mean(attended * attended, axis=-1, keepdims=True) + head_eps)
        * gain_head
    )
    return normed.reshape(row_count, head_count * HV) * jax.nn.silu(gate_rows)


def per_device(
    tokens_in,
    cotangent,
    doc_lengths,
    mixer_gain,
    w_query,
    w_key,
    w_value,
    w_outgate,
    w_rank_in,
    w_rank_out,
    decay_bias,
    head_gain,
    w_output,
    ffn_gain,
    w_gate,
    w_up,
    w_down,
):
    inputs = tokens_in.astype(jnp.float32)
    inv_one = lax.rsqrt(feature_sum(jnp.sum(inputs * inputs, axis=1)) / D + norm_eps)
    normed_one = inputs * inv_one[:, None]
    gain_one = mixer_gain.astype(jnp.float32)
    first_all = col_tokens((normed_one * gain_one).astype(jnp.bfloat16))
    partials = (
        product(first_all, w_query),
        product(first_all, w_key),
        product(first_all, w_value),
        product(first_all, w_outgate),
        product(first_all, w_rank_in),
    )
    queries, key_rows, value_rows, gate_rows, rank_rows = (
        lax.psum_scatter(partials[0], "row", scatter_dimension=0, tiled=True),
        lax.psum_scatter(partials[1], "row", scatter_dimension=0, tiled=True),
        lax.psum_scatter(partials[2], "row", scatter_dimension=0, tiled=True),
        lax.psum_scatter(partials[3], "row", scatter_dimension=0, tiled=True),
        lax.psum_scatter(partials[4], "row", scatter_dimension=0, tiled=True),
    )
    rank_out = w_rank_out.astype(jnp.float32)
    decay_pre = jnp.dot(rank_rows, rank_out, precision=exact_mode) + decay_bias.astype(jnp.float32)
    segments = segment_ids(doc_lengths, SEQ_LEN)
    mixed, mixer_pull = jax.vjp(
        partial(local_mixer, segments),
        queries,
        key_rows,
        value_rows,
        gate_rows,
        decay_pre,
        head_gain.astype(jnp.float32),
    )
    heads_all = lax.all_gather(mixed.astype(jnp.bfloat16), "row", axis=0, tiled=True)
    residual = inputs + col_parts(product(heads_all, w_output))
    inv_two = lax.rsqrt(feature_sum(jnp.sum(residual * residual, axis=1)) / D + norm_eps)
    normed_two = residual * inv_two[:, None]
    gain_two = ffn_gain.astype(jnp.float32)
    second_all = col_tokens((normed_two * gain_two).astype(jnp.bfloat16))
    gate_pre, up_pre = (
        lax.psum_scatter(product(second_all, w_gate), "row", scatter_dimension=0, tiled=True),
        lax.psum_scatter(product(second_all, w_up), "row", scatter_dimension=0, tiled=True),
    )
    sigmoid_gate = jax.nn.sigmoid(gate_pre)
    silu_gate = gate_pre * sigmoid_gate
    hidden_all = lax.all_gather(
        (silu_gate * up_pre).astype(jnp.bfloat16), "row", axis=0, tiled=True
    )
    output_rows = (residual + col_parts(product(hidden_all, w_down))).astype(jnp.bfloat16)
    grad_out = cotangent.astype(jnp.float32)
    cot_all = col_tokens(cotangent)
    grad_down_w = gram_of(hidden_all, cot_all)
    hidden_grad = lax.psum_scatter(
        times_transpose(cot_all, w_down), "row", scatter_dimension=0, tiled=True
    )
    gate_grad = (
        hidden_grad * up_pre * sigmoid_gate * (1.0 + gate_pre * (1.0 - sigmoid_gate))
    ).astype(jnp.bfloat16)
    up_grad = (hidden_grad * silu_gate).astype(jnp.bfloat16)
    gate_grad_all, up_grad_all = (
        lax.all_gather(gate_grad, "row", axis=0, tiled=True),
        lax.all_gather(up_grad, "row", axis=0, tiled=True),
    )
    grad_gate_w = gram_of(second_all, gate_grad_all)
    grad_up_w = gram_of(second_all, up_grad_all)
    second_grad = col_parts(
        times_transpose(gate_grad_all, w_gate) + times_transpose(up_grad_all, w_up)
    )
    scaled_two = second_grad * gain_two
    gain_two_part = jnp.sum(second_grad * normed_two, axis=0)
    mean_two = feature_sum(jnp.sum(scaled_two * normed_two, axis=1)) / D
    resid_grad = grad_out + inv_two[:, None] * (scaled_two - normed_two * mean_two[:, None])
    resid_all = col_tokens(resid_grad.astype(jnp.bfloat16))
    grad_output_w = gram_of(heads_all, resid_all)
    mixed_grad = lax.psum_scatter(
        times_transpose(resid_all, w_output).astype(jnp.bfloat16),
        "row",
        scatter_dimension=0,
        tiled=True,
    ).astype(jnp.float32)
    query_grad, key_grad, value_grad, outgate_grad, decay_grad, head_gain_part = mixer_pull(
        mixed_grad
    )
    decay_low = decay_grad.astype(jnp.bfloat16)
    sent = (
        query_grad.astype(jnp.bfloat16),
        key_grad.astype(jnp.bfloat16),
        value_grad.astype(jnp.bfloat16),
        outgate_grad.astype(jnp.bfloat16),
        decay_low,
    )
    query_all, key_all, value_all, outgate_all, decay_all = (
        lax.all_gather(sent[0], "row", axis=0, tiled=True),
        lax.all_gather(sent[1], "row", axis=0, tiled=True),
        lax.all_gather(sent[2], "row", axis=0, tiled=True),
        lax.all_gather(sent[3], "row", axis=0, tiled=True),
        lax.all_gather(sent[4], "row", axis=0, tiled=True),
    )
    grad_query_w = gram_of(first_all, query_all)
    grad_key_w = gram_of(first_all, key_all)
    grad_value_w = gram_of(first_all, value_all)
    grad_outgate_w = gram_of(first_all, outgate_all)
    rank_grad = lax.dot_general(
        decay_all.astype(jnp.float32),
        rank_out,
        contract_cols,
        precision=exact_mode,
        preferred_element_type=jnp.float32,
    )
    rank_in_part = lax.dot_general(
        first_all.astype(jnp.float32),
        rank_grad,
        contract_rows,
        precision=exact_mode,
        preferred_element_type=jnp.float32,
    )
    decay_local = decay_low.astype(jnp.float32)
    rank_out_part = lax.dot_general(
        rank_rows,
        decay_local,
        contract_rows,
        precision=exact_mode,
        preferred_element_type=jnp.float32,
    )
    bias_part = jnp.sum(decay_local, axis=0)
    rank_back = lax.dot_general(
        rank_grad,
        w_rank_in.astype(jnp.float32),
        contract_cols,
        precision=exact_mode,
        preferred_element_type=jnp.float32,
    )
    first_grad = col_parts(
        times_transpose(query_all, w_query)
        + times_transpose(key_all, w_key)
        + times_transpose(value_all, w_value)
        + times_transpose(outgate_all, w_outgate)
        + rank_back
    )
    scaled_one = first_grad * gain_one
    gain_one_part = jnp.sum(first_grad * normed_one, axis=0)
    mean_one = feature_sum(jnp.sum(scaled_one * normed_one, axis=1)) / D
    grad_tokens = resid_grad + inv_one[:, None] * (scaled_one - normed_one * mean_one[:, None])
    every_sum = data_sum(
        (
            grad_query_w,
            grad_key_w,
            grad_value_w,
            grad_outgate_w,
            grad_output_w,
            grad_gate_w,
            grad_up_w,
            grad_down_w,
        )
    )
    (
        grad_query_w,
        grad_key_w,
        grad_value_w,
        grad_outgate_w,
        grad_output_w,
        grad_gate_w,
        grad_up_w,
        grad_down_w,
    ) = every_sum
    row_at = lax.axis_index("row")
    col_at = lax.axis_index("col")
    feature_width = mixer_gain.shape[0]
    key_width = decay_bias.shape[0]
    rank_count = w_rank_in.shape[1]
    full_one = lax.dynamic_update_slice(
        jnp.zeros((D,), jnp.float32), gain_one_part, (row_at * feature_width,)
    )
    full_two = lax.dynamic_update_slice(
        jnp.zeros((D,), jnp.float32), gain_two_part, (row_at * feature_width,)
    )
    full_rank_in = lax.dynamic_update_slice(
        jnp.zeros((D, rank_count), jnp.float32), rank_in_part, (row_at * feature_width, 0)
    )
    full_rank_out = lax.dynamic_update_slice(
        jnp.zeros((rank_count, DK), jnp.float32), rank_out_part, (0, col_at * key_width)
    )
    full_bias = lax.dynamic_update_slice(
        jnp.zeros((DK,), jnp.float32), bias_part, (col_at * key_width,)
    )
    sum_one, sum_two, sum_rank_in, sum_rank_out, sum_bias, sum_head = lax.psum(
        (full_one, full_two, full_rank_in, full_rank_out, full_bias, head_gain_part),
        ("dp", "row", "col"),
    )
    grad_mixer_gain = lax.dynamic_slice_in_dim(sum_one, row_at * feature_width, feature_width, 0)
    grad_ffn_gain = lax.dynamic_slice_in_dim(sum_two, row_at * feature_width, feature_width, 0)
    grad_rank_in = lax.dynamic_slice_in_dim(sum_rank_in, row_at * feature_width, feature_width, 0)
    grad_rank_out = lax.dynamic_slice_in_dim(sum_rank_out, col_at * key_width, key_width, 1)
    grad_bias = lax.dynamic_slice_in_dim(sum_bias, col_at * key_width, key_width, 0)
    return (
        output_rows,
        grad_tokens,
        grad_mixer_gain,
        grad_query_w,
        grad_key_w,
        grad_value_w,
        grad_outgate_w,
        grad_rank_in,
        grad_rank_out,
        grad_bias,
        sum_head,
        grad_output_w,
        grad_ffn_gain,
        grad_gate_w,
        grad_up_w,
        grad_down_w,
    )


def solution(mesh):
    in_specs = (
        P(("dp", "col"), "row"),
        P(("dp", "col"), "row"),
        P(("dp", "row"), None),
        P("row"),
        P("row", "col"),
        P("row", "col"),
        P("row", "col"),
        P("row", "col"),
        P("row", None),
        P(None, "col"),
        P("col"),
        P(),
        P("col", "row"),
        P("row"),
        P("row", "col"),
        P("row", "col"),
        P("col", "row"),
    )
    out_specs = (
        P(("dp", "col"), "row"),
        P(("dp", "col"), "row"),
        P("row"),
        P("row", "col"),
        P("row", "col"),
        P("row", "col"),
        P("row", "col"),
        P("row", None),
        P(None, "col"),
        P("col"),
        P(),
        P("col", "row"),
        P("row"),
        P("row", "col"),
        P("row", "col"),
        P("col", "row"),
    )
    return jax.shard_map(
        per_device, mesh=mesh, in_specs=in_specs, out_specs=out_specs, check_vma=False
    )
```

profile of v0, /device:TPU:0, one launch (start us, length us, event | category | flops | bytes accessed | tf_op | source)
XLA Modules:
  0.0 2682.2 jit_solution(10545545383116421357)
XLA Ops:
  21.3 81.1 %all-gather.14.cloned.1.call-done = bf16[8192,256]{1,0:T(8,128)(2,1)} async-done(((bf16[2048,256]{1,0:T(8,128)(2,1)}), bf16[8192,256]{1,0:T(8,128)(2,1)}) %all-gather.14.cloned.1.call-update) | async-done | bytes 4194320 | tf_op jit(solution)/shard_map/all_gather | solution.py:40
  144.3 29.8 %reduce-scatter.16.cloned.1.call-done = f32[2048,128]{1,0:T(8,128)} async-done(((f32[8192,128]{1,0:T(8,128)}), f32[2048,128]{1,0:T(8,128)}) %reduce-scatter.16.cloned.1.call-update) | async-done | bytes 1048592 | tf_op jit(solution)/shard_map/reduce_scatter | solution.py:174
  175.4 45.7 %reduce-scatter.20.cloned.1.call-done = f32[2048,128]{1,0:T(8,128)} async-done(((f32[8192,128]{1,0:T(8,128)}), f32[2048,128]{1,0:T(8,128)}) %reduce-scatter.20.cloned.1.call-update) | async-done | bytes 1048592 | tf_op jit(solution)/shard_map/reduce_scatter | solution.py:175
  226.3 68.6 %reduce-scatter.14.cloned.1.call-done = f32[2048,256]{1,0:T(8,128)} async-done(((f32[8192,256]{1,0:T(8,128)}), f32[2048,256]{1,0:T(8,128)}) %reduce-scatter.14.cloned.1.call-update) | async-done | bytes 2097168 | tf_op jit(solution)/shard_map/reduce_scatter | solution.py:176
  309.9 196.0 %while.36 = (s32[]{:T(128)}, f32[1,1,128,256]{3,2,1,0:T(8,128)S(1)}, f32[32,1,1,128,256]{4,3,2,1,0:T(8,128)}, f32[32,1,1,1]{0,3,2,1:T(1,128)S(1)}, f32[32,1,1,12...) while((s32[]{:T(128)}, ...), condition=%wide.region_10.11_spmd.clone, body=%wide.region_9.10_spmd.clone.sunk | while | flops 131331 | bytes 659604 | solution.py:108
  519.8 34.6 %all-gather.16.cloned.1.call-done = bf16[8192,256]{1,0:T(8,128)(2,1)} async-done(((bf16[2048,256]{1,0:T(8,128)(2,1)}), bf16[8192,256]{1,0:T(8,128)(2,1)}) %all-gather.16.cloned.1.call-update) | async-done | bytes 4194320 | tf_op jit(solution)/shard_map/all_gather | solution.py:192
  562.5 143.4 %reduce-scatter.24.cloned.1.call-done = f32[2048,256]{1,0:T(8,128)} async-done(((f32[8192,256]{1,0:T(8,128)}), f32[2048,256]{1,0:T(8,128)}) %reduce-scatter.24.cloned.1.call-update) | async-done | bytes 2097168 | tf_op jit(solution)/shard_map/reduce_scatter | solution.py:44
  719.5 69.4 %all-gather.22.cloned.1.call-done = bf16[8192,256]{1,0:T(8,128)(2,1)} async-done(((bf16[2048,256]{1,0:T(8,128)(2,1)}), bf16[8192,256]{1,0:T(8,128)(2,1)}) %all-gather.22.cloned.1.call-update) | async-done | bytes 4194320 | tf_op jit(solution)/shard_map/all_gather | solution.py:40
  803.0 66.5 %all-gather.18.cloned.1.call-done = bf16[8192,256]{1,0:T(8,128)(2,1)} async-done(((bf16[2048,256]{1,0:T(8,128)(2,1)}), bf16[8192,256]{1,0:T(8,128)(2,1)}) %all-gather.18.cloned.1.call-update) | async-done | bytes 4194320 | tf_op jit(solution)/shard_map/all_gather | solution.py:40
  903.2 130.5 %reduce-scatter.32.cloned.1.call-done = f32[2048,704]{0,1:T(8,128)} async-done(((f32[8192,704]{0,1:T(8,128)}), f32[2048,704]{0,1:T(8,128)}) %reduce-scatter.32.cloned.1.call-update) | async-done | bytes 5767184 | tf_op jit(solution)/shard_map/reduce_scatter | solution.py:211
  1033.7 165.5 %reduce-scatter.26.cloned.1.call-done = f32[2048,704]{0,1:T(8,128)} async-done(((f32[8192,704]{0,1:T(8,128)}), f32[2048,704]{0,1:T(8,128)}) %reduce-scatter.26.cloned.1.call-update) | async-done | bytes 5767184 | tf_op jit(solution)/shard_map/reduce_scatter | solution.py:199
  1199.1 165.6 %reduce-scatter.28.cloned.1.call-done = f32[2048,704]{0,1:T(8,128)} async-done(((f32[8192,704]{0,1:T(8,128)}), f32[2048,704]{0,1:T(8,128)}) %reduce-scatter.28.cloned.1.call-update) | async-done | bytes 5767184 | tf_op jit(solution)/shard_map/reduce_scatter | solution.py:200
  1376.3 75.5 %all-gather.24.cloned.1.call-done = bf16[8192,704]{0,1:T(8,128)(2,1)} async-done(((bf16[2048,704]{0,1:T(8,128)(2,1)}), bf16[8192,704]{0,1:T(8,128)(2,1)}) %all-gather.24.cloned.1.call-update) | async-done | bytes 11534352 | tf_op jit(solution)/shard_map/all_gather | solution.py:219
  1463.9 65.4 %all-gather.26.cloned.1.call-done = bf16[8192,704]{0,1:T(8,128)(2,1)} async-done(((bf16[2048,704]{0,1:T(8,128)(2,1)}), bf16[8192,704]{0,1:T(8,128)(2,1)}) %all-gather.26.cloned.1.call-update) | async-done | bytes 11534352 | tf_op jit(solution)/shard_map/all_gather | solution.py:220
  1543.1 144.7 %reduce-scatter.34.cloned.1.call-done = f32[2048,256]{1,0:T(8,128)} async-done(((f32[8192,256]{1,0:T(8,128)}), f32[2048,256]{1,0:T(8,128)}) %reduce-scatter.34.cloned.1.call-update) | async-done | bytes 2097168 | tf_op jit(solution)/shard_map/reduce_scatter | solution.py:44
  1700.2 81.2 %all-gather.28.cloned.1.call-done = bf16[8192,256]{1,0:T(8,128)(2,1)} async-done(((bf16[2048,256]{1,0:T(8,128)(2,1)}), bf16[8192,256]{1,0:T(8,128)(2,1)}) %all-gather.28.cloned.1.call-update) | async-done | bytes 4194320 | tf_op jit(solution)/shard_map/all_gather | solution.py:40
  1787.8 42.4 %reduce-scatter.36.cloned.1.call-done = bf16[2048,256]{1,0:T(8,128)(2,1)} async-done(((bf16[8192,256]{1,0:T(8,128)(2,1)}), bf16[2048,256]{1,0:T(8,128)(2,1)}) %reduce-scatter.36.cloned.1.call-update) | async-done | bytes 1048592 | tf_op jit(solution)/shard_map/reduce_scatter | solution.py:233
  1848.7 171.2 %while.37 = (s32[]{:T(128)}, f32[1,1,128,256]{3,2,1,0:T(8,128)S(1)}, f32[32,1,1,128]{3,2,1,0:T(1,128)S(1)}, f32[32,1,1,128,256]{4,3,2,1,0:T(8,128)}, f32[32,1,1,...) while((s32[]{:T(128)}, ...), condition=%wide.region_27.28_spmd.clone, body=%wide.region_25.27_spmd.clone.sunk | while | flops 196612 | bytes 1313960 | solution.py:108
  2161.6 31.1 %all-gather.36.cloned.1.call-done = bf16[8192,256]{1,0:T(8,128)(2,1)} async-done(((bf16[2048,256]{1,0:T(8,128)(2,1)}), bf16[8192,256]{1,0:T(8,128)(2,1)}) %all-gather.36.cloned.1.call-update) | async-done | bytes 4194320 | tf_op jit(solution)/shard_map/all_gather | solution.py:254
  2224.9 92.7 %all-reduce.6.cloned.1.call-done = f32[1024,16]{0,1:T(8,128)} async-done(((f32[1024,16]{0,1:T(8,128)}), f32[1024,16]{0,1:T(8,128)}) %all-reduce.6.cloned.1.call-update) | async-done | bytes 65552 | tf_op jit(solution)/shard_map/psum | solution.py:344
  2318.9 56.0 %all-reduce.8.cloned.1.call-done = (bf16[256,128]{1,0:T(8,128)(2,1)}, bf16[256,128]{1,0:T(8,128)(2,1)}, bf16[256,256]{1,0:T(8,128)(2,1)}, bf16[256,256]{1,0:T(8,...) async-done(((bf16[256,128]{1,0:T(8,128)(2,1)}, bf16[256,128]{1,0:T(8,128)(2,1)}, ...) | async-done | bytes 1605648 | tf_op jit(solution)/shard_map/psum | solution.py:49
  2386.9 134.9 %reduce-scatter.38.cloned.1.call-done = f32[2048,256]{1,0:T(8,128)} async-done(((f32[8192,256]{1,0:T(8,128)}), f32[2048,256]{1,0:T(8,128)}) %reduce-scatter.38.cloned.1.call-update) | async-done | bytes 2097168 | tf_op jit(solution)/shard_map/reduce_scatter | solution.py:44
  2524.5 46.0 %all-reduce.1 = (f32[1024]{0:T(1024)S(1)}, f32[16,512]{1,0:T(8,128)S(1)}, f32[512]{0:T(512)S(1)}, f32[256]{0:T(256)}, f32[1024]{0:T(1024)S(1)}) all-reduce(f32[1024]{0:T(1024)S(1)} %dynamic_update_slice.46, f32[16,512]{1,0:T(8,128)S(1)} %convolution_dynamic-update-slice_fusion.1, ...), channel_id=1, replica_groups=mesh['dp'=2,'row'=4,'col'=4] {'dp','row','col'}, use_global_device_ids=true, to_apply=%region_34.35 | all-reduce | flops 11008 | bytes 88064 | tf_op jit(solution)/shard_map/psum | solution.py:344
  2579.1 91.2 %reduce-scatter.30.cloned.1.call-done = f32[2048,256]{1,0:T(8,128)} async-done(((f32[8192,256]{1,0:T(8,128)}), f32[2048,256]{1,0:T(8,128)}) %reduce-scatter.30.cloned.1.call-update) | async-done | bytes 2097168 | tf_op jit(solution)/shard_map/reduce_scatter | solution.py:44
  (745 shorter events, 803.3 us)
Async XLA Ops:
  21.2 116.8 %reduce-scatter.18.cloned.1.call-start = ((), (), s32[]{:S(2)}) async-start(), calls=%async_computation.16 | async-start | bytes 655360 | tf_op jit(solution)/shard_map/reduce_scatter | solution.py:178
  112.2 108.9 %reduce-scatter.20.cloned.1.call-start = ((), (), s32[]{:S(2)}) async-start(), calls=%async_computation.17 | async-start | bytes 5242880 | tf_op jit(solution)/shard_map/reduce_scatter | solution.py:175
  118.5 176.5 %reduce-scatter.14.cloned.1.call-start = ((), (), s32[]{:S(2)}) async-start(), calls=%async_computation.14 | async-start | bytes 10485760 | tf_op jit(solution)/shard_map/reduce_scatter | solution.py:176
  126.2 390.0 %reduce-scatter.22.cloned.1.call-start = ((), (), s32[]{:S(2)}) async-start(), calls=%async_computation.18 | async-start | bytes 10485760 | tf_op jit(solution)/shard_map/reduce_scatter | solution.py:177
  137.5 416.9 %all-gather.16.cloned.1.call-start = ((), (), s32[]{:S(2)}) async-start(), calls=%async_computation.19 | async-start | bytes 5242880 | tf_op jit(solution)/shard_map/all_gather | solution.py:192
  519.7 186.2 %reduce-scatter.24.cloned.1.call-start = ((), (), s32[]{:S(2)}) async-start(), calls=%async_computation.20 | async-start | bytes 10485760 | tf_op jit(solution)/shard_map/reduce_scatter | solution.py:44
  561.1 227.7 %all-gather.22.cloned.1.call-start = ((), (), s32[]{:S(2)}) async-start(), calls=%async_computation.26 | async-start | bytes 5242880 | tf_op jit(solution)/shard_map/all_gather | solution.py:40
  561.9 307.7 %all-gather.18.cloned.1.call-start = ((), (), s32[]{:S(2)}) async-start(), calls=%async_computation.21 | async-start | bytes 5242880 | tf_op jit(solution)/shard_map/all_gather | solution.py:40
  719.0 314.6 %reduce-scatter.32.cloned.1.call-start = ((), (), s32[]{:S(2)}) async-start(), calls=%async_computation.27 | async-start | bytes 28835840 | tf_op jit(solution)/shard_map/reduce_scatter | solution.py:211
  803.0 396.2 %reduce-scatter.26.cloned.1.call-start = ((), (), s32[]{:S(2)}) async-start(), calls=%async_computation.22 | async-start | bytes 28835840 | tf_op jit(solution)/shard_map/reduce_scatter | solution.py:199
  886.2 478.6 %reduce-scatter.28.cloned.1.call-start = ((), (), s32[]{:S(2)}) async-start(), calls=%async_computation.23 | async-start | bytes 28835840 | tf_op jit(solution)/shard_map/reduce_scatter | solution.py:200
  903.1 548.7 %all-gather.24.cloned.1.call-start = ((), (), s32[]{:S(2)}) async-start(), calls=%async_computation.28 | async-start | bytes 14417920 | tf_op jit(solution)/shard_map/all_gather | solution.py:219
  1375.5 153.9 %all-gather.26.cloned.1.call-start = ((), (), s32[]{:S(2)}) async-start(), calls=%async_computation.29 | async-start | bytes 14417920 | tf_op jit(solution)/shard_map/all_gather | solution.py:220
  1376.1 311.7 %reduce-scatter.34.cloned.1.call-start = ((), (), s32[]{:S(2)}) async-start(), calls=%async_computation.30 | async-start | bytes 10485760 | tf_op jit(solution)/shard_map/reduce_scatter | solution.py:44
  1543.1 238.4 %all-gather.28.cloned.1.call-start = ((), (), s32[]{:S(2)}) async-start(), calls=%async_computation.31 | async-start | bytes 5242880 | tf_op jit(solution)/shard_map/all_gather | solution.py:40
  1700.2 130.0 %reduce-scatter.36.cloned.1.call-start = ((), (), s32[]{:S(2)}) async-start(), calls=%async_computation.32 | async-start | bytes 5242880 | tf_op jit(solution)/shard_map/reduce_scatter | solution.py:233
  1787.0 286.9 %all-gather.20.cloned.1.call-start = ((), (), s32[]{:S(2)}) async-start(), calls=%async_computation.24 | async-start | bytes 14417920 | tf_op jit(solution)/shard_map/all_gather | solution.py:204
  1787.7 297.9 %all-gather.38.cloned.1.call-start = ((), (), s32[]{:S(2)}) async-start(), calls=%async_computation.37 | async-start | bytes 2621440 | tf_op jit(solution)/shard_map/all_gather | solution.py:255
  2048.8 107.4 %all-gather.34.cloned.1.call-start = ((), (), s32[]{:S(2)}) async-start(), calls=%async_computation.35 | async-start | bytes 5242880 | tf_op jit(solution)/shard_map/all_gather | solution.py:253
  2056.6 136.0 %all-gather.36.cloned.1.call-start = ((), (), s32[]{:S(2)}) async-start(), calls=%async_computation.36 | async-start | bytes 5242880 | tf_op jit(solution)/shard_map/all_gather | solution.py:254
  2057.2 260.4 %all-reduce.6.cloned.1.call-start = ((), (), s32[]{:S(2)}) async-start(), calls=%async_computation.39 | async-start | bytes 131072 | tf_op jit(solution)/shard_map/psum | solution.py:344
  2092.5 282.4 %all-reduce.8.cloned.1.call-start = ((), (), s32[]{:S(2)}) async-start(), calls=%async_computation.40 | async-start | bytes 3211264 | tf_op jit(solution)/shard_map/psum | solution.py:49
  2198.1 323.7 %reduce-scatter.38.cloned.1.call-start = ((), (), s32[]{:S(2)}) async-start(), calls=%async_computation.38 | async-start | bytes 10485760 | tf_op jit(solution)/shard_map/reduce_scatter | solution.py:44
  2211.3 459.0 %reduce-scatter.30.cloned.1.call-start = ((), (), s32[]{:S(2)}) async-start(), calls=%async_computation.25 | async-start | bytes 10485760 | tf_op jit(solution)/shard_map/reduce_scatter | solution.py:44
  (78 other events, 6516.9 us)
Sparse Core Ops, SparseCore 0:
  21.4 81.0 all-gather.13
  129.4 44.5 reduce-scatter.15
  176.5 44.5 reduce-scatter.19
  223.5 71.3 reduce-scatter.13
  297.4 71.3 reduce-scatter.21
  519.8 34.4 all-gather.15
  561.3 144.6 reduce-scatter.23
  707.5 81.3 all-gather.21
  790.3 79.2 all-gather.17
  872.1 161.4 reduce-scatter.31
  1036.1 162.9 reduce-scatter.25
  1201.7 162.9 reduce-scatter.27
  1375.6 76.1 all-gather.23
  1453.2 76.1 all-gather.25
  1543.2 144.6 reduce-scatter.33
  1700.3 81.1 all-gather.27
  1787.1 43.0 reduce-scatter.35
  1831.7 76.0 all-gather.19
  2121.7 34.4 all-gather.33
  2158.1 34.4 all-gather.35
  2198.2 119.3 all-reduce.5
  2321.3 53.5 all-reduce.7
  2377.1 144.6 reduce-scatter.37
  2524.1 146.1 reduce-scatter.29
  (4 shorter events, 87.6 us)
where the time goes:
time: 2690 us; the launch traced here: 2680 us
  waiting for transfers between devices  1860 us (69%)
  other arithmetic  296 us (11%)
  matrix products  273 us (10%)
  local copies, waits for them, and re-layouts  158 us (6%)
  blocking collectives  74 us (3%)
    reduce_scatter x4, waiting for transfers between devices, col_parts(): return lax.psum_scatter(partial_sum, 'col', scatter_dimension=0, tiled=True)  514 us
    all_gather x4, waiting for transfers between devices, col_tokens(): return lax.all_gather(block, 'col', axis=0, tiled=True)  298 us
    reduce_scatter x1, waiting for transfers between devices, per_device(): lax.psum_scatter(product(second_all, w_up), 'row', scatter_dimension=0, t...  166 us
    reduce_scatter x1, waiting for transfers between devices, per_device(): lax.psum_scatter(product(second_all, w_gate), 'row', scatter_dimension=0,...  165 us
    reduce_scatter x1, waiting for transfers between devices, per_device(): lax.psum_scatter(times_transpose(cot_all, w_down), 'row', scatter_dimensi...  130 us
    dynamic_update_slice x128, other arithmetic, span_attend(): lax.scan(advance, start_state, (jnp.moveaxis(fade_out, 1, 0), jnp.moveaxi...  121 us
    psum x1, waiting for transfers between devices, per_device(): lax.psum((full_one, full_two, full_rank_in, full_rank_out, full_bias, hea...  92.7 us
    dynamic_slice x128, local copies, waits for them, and re-layouts, span_attend(): lax.scan(advance, start_state, (jnp.moveaxis(fade_out, 1, 0), jnp.moveaxi...  91 us
  transfers between devices with their start and end apart: 28, of which 24 were waited for; matrix products, arithmetic and copies ran while one was open for 25% of the time, Pallas kernels for 0%

commit v1 on v0

v1 whole, which is shorter than its diff:
```python
import jax
import jax.numpy as jnp
from jax import lax
from jax.experimental import pallas as pl
from jax.experimental.pallas import tpu as pltpu
from jax.sharding import PartitionSpec as P

D = 1024
SEQ_LEN = 2048
SPAN = 64
HK = 128
HV = 256
RANK = 16

exact_mode = lax.Precision.HIGHEST
norm_eps = 1e-05
head_eps = 1.0
f32 = jnp.float32
b16 = jnp.bfloat16
GRID = ("col", "row")
PACK = 2 * HK + HV + HK
NT = (((1,), (1,)), ((), ()))
TN = (((0,), (0,)), ((), ()))


def dot(left, right, dims=(((1,), (0,)), ((), ()))):
    return lax.dot_general(left, right, dims, preferred_element_type=f32)


def exchange(blocks):
    return lax.all_to_all(blocks, "row", 0, 0)


def span_parts(starts_ref, base, x):
    docs = starts_ref.shape[0]
    rows = lax.broadcasted_iota(jnp.int32, (SPAN, HK), 0) + base
    first = jnp.zeros((SPAN, HK), jnp.int32)
    last_first = jnp.int32(0)
    for d in range(docs):
        s = starts_ref[d]
        first = jnp.where(rows >= s, jnp.maximum(first, s), first)
        last_first = jnp.where(base + SPAN - 1 >= s, jnp.maximum(last_first, s), last_first)
    i = lax.broadcasted_iota(jnp.int32, (SPAN, SPAN), 0)
    j = lax.broadcasted_iota(jnp.int32, (SPAN, SPAN), 1)
    allowed = (j <= i) & (j + base >= first[:, :SPAN])
    reads = (first < base).astype(f32)
    tail = (rows >= last_first).astype(f32)
    keep = (last_first < base).astype(f32)
    q = x[:, :HK].astype(f32) * HK ** (-0.5)
    k = x[:, HK : 2 * HK].astype(f32)
    v = x[:, 2 * HK : 2 * HK + HV]
    lam = x[:, 2 * HK + HV :]
    tri = (j <= i).astype(b16)
    cum = dot(tri, lam)
    final = cum[SPAN - 1 :, :]
    e_pos = jnp.exp(cum)
    e_neg = jnp.exp(-cum)
    e_end = jnp.exp(final - cum)
    qs = (q * e_pos).astype(b16)
    ks = (k * e_neg).astype(b16)
    ke = (k * e_end * tail).astype(b16)
    qr = (qs.astype(f32) * reads).astype(b16)
    fade = jnp.exp(final) * keep
    scores = jnp.where(allowed, dot(qs, ks, NT), 0.0).astype(b16)
    return v, lam, e_pos, e_neg, e_end, qs, ks, ke, qr, fade, scores, allowed, reads, tail, i, j


def mix_forward(starts_ref, x_ref, o_ref, states_ref, carry_ref):
    step = pl.program_id(0)

    @pl.when(step == 0)
    def _():
        carry_ref[...] = jnp.zeros_like(carry_ref)

    rows = x_ref.shape[0]
    state = carry_ref[...]
    for n in range(rows // SPAN):
        at = pl.ds(n * SPAN, SPAN)
        part = span_parts(starts_ref, step * rows + n * SPAN, x_ref[at, :])
        v, ke, qr, fade, scores = part[0], part[7], part[8], part[9], part[10]
        low = state.astype(b16)
        states_ref[n] = low
        o_ref[at, :] = (dot(scores, v) + dot(qr, low, NT)).astype(b16)
        state = state * fade + dot(v, ke, TN)
    carry_ref[...] = state


def mix_backward(starts_ref, x_ref, do_ref, states_ref, out_ref, carry_ref):
    step = pl.program_id(0)
    steps = pl.num_programs(0)

    @pl.when(step == 0)
    def _():
        carry_ref[...] = jnp.zeros_like(carry_ref)

    rows = x_ref.shape[0]
    grad = carry_ref[...]
    for n in reversed(range(rows // SPAN)):
        at = pl.ds(n * SPAN, SPAN)
        (v, lam, e_pos, e_neg, e_end, qs, ks, ke, qr, fade, scores, allowed, reads, tail, i, j) = (
            span_parts(starts_ref, (steps - 1 - step) * rows + n * SPAN, x_ref[at, :])
        )
        do = do_ref[at, :]
        low = grad.astype(b16)
        before = states_ref[n]
        d_scores = jnp.where(allowed, dot(do, v, NT), 0.0).astype(b16)
        dv = dot(scores, do, TN) + dot(ke, low, NT)
        dqs = dot(d_scores, ks) + dot(do, before) * reads
        dks = dot(d_scores, qs, TN)
        dke = dot(v, low) * tail
        d_fade = jnp.sum(before.astype(f32) * grad, axis=0, keepdims=True)
        grad = grad * fade + dot(do, qr, TN)
        end_part = dke * ke.astype(f32)
        d_cum = dqs * qs.astype(f32) - dks * ks.astype(f32) - end_part
        d_final = jnp.sum(end_part, axis=0, keepdims=True) + d_fade * fade
        upper = (j >= i).astype(b16)
        high = d_cum.astype(b16)
        rest = (d_cum - high.astype(f32)).astype(b16)
        d_lam = dot(upper, high) + dot(upper, rest) + d_final
        d_zeta = d_lam * ((1.0 - jnp.exp(lam.astype(f32) * 16.0)) / 16.0)
        out_ref[at, :HK] = (dqs * e_pos * HK ** (-0.5)).astype(b16)
        out_ref[at, HK : 2 * HK] = (dks * e_neg + dke * e_end).astype(b16)
        out_ref[at, 2 * HK : 2 * HK + HV] = dv.astype(b16)
        out_ref[at, 2 * HK + HV :] = d_zeta.astype(b16)
    carry_ref[...] = grad


BLOCK = 512


def run_forward(starts, packed):
    rows = packed.shape[0]
    spans = BLOCK // SPAN
    return pl.pallas_call(
        mix_forward,
        out_shape=(
            jax.ShapeDtypeStruct((rows, HV), b16),
            jax.ShapeDtypeStruct((rows // SPAN, HV, HK), b16),
        ),
        grid=(rows // BLOCK,),
        in_specs=[
            pl.BlockSpec(memory_space=pltpu.SMEM),
            pl.BlockSpec((BLOCK, PACK), lambda s: (s, 0)),
        ],
        out_specs=(
            pl.BlockSpec((BLOCK, HV), lambda s: (s, 0)),
            pl.BlockSpec((spans, HV, HK), lambda s: (s, 0, 0)),
        ),
        scratch_shapes=[pltpu.VMEM((HV, HK), f32)],
        cost_estimate=pl.CostEstimate(
            flops=rows * 180000, bytes_accessed=rows * 2600, transcendentals=rows * 400
        ),
        name="mix_forward",
    )(starts, packed)


def run_backward(starts, packed, d_out, states):
    rows = packed.shape[0]
    spans = BLOCK // SPAN
    steps = rows // BLOCK
    return pl.pallas_call(
        mix_backward,
        out_shape=jax.ShapeDtypeStruct((rows, PACK), b16),
        grid=(steps,),
        in_specs=[
            pl.BlockSpec(memory_space=pltpu.SMEM),
            pl.BlockSpec((BLOCK, PACK), lambda s: (steps - 1 - s, 0)),
            pl.BlockSpec((BLOCK, HV), lambda s: (steps - 1 - s, 0)),
            pl.BlockSpec((spans, HV, HK), lambda s: (steps - 1 - s, 0, 0)),
        ],
        out_specs=pl.BlockSpec((BLOCK, PACK), lambda s: (steps - 1 - s, 0)),
        scratch_shapes=[pltpu.VMEM((HV, HK), f32)],
        cost_estimate=pl.CostEstimate(
            flops=rows * 500000, bytes_accessed=rows * 4200, transcendentals=rows * 600
        ),
        name="mix_backward",
    )(starts, packed, d_out, states)


def gather_blocks(block, rows, cols):
    whole = lax.all_gather(block, GRID, axis=0, tiled=True)
    return whole.reshape(cols, rows, block.shape[0], block.shape[1])


def scatter_blocks(blocks):
    flat = blocks.reshape(-1, blocks.shape[-1])
    return lax.psum_scatter(flat, GRID, scatter_dimension=0, tiled=True)


def batch_sum(part, pair):
    if pair == 2:
        other = lax.ppermute(part, "dp", [(0, 1), (1, 0)])
        return part.astype(f32) + other.astype(f32)
    return lax.psum(part, "dp").astype(f32)


def wide(blocks):
    c, r, a, b = blocks.shape
    return blocks.transpose(0, 2, 1, 3).reshape(c, a, r * b)


def split_wide(whole, r):
    c, a, b = whole.shape
    return whole.reshape(c, a, r, b // r).transpose(0, 2, 1, 3)


def make_body(dp, rows, cols):
    def per_device(
        tokens_in,
        cotangent,
        doc_lengths,
        mixer_gain,
        w_query,
        w_key,
        w_value,
        w_outgate,
        w_rank_in,
        w_rank_out,
        decay_bias,
        head_gain,
        w_output,
        ffn_gain,
        w_gate,
        w_up,
        w_down,
    ):
        feat = tokens_in.shape[1]
        count = tokens_in.shape[0] // rows
        narrow = 2 * HK + 2 * HV
        cross = [(a * cols + b, b * cols + a) for a in range(rows) for b in range(cols)]
        lengths = lax.ppermute(doc_lengths, ("row", "col"), cross)[0]
        starts = jnp.cumsum(lengths, dtype=jnp.int32) - lengths
        key_side = jnp.concatenate([w_rank_out.T, decay_bias[:, None]], axis=1)
        side = jnp.concatenate(
            [
                w_rank_in,
                mixer_gain[:, None],
                ffn_gain[:, None],
                jnp.pad(key_side, ((0, feat - HK), (0, 0))),
                jnp.zeros((feat, 128 - 2 * RANK - 3), b16),
            ],
            axis=1,
        )
        first_w = gather_blocks(
            jnp.concatenate([w_query, w_key, w_value, w_outgate, side], axis=1), rows, cols
        )
        out_w = gather_blocks(w_output, rows, cols)
        gate_w = gather_blocks(w_gate, rows, cols)
        up_w = gather_blocks(w_up, rows, cols)
        down_w = gather_blocks(w_down, rows, cols)
        extra = first_w[0, :, :, narrow:].reshape(D, 128)
        rank_in = extra[:, :RANK]
        gain_one = extra[:, RANK].astype(f32)
        gain_two = extra[:, RANK + 1].astype(f32)
        keys_extra = first_w[:, 0, :HK, narrow:]
        rank_out = keys_extra[:, :, RANK + 2 : 2 * RANK + 2].astype(f32)
        bias = keys_extra[:, :, 2 * RANK + 2].astype(f32)
        first_w = first_w.reshape(cols, D, narrow + 128)[:, :, :narrow]
        gate_w = gate_w.reshape(cols, D, -1)
        up_w = up_w.reshape(cols, D, -1)
        out_w = wide(out_w)
        down_w = wide(down_w)

        both = jnp.stack(
            [tokens_in.reshape(rows, count, feat), cotangent.reshape(rows, count, feat)], axis=1
        )
        both = exchange(both).transpose(1, 2, 0, 3).reshape(2, count, D)
        inputs = both[0].astype(f32)
        cot = both[1]
        inv_one = lax.rsqrt(jnp.mean(inputs * inputs, axis=1, keepdims=True) + norm_eps)
        normed_one = inputs * inv_one
        first = (normed_one * gain_one).astype(b16)
        proj = jnp.einsum("td,cdn->ctn", first, first_w, preferred_element_type=f32)
        rank_rows = dot(first, rank_in)
        zeta = (
            jnp.einsum("ts,cks->ctk", rank_rows, rank_out, precision=exact_mode)
            + bias[:, None, :]
        )
        lam = jax.nn.log_sigmoid(zeta) / 16.0
        gates = proj[:, :, 2 * HK + HV :]
        packed = jnp.concatenate([proj[:, :, : 2 * HK + HV], lam], axis=2).astype(b16)
        packed = exchange(packed).reshape(SEQ_LEN, PACK)
        attended, states = run_forward(starts, packed)
        heads = exchange(attended.reshape(rows, count, HV)).astype(f32)
        gain_head = head_gain.astype(f32)
        inv_head = lax.rsqrt(jnp.mean(heads * heads, axis=-1, keepdims=True) + head_eps)
        unit = heads * inv_head
        sig_out = jax.nn.sigmoid(gates)
        silu_out = gates * sig_out
        mixed = (unit * gain_head * silu_out).astype(b16)
        residual = inputs + jnp.einsum("ctv,cve->te", mixed, out_w, preferred_element_type=f32)
        inv_two = lax.rsqrt(jnp.mean(residual * residual, axis=1, keepdims=True) + norm_eps)
        normed_two = residual * inv_two
        second = (normed_two * gain_two).astype(b16)
        gate_pre = jnp.einsum("td,cdn->ctn", second, gate_w, preferred_element_type=f32)
        up_pre = jnp.einsum("td,cdn->ctn", second, up_w, preferred_element_type=f32)
        sig_gate = jax.nn.sigmoid(gate_pre)
        silu_gate = gate_pre * sig_gate
        hidden = (silu_gate * up_pre).astype(b16)

        grad_down = jnp.einsum("ctn,te->cne", hidden, cot, preferred_element_type=f32)
        grad_down = scatter_blocks(split_wide(grad_down.astype(b16), rows))
        d_hidden = jnp.einsum("te,cne->ctn", cot, down_w, preferred_element_type=f32)
        d_gate = (d_hidden * up_pre * sig_gate * (1.0 + gate_pre * (1.0 - sig_gate))).astype(b16)
        d_up = (d_hidden * silu_gate).astype(b16)
        grad_gate = jnp.einsum("td,ctn->cdn", second, d_gate, preferred_element_type=f32)
        grad_gate = scatter_blocks(grad_gate.astype(b16))
        grad_up = jnp.einsum("td,ctn->cdn", second, d_up, preferred_element_type=f32)
        grad_up = scatter_blocks(grad_up.astype(b16))
        out_rows = (
            residual + jnp.einsum("ctn,cne->te", hidden, down_w, preferred_element_type=f32)
        ).astype(b16)
        d_second = jnp.einsum(
            "ctn,cdn->td", d_gate, gate_w, preferred_element_type=f32
        ) + jnp.einsum("ctn,cdn->td", d_up, up_w, preferred_element_type=f32)
        part_two = jnp.sum(d_second * normed_two, axis=0)
        scaled_two = d_second * gain_two
        mean_two = jnp.mean(scaled_two * normed_two, axis=1, keepdims=True)
        d_resid = cot.astype(f32) + inv_two * (scaled_two - normed_two * mean_two)
        d_low = d_resid.astype(b16)
        grad_out = jnp.einsum("ctv,te->cve", mixed, d_low, preferred_element_type=f32)
        grad_out = scatter_blocks(split_wide(grad_out.astype(b16), rows))
        d_mixed = jnp.einsum("te,cve->ctv", d_low, out_w, preferred_element_type=f32)
        gated = d_mixed * silu_out
        part_head = jnp.sum(gated * unit, axis=(0, 1))
        d_gates = d_mixed * unit * gain_head * sig_out * (1.0 + gates * (1.0 - sig_out))
        d_unit = gated * gain_head
        d_heads = inv_head * (d_unit - unit * jnp.mean(d_unit * unit, axis=-1, keepdims=True))
        d_attended = exchange(d_heads.astype(b16)).reshape(SEQ_LEN, HV)
        d_packed = run_backward(starts, packed, d_attended, states)
        d_packed = exchange(d_packed.reshape(rows, count, PACK))
        d_zeta = d_packed[:, :, 2 * HK + HV :].astype(f32)
        d_proj = jnp.concatenate([d_packed[:, :, : 2 * HK + HV], d_gates.astype(b16)], axis=2)
        d_rank = jnp.einsum("ctk,cks->ts", d_zeta, rank_out, precision=exact_mode)
        d_first = jnp.einsum(
            "ctn,cdn->td", d_proj, first_w, preferred_element_type=f32
        ) + lax.dot_general(
            d_rank, rank_in.astype(f32), NT, precision=exact_mode, preferred_element_type=f32
        )
        part_one = jnp.sum(d_first * normed_one, axis=0)
        scaled_one = d_first * gain_one
        mean_one = jnp.mean(scaled_one * normed_one, axis=1, keepdims=True)
        grad_tokens = d_resid + inv_one * (scaled_one - normed_one * mean_one)
        grad_first = jnp.einsum("td,ctn->cdn", first, d_proj, preferred_element_type=f32)
        part_rank_in = lax.dot_general(
            first.astype(f32), d_rank, TN, precision=exact_mode, preferred_element_type=f32
        )
        part_rank_out = jnp.einsum("ctk,ts->cks", d_zeta, rank_rows, precision=exact_mode)
        part_bias = jnp.sum(d_zeta, axis=1)
        row_side = jnp.concatenate(
            [part_rank_in, part_one[:, None], part_two[:, None]], axis=1
        ).reshape(1, rows, feat, RANK + 2)
        col_side = jnp.concatenate([part_rank_out, part_bias[:, :, None]], axis=2)
        col_side = jnp.pad(col_side, ((0, 0), (0, feat - HK), (0, 0)))[:, None]
        gain_side = part_head.reshape(1, 1, feat, 1)
        whole = (cols, rows, feat)
        side_grad = jnp.concatenate(
            [
                jnp.broadcast_to(row_side, whole + (RANK + 2,)),
                jnp.broadcast_to(col_side, whole + (RANK + 1,)),
                jnp.broadcast_to(gain_side, whole + (1,)),
                jnp.zeros(whole + (128 - 2 * RANK - 4,), f32),
            ],
            axis=3,
        ).reshape(cols, D, 128)
        grad_first = jnp.concatenate([grad_first.astype(b16), side_grad.astype(b16)], axis=2)
        grad_first = scatter_blocks(grad_first)

        out_rows = exchange(out_rows.reshape(count, rows, feat).transpose(1, 0, 2))
        grad_tokens = exchange(
            grad_tokens.astype(b16).reshape(count, rows, feat).transpose(1, 0, 2)
        )
        grad_down = batch_sum(grad_down, dp)
        grad_gate = batch_sum(grad_gate, dp)
        grad_up = batch_sum(grad_up, dp)
        grad_out = batch_sum(grad_out, dp)
        grad_first = batch_sum(grad_first, dp)
        side_sum = grad_first[:, narrow:]
        return (
            out_rows.reshape(rows * count, feat),
            grad_tokens.reshape(rows * count, feat).astype(f32),
            side_sum[:, RANK],
            grad_first[:, :HK],
            grad_first[:, HK : 2 * HK],
            grad_first[:, 2 * HK : 2 * HK + HV],
            grad_first[:, 2 * HK + HV : narrow],
            side_sum[:, :RANK],
            side_sum[:HK, RANK + 2 : 2 * RANK + 2].T,
            side_sum[:HK, 2 * RANK + 2],
            side_sum[:, 2 * RANK + 3],
            grad_out,
            side_sum[:, RANK + 1],
            grad_gate,
            grad_up,
            grad_down,
        )

    return per_device


def solution(mesh):
    grid = P("row", "col")
    flipped = P("col", "row")
    tokens = P(("dp", "col"), "row")
    in_specs = (
        tokens,
        tokens,
        P(("dp", "row"), None),
        P("row"),
        grid,
        grid,
        grid,
        grid,
        P("row", None),
        P(None, "col"),
        P("col"),
        P(),
        flipped,
        P("row"),
        grid,
        grid,
        flipped,
    )
    out_specs = (
        tokens,
        tokens,
        P("row"),
        grid,
        grid,
        grid,
        grid,
        P("row", None),
        P(None, "col"),
        P("col"),
        P(),
        flipped,
        P("row"),
        grid,
        grid,
        flipped,
    )
    body = make_body(mesh.shape["dp"], mesh.shape["row"], mesh.shape["col"])
    return jax.shard_map(
        body, mesh=mesh, in_specs=in_specs, out_specs=out_specs, check_vma=False
    )
```

time: 2690 us -> 838 us (0.31)
  waiting for transfers between devices: 1860 us -> 456 us
  other arithmetic: 296 us -> 30.9 us
  matrix products: 273 us -> 106 us
  local copies, waits for them, and re-layouts: 158 us -> 117 us
    reduce_scatter x13 -> x5, waiting for transfers between devices: 1160 us -> 198 us  [scatter_blocks(): return lax.psum_scatter(flat, GRID, scatter_dimension=0, tiled=True)]
    all_gather x13 -> x5, waiting for transfers between devices: 545 us -> 145 us  [gather_blocks(): whole = lax.all_gather(block, GRID, axis=0, tiled=True)]
    dot_general x42 -> x21, matrix products: 273 us -> 106 us  [the longest x1 11.3 us: per_device(): jnp.einsum('te,cne->ctn', cot, down_w, preferred_element_type=f32)]
    psum x2 -> x0, waiting for transfers between devices: 149 us -> none  [the longest x1 92.7 us: per_device(): lax.psum((full_one, full_two, full_rank_in, full_rank_out, full_bias, hea...]
    dynamic_update_slice x128 -> x0, other arithmetic: 121 us -> none  [span_attend(): lax.scan(advance, start_state, (jnp.moveaxis(fade_out, 1, 0), jnp.moveaxi...]
    all_to_all x0 -> x5, waiting for transfers between devices: none -> 98.3 us  [exchange(): return lax.all_to_all(blocks, 'row', 0, 0)]
    dynamic_slice x133 -> x0, local copies, waits for them, and re-layouts: 94.8 us -> none  [the longest x128 91 us: span_attend(): lax.scan(advance, start_state, (jnp.moveaxis(fade_out, 1, 0), jnp.moveaxi...]
    psum x5 -> x0, blocking collectives: 74 us -> none  [the longest x1 46 us: per_device(): lax.psum((full_one, full_two, full_rank_in, full_rank_out, full_bias, hea...]
  transfers between devices with their start and end apart: 28 -> 21, of which waited for: 24 -> 12; matrix products, arithmetic and copies ran while one was open for 25% -> 24% of each run, Pallas kernels for 0% -> 3%
where the time goes in v1:
time: 838 us; the launch traced here: 828 us
  waiting for transfers between devices  456 us (54%)
  local copies, waits for them, and re-layouts  117 us (14%)
  matrix products  106 us (13%)
  blocking collectives  51.7 us (6%)
  other arithmetic  30.9 us (4%)
  starting transfers between devices  28.7 us (3%)
  Pallas kernels  23 us (3%)
  between operations  15 us (2%)
    reduce_scatter x5, waiting for transfers between devices, scatter_blocks(): return lax.psum_scatter(flat, GRID, scatter_dimension=0, tiled=True)  198 us
    all_gather x5, waiting for transfers between devices, gather_blocks(): whole = lax.all_gather(block, GRID, axis=0, tiled=True)  145 us
    all_to_all x5, waiting for transfers between devices, exchange(): return lax.all_to_all(blocks, 'row', 0, 0)  98.3 us
    all_to_all x2, blocking collectives, exchange(): return lax.all_to_all(blocks, 'row', 0, 0)  51.7 us
    all_to_all x5, starting transfers between devices, exchange(): return lax.all_to_all(blocks, 'row', 0, 0)  19.8 us
  transfers between devices with their start and end apart: 21, of which 12 were waited for; matrix products, arithmetic and copies ran while one was open for 24% of the time, Pallas kernels for 3%

profile of v1, /device:TPU:0, one launch (start us, length us, event | category | flops | bytes accessed | tf_op | source)
XLA Modules:
  0.0 828.2 jit_solution(10124119703835459056)
XLA Ops:
  16.5 34.6 %all_to_all.35 = bf16[4,2,512,256]{3,2,1,0:T(8,128)(2,1)S(1)} all-to-all(bf16[4,2,512,256]{3,2,1,0:T(8,128)(2,1)S(1)} %pad_maximum_fusion.3), channel_id=1, replica_groups=mesh['dp'=2,'row'=4,'col'=4] {'row'}, dimensions={0} | all-to-all | bytes 4194304 | tf_op jit(solution)/shard_map/all_to_all | solution.py:31
  54.5 31.2 %all-gather.6.cloned.1.call-done = bf16[4096,896]{1,0:T(8,128)(2,1)} async-done(((bf16[256,896]{1,0:T(8,128)(2,1)}), bf16[4096,896]{1,0:T(8,128)(2,1)}) %all-gather.6.cloned.1.call-update) | async-done | bytes 7340048 | tf_op jit(solution)/shard_map/all_gather | solution.py:181
  106.8 35.6 %all-to-all-done.1 = bf16[4,512,640]{1,2,0:T(8,128)(2,1)} async-done(((bf16[4,512,640]{1,2,0:T(8,128)(2,1)}), bf16[4,512,640]{1,2,0:T(8,128)(2,1)}, u32[]{:S(2)}, u32[]{:S(2)}) %all-to-all-start.1) | async-done | bytes 2621472 | tf_op jit(solution)/shard_map/all_to_all | solution.py:31
  146.8 9.0 %mix_forward.1 = (bf16[2048,256]{1,0:T(8,128)(2,1)}, bf16[32,256,128]{2,1,0:T(8,128)(2,1)}) custom-call(s32[6]{0:T(128)} %bitcast_subtract_fusion.starts_ref, bf16[2048,640]{1,0:T(8,128)(2,1)} %bitcast.204), custom_call_target="tpu_custom_call" | custom-call | flops 368640000 | bytes 5324800 | tf_op jit(solution)/shard_map/mix_forward/pallas_call | solution.py:134
  179.7 24.2 %all-gather.14.cloned.1.call-done = bf16[11264,256]{1,0:T(8,128)(2,1)} async-done(((bf16[704,256]{1,0:T(8,128)(2,1)}), bf16[11264,256]{1,0:T(8,128)(2,1)}) %all-gather.14.cloned.1.call-update) | async-done | bytes 5767184 | tf_op jit(solution)/shard_map/all_gather | solution.py:181
  203.9 9.5 %copy.192 = bf16[4,4,704,256]{3,1,2,0:T(4,128)(2,1)} copy(bf16[4,4,704,256]{3,2,1,0:T(8,128)(2,1)} %bitcast.222) | data formatting | bytes 11534336 | tf_op jit(solution)/shard_map/reshape | solution.py:182
  213.4 10.5 %reshape.211 = bf16[4,704,1024]{2,1,0:T(8,128)(2,1)} reshape(bf16[4,704,4,256]{3,2,1,0:T(4,128)(2,1)} %bitcast.209) | data formatting | bytes 11534336 | tf_op jit(solution)/shard_map/reshape | solution.py:199
  230.7 35.5 %all-gather.12.cloned.1.call-done = bf16[4096,704]{0,1:T(8,128)(2,1)} async-done(((bf16[256,704]{0,1:T(8,128)(2,1)}), bf16[4096,704]{0,1:T(8,128)(2,1)}) %all-gather.12.cloned.1.call-update) | async-done | bytes 5767184 | tf_op jit(solution)/shard_map/all_gather | solution.py:181
  266.3 8.6 %fusion.2 = f32[512,4,704]{0,2,1:T(8,128)} fusion(bf16[512,1024,1]{1,0,2:T(8,128)(2,1)} %fusion.51, bf16[88,4,8,1024]{3,2,1,0:T(8,128)(2,1)} %bitcast.247), kind=kOutput, calls=%fused_computation.4 | convolution fusion | flops 2952790016 | bytes 12582912 | tf_op jit(solution)/shard_map/td,cdn->ctn/dot_general | solution.py:296
  274.9 53.7 %all-gather.10.cloned.1.call-done = bf16[4096,704]{0,1:T(8,128)(2,1)} async-done(((bf16[256,704]{0,1:T(8,128)(2,1)}), bf16[4096,704]{0,1:T(8,128)(2,1)}) %all-gather.10.cloned.1.call-update) | async-done | bytes 5767184 | tf_op jit(solution)/shard_map/all_gather | solution.py:181
  328.5 8.7 %fusion.6 = f32[512,4,704]{0,2,1:T(8,128)} fusion(bf16[512,1024,1]{1,0,2:T(8,128)(2,1)} %fusion.51, bf16[88,4,8,1024]{3,2,1,0:T(8,128)(2,1)} %bitcast.251), kind=kOutput, calls=%fused_computation.8 | convolution fusion | flops 2952790016 | bytes 12582912 | tf_op jit(solution)/shard_map/td,cdn->ctn/dot_general | solution.py:295
  337.3 11.3 %fusion.10 = (bf16[4,512,704]{1,2,0:T(8,128)(2,1)S(1)}, bf16[4,512,704]{1,2,0:T(8,128)(2,1)}, bf16[4,512,704]{1,2,0:T(8,128)(2,1)S(1)}) fusion(f32[512,4,704]{0,2,1:T(8,128)} %fusion.2, f32[512,4,704]{0,2,1:T(8,128)} %fusion.6, bf16[512,1024,1]{1,0,2:T(8,128)(2,1)S(1)} %copy-done.6, bf16[4,704,1024]{2,1,0:T(8,128)(2,1)} %reshape.211), kind=kOutput, calls=%fused_computation.14 | convolution fusion | flops 2974416896 | bytes 27000832 | tf_op jit(solution)/shard_map/te,cne->ctn/dot_general | solution.py:303
  369.9 7.8 convolution_convert_fusion
  377.7 10.6 %reshape.223 = bf16[4,704,4,256]{3,2,1,0:T(4,128)(2,1)} reshape(bf16[4,704,1024]{2,1,0:T(8,128)(2,1)} %convolution_convert_fusion) | data formatting | bytes 11534336 | tf_op jit(solution)/shard_map/reshape | solution.py:204
  420.1 17.1 %all_to_all.36 = bf16[4,512,256]{1,2,0:T(8,128)(2,1)S(1)} all-to-all(bf16[4,512,256]{1,2,0:T(8,128)(2,1)S(1)} %fusion.38), channel_id=1, replica_groups=mesh['dp'=2,'row'=4,'col'=4] {'row'}, dimensions={0} | all-to-all | bytes 2097152 | tf_op jit(solution)/shard_map/all_to_all | solution.py:31
  438.5 14.0 %mix_backward.1 = bf16[2048,640]{1,0:T(8,128)(2,1)} custom-call(s32[6]{0:T(128)} %bitcast_subtract_fusion.starts_ref, bf16[2048,640]{1,0:T(8,128)(2,1)} %bitcast.205, bf16[2048,256]{1,0:T(8,128)(2,1)} %bitcast.223, bf16[32,256,128]{2,1,0:T(8,128)(2,1)} %get-tuple-element.19.states_ref), custom_call_target="tpu_custom_call" | custom-call | flops 1024000000 | bytes 8601600 | tf_op jit(solution)/shard_map/mix_backward/pallas_call | solution.py:161
  462.4 41.5 %all-to-all-done.5 = bf16[4,512,640]{2,1,0:T(8,128)(2,1)} async-done(((bf16[4,512,640]{2,1,0:T(8,128)(2,1)}), bf16[4,512,640]{2,1,0:T(8,128)(2,1)}, u32[]{:S(2)}, u32[]{:S(2)}) %all-to-all-start.5) | async-done | bytes 2621472 | tf_op jit(solution)/shard_map/all_to_all | solution.py:31
  522.8 8.4 %convert_bitcast_fusion = bf16[4,1024,768]{1,2,0:T(8,128)(2,1)} fusion(bf16[4,512,256]{2,1,0:T(8,128)(2,1)} %copy.141, bf16[4,512,512]{2,1,0:T(8,128)(2,1)} %copy-done.5, bf16[512,1024]{1,0:T(8,128)(2,1)} %copy-done.3), kind=kOutput, calls=%fused_computation.1 | convolution fusion | flops 3230662656 | bytes 10485760 | tf_op jit(solution)/shard_map/td,ctn->cdn/dot_general | solution.py:344
  537.7 11.4 %copy.147 = bf16[4,1024,896]{2,1,0:T(8,128)(2,1)} copy(bf16[4,1024,896]{1,2,0:T(8,128)(2,1)} %pad_maximum_fusion) | data formatting | bytes 14680064 | tf_op jit(solution)/shard_map/concatenate | solution.py:366
  549.2 8.0 fusion.45
  566.2 21.2 %all-to-all-done.3 = bf16[4,512,256]{2,1,0:T(8,128)(2,1)S(1)} async-done(((bf16[4,512,256]{2,1,0:T(8,128)(2,1)}), bf16[4,512,256]{2,1,0:T(8,128)(2,1)S(1)}, u32[]{:S(2)}, u32[]{:S(2)}) %all-to-all-start.3) | async-done | bytes 1048608 | tf_op jit(solution)/shard_map/all_to_all | solution.py:31
  599.9 24.5 %reduce-scatter.12.cloned.1.call-done = bf16[256,704]{0,1:T(8,128)(2,1)} async-done(((bf16[4096,704]{0,1:T(8,128)(2,1)}), bf16[256,704]{0,1:T(8,128)(2,1)}) %reduce-scatter.12.cloned.1.call-update) | async-done | bytes 360464 | tf_op jit(solution)/shard_map/reduce_scatter | solution.py:187
  627.4 81.5 %reduce-scatter.10.cloned.1.call-done = bf16[256,704]{0,1:T(8,128)(2,1)} async-done(((bf16[4096,704]{0,1:T(8,128)(2,1)}), bf16[256,704]{0,1:T(8,128)(2,1)}) %reduce-scatter.10.cloned.1.call-update) | async-done | bytes 360464 | tf_op jit(solution)/shard_map/reduce_scatter | solution.py:187
  711.3 92.3 %reduce-scatter.6.cloned.1.call-done = bf16[256,896]{1,0:T(8,128)(2,1)} async-done(((bf16[4096,896]{1,0:T(8,128)(2,1)}), bf16[256,896]{1,0:T(8,128)(2,1)}) %reduce-scatter.6.cloned.1.call-update) | async-done | bytes 458768 | tf_op jit(solution)/shard_map/reduce_scatter | solution.py:187
  (202 shorter events, 202.6 us)
Async XLA Ops:
  7.2 78.5 %all-gather.6.cloned.1.call-start = ((), (), s32[]{:S(2)}) async-start(), calls=%async_computation.12 | async-start | bytes 7798784 | tf_op jit(solution)/shard_map/all_gather | solution.py:181
  12.4 158.3 %all-gather.8.cloned.1.call-start = ((), (), s32[]{:S(2)}) async-start(), calls=%async_computation.13 | async-start | bytes 2228224 | tf_op jit(solution)/shard_map/all_gather | solution.py:181
  13.2 190.7 %all-gather.14.cloned.1.call-start = ((), (), s32[]{:S(2)}) async-start(), calls=%async_computation.16 | async-start | bytes 6127616 | tf_op jit(solution)/shard_map/all_gather | solution.py:181
  13.9 252.4 %all-gather.12.cloned.1.call-start = ((), (), s32[]{:S(2)}) async-start(), calls=%async_computation.15 | async-start | bytes 6127616 | tf_op jit(solution)/shard_map/all_gather | solution.py:181
  14.5 314.0 %all-gather.10.cloned.1.call-start = ((), (), s32[]{:S(2)}) async-start(), calls=%async_computation.14 | async-start | bytes 6127616 | tf_op jit(solution)/shard_map/all_gather | solution.py:181
  100.7 41.7 %all-to-all-start.1 = ((bf16[4,512,640]{1,2,0:T(8,128)(2,1)}), bf16[4,512,640]{1,2,0:T(8,128)(2,1)}, u32[]{:S(2)}, u32[]{:S(2)}) async-start(bf16[4,512,640]{1,2,0:T(8,128)(2,1)} %pad_maximum_fusion.2), calls=%async_computation.1 | async-start | bytes 5242880 | tf_op jit(solution)/shard_map/all_to_all | solution.py:31
  105.4 0.7 collective-permute-start
  158.1 65.8 %all-to-all-start.2 = ((bf16[4,512,256]{1,2,0:T(8,128)(2,1)}), bf16[4,512,256]{1,2,0:T(8,128)(2,1)S(1)}, u32[]{:S(2)}, u32[]{:S(2)}) async-start(bf16[4,512,256]{1,2,0:T(8,128)(2,1)} %copy.130), calls=%async_computation.2 | async-start | bytes 2097152 | tf_op jit(solution)/shard_map/all_to_all | solution.py:31
  161.6 429.4 %reduce-scatter.8.cloned.1.call-start = ((), (), s32[]{:S(2)}) async-start(), calls=%async_computation.18 | async-start | bytes 2228224 | tf_op jit(solution)/shard_map/reduce_scatter | solution.py:187
  369.9 228.8 %reduce-scatter.14.cloned.1.call-start = ((), (), s32[]{:S(2)}) async-start(), calls=%async_computation.21 | async-start | bytes 6127616 | tf_op jit(solution)/shard_map/reduce_scatter | solution.py:187
  394.5 229.8 %reduce-scatter.12.cloned.1.call-start = ((), (), s32[]{:S(2)}) async-start(), calls=%async_computation.20 | async-start | bytes 6127616 | tf_op jit(solution)/shard_map/reduce_scatter | solution.py:187
  403.6 305.3 %reduce-scatter.10.cloned.1.call-start = ((), (), s32[]{:S(2)}) async-start(), calls=%async_computation.19 | async-start | bytes 6127616 | tf_op jit(solution)/shard_map/reduce_scatter | solution.py:187
  452.5 51.4 %all-to-all-start.5 = ((bf16[4,512,640]{2,1,0:T(8,128)(2,1)}), bf16[4,512,640]{2,1,0:T(8,128)(2,1)}, u32[]{:S(2)}, u32[]{:S(2)}) async-start(bf16[4,512,640]{2,1,0:T(8,128)(2,1)} %bitcast.213), calls=%async_computation.5 | async-start | bytes 5242880 | tf_op jit(solution)/shard_map/all_to_all | solution.py:31
  457.1 346.5 %reduce-scatter.6.cloned.1.call-start = ((), (), s32[]{:S(2)}) async-start(), calls=%async_computation.17 | async-start | bytes 7798784 | tf_op jit(solution)/shard_map/reduce_scatter | solution.py:187
  558.2 29.3 %all-to-all-start.3 = ((bf16[4,512,256]{2,1,0:T(8,128)(2,1)}), bf16[4,512,256]{2,1,0:T(8,128)(2,1)S(1)}, u32[]{:S(2)}, u32[]{:S(2)}) async-start(bf16[4,512,256]{2,1,0:T(8,128)(2,1)} %bitcast.225), calls=%async_computation.3 | async-start | bytes 2097152 | tf_op jit(solution)/shard_map/all_to_all | solution.py:31
  587.5 38.4 %all-to-all-start.6 = ((bf16[4,512,256]{2,1,0:T(8,128)(2,1)}), bf16[4,512,256]{2,1,0:T(8,128)(2,1)S(1)}, u32[]{:S(2)}, u32[]{:S(2)}) async-start(bf16[4,512,256]{2,1,0:T(8,128)(2,1)} %bitcast.195), calls=%async_computation.6 | async-start | bytes 2097152 | tf_op jit(solution)/shard_map/all_to_all | solution.py:31
  591.0 6.1 collective-permute-start.2
  598.7 111.7 %copy-start.11 = (bf16[704,256]{1,0:T(8,128)(2,1)S(1)}, bf16[704,256]{1,0:T(8,128)(2,1)}, u32[]{:S(2)}) copy-start(bf16[704,256]{1,0:T(8,128)(2,1)} %reduce-scatter.14.cloned.1.call-done) | copy-start | bytes 1081348
  598.7 111.7 %collective-permute-start.5 = (bf16[704,256]{1,0:T(8,128)(2,1)}, bf16[704,256]{1,0:T(8,128)(2,1)S(1)}, u32[]{:S(2)}, u32[]{:S(2)}) collective-permute-start(bf16[704,256]{1,0:T(8,128)(2,1)} %reduce-scatter.14.cloned.1.call-done), channel_id=1, source_target_pairs={{0,16},{16,0},{1,17},{17,1},{2,18},{18,2},{3,19},{19,3},{4,20},{20... | collective-permute-start | bytes 1081352 | tf_op jit(solution)/shard_map/ppermute | solution.py:192
  624.3 180.8 %copy-start.12 = (bf16[256,704]{0,1:T(8,128)(2,1)S(1)}, bf16[256,704]{0,1:T(8,128)(2,1)}, u32[]{:S(2)}) copy-start(bf16[256,704]{0,1:T(8,128)(2,1)} %reduce-scatter.12.cloned.1.call-done) | copy-start | bytes 1081348
  624.3 180.8 %collective-permute-start.4 = (bf16[256,704]{0,1:T(8,128)(2,1)}, bf16[256,704]{0,1:T(8,128)(2,1)}, u32[]{:S(2)}, u32[]{:S(2)}) collective-permute-start(bf16[256,704]{0,1:T(8,128)(2,1)} %reduce-scatter.12.cloned.1.call-done), channel_id=1, source_target_pairs={{0,16},{16,0},{1,17},{17,1},{2,18},{18,2},{3,19},{19,3},{4,20},{20... | collective-permute-start | bytes 1081352 | tf_op jit(solution)/shard_map/ppermute | solution.py:192
  708.9 98.1 %copy-start.13 = (bf16[256,704]{0,1:T(8,128)(2,1)S(1)}, bf16[256,704]{0,1:T(8,128)(2,1)}, u32[]{:S(2)}) copy-start(bf16[256,704]{0,1:T(8,128)(2,1)} %reduce-scatter.10.cloned.1.call-done) | copy-start | bytes 1081348
  708.9 98.1 %collective-permute-start.3 = (bf16[256,704]{0,1:T(8,128)(2,1)}, bf16[256,704]{0,1:T(8,128)(2,1)S(1)}, u32[]{:S(2)}, u32[]{:S(2)}) collective-permute-start(bf16[256,704]{0,1:T(8,128)(2,1)} %reduce-scatter.10.cloned.1.call-done), channel_id=1, source_target_pairs={{0,16},{16,0},{1,17},{17,1},{2,18},{18,2},{3,19},{19,3},{4,20},{20... | collective-permute-start | bytes 1081352 | tf_op jit(solution)/shard_map/ppermute | solution.py:192
  803.6 11.9 %collective-permute-start.1 = (bf16[256,896]{1,0:T(8,128)(2,1)}, bf16[256,896]{1,0:T(8,128)(2,1)S(1)}, u32[]{:S(2)}, u32[]{:S(2)}) collective-permute-start(bf16[256,896]{1,0:T(8,128)(2,1)} %reduce-scatter.6.cloned.1.call-done), channel_id=1, source_target_pairs={{0,16},{16,0},{1,17},{17,1},{2,18},{18,2},{3,19},{19,3},{4,20},{20... | collective-permute-start | bytes 1376264 | tf_op jit(solution)/shard_map/ppermute | solution.py:192
  (28 other events, 230.3 us)
Sparse Core Ops, SparseCore 0:
  12.5 73.1 all-gather.5
  87.9 44.2 all-gather.7
  134.5 69.3 all-gather.13
  205.9 60.3 all-gather.11
  268.3 60.2 all-gather.9
  370.0 59.9 reduce-scatter.7
  433.9 96.0 reduce-scatter.13
  533.9 90.3 reduce-scatter.11
  628.2 80.6 reduce-scatter.9
  712.7 90.8 reduce-scatter.5

commit v2 on v1

--- a/solution.py
+++ b/solution.py
@@ -182,11 +182,6 @@
     return whole.reshape(cols, rows, block.shape[0], block.shape[1])
 
 
-def scatter_blocks(blocks):
-    flat = blocks.reshape(-1, blocks.shape[-1])
-    return lax.psum_scatter(flat, GRID, scatter_dimension=0, tiled=True)
-
-
 def batch_sum(part, pair):
     if pair == 2:
         other = lax.ppermute(part, "dp", [(0, 1), (1, 0)])
@@ -194,14 +189,39 @@
     return lax.psum(part, "dp").astype(f32)
 
 
-def wide(blocks):
-    c, r, a, b = blocks.shape
-    return blocks.transpose(0, 2, 1, 3).reshape(c, a, r * b)
-
-
-def split_wide(whole, r):
-    c, a, b = whole.shape
-    return whole.reshape(c, a, r, b // r).transpose(0, 2, 1, 3)
+def swap(part, bit, rows):
+    return lax.ppermute(part, "row", [(i, i ^ bit) for i in range(rows)])
+
+
+def pair_features(whole, rows):
+    feat = whole.shape[1] // rows
+    me = lax.axis_index("row")
+
+    def piece(bit):
+        return lax.dynamic_slice_in_dim(whole, (me ^ bit) * feat, feat, 1)
+
+    other = swap(jnp.stack([piece(1), piece(3)]), 1, rows)
+    keep = jnp.concatenate([piece(0), other[0]], axis=0)
+    send = jnp.concatenate([piece(2), other[1]], axis=0)
+    return keep, send
+
+
+def pair_tokens(blocks, rows):
+    return jnp.concatenate([blocks, swap(blocks, 1, rows)], axis=1)
+
+
+def weight_grad(features, blocks, rows, side=None):
+    keep, send = features
+    away = jnp.einsum("td,ctn->cdn", send, blocks, preferred_element_type=f32).astype(b16)
+    if side is not None:
+        away = jnp.concatenate([away, side[1]], axis=2)
+    came = swap(away, 2, rows)
+    held = jnp.einsum("td,ctn->cdn", keep, blocks, preferred_element_type=f32)
+    if side is not None:
+        held = jnp.concatenate([held, side[0]], axis=2)
+    total = (held + came.astype(f32)).astype(b16)
+    flat = total.reshape(-1, total.shape[-1])
+    return lax.psum_scatter(flat, "col", scatter_dimension=0, tiled=True)
 
 
 def make_body(dp, rows, cols):
@@ -244,10 +264,9 @@
         first_w = gather_blocks(
             jnp.concatenate([w_query, w_key, w_value, w_outgate, side], axis=1), rows, cols
         )
-        out_w = gather_blocks(w_output, rows, cols)
-        gate_w = gather_blocks(w_gate, rows, cols)
-        up_w = gather_blocks(w_up, rows, cols)
-        down_w = gather_blocks(w_down, rows, cols)
+        late_w = gather_blocks(
+            jnp.concatenate([w_gate, w_up, w_output.T, w_down.T], axis=1), rows, cols
+        )
         extra = first_w[0, :, :, narrow:].reshape(D, 128)
         rank_in = extra[:, :RANK]
         gain_one = extra[:, RANK].astype(f32)
@@ -256,10 +275,11 @@
         rank_out = keys_extra[:, :, RANK + 2 : 2 * RANK + 2].astype(f32)
         bias = keys_extra[:, :, 2 * RANK + 2].astype(f32)
         first_w = first_w.reshape(cols, D, narrow + 128)[:, :, :narrow]
-        gate_w = gate_w.reshape(cols, D, -1)
-        up_w = up_w.reshape(cols, D, -1)
-        out_w = wide(out_w)
-        down_w = wide(down_w)
+        late_w = late_w.reshape(cols, D, -1)
+        hid = w_gate.shape[1]
+        late_w_hid = late_w[:, :, : 2 * hid]
+        out_w = late_w[:, :, 2 * hid : 2 * hid + HV]
+        down_w = late_w[:, :, 2 * hid + HV :]
 
         both = jnp.stack(
             [tokens_in.reshape(rows, count, feat), cotangent.reshape(rows, count, feat)], axis=1
@@ -288,39 +308,35 @@
         sig_out = jax.nn.sigmoid(gates)
         silu_out = gates * sig_out
         mixed = (unit * gain_head * silu_out).astype(b16)
-        residual = inputs + jnp.einsum("ctv,cve->te", mixed, out_w, preferred_element_type=f32)
+        residual = inputs + jnp.einsum("ctv,cdv->td", mixed, out_w, preferred_element_type=f32)
         inv_two = lax.rsqrt(jnp.mean(residual * residual, axis=1, keepdims=True) + norm_eps)
         normed_two = residual * inv_two
         second = (normed_two * gain_two).astype(b16)
-        gate_pre = jnp.einsum("td,cdn->ctn", second, gate_w, preferred_element_type=f32)
-        up_pre = jnp.einsum("td,cdn->ctn", second, up_w, preferred_element_type=f32)
+        pre = jnp.einsum("td,cdn->ctn", second, late_w_hid, preferred_element_type=f32)
+        gate_pre = pre[:, :, :hid]
+        up_pre = pre[:, :, hid:]
         sig_gate = jax.nn.sigmoid(gate_pre)
         silu_gate = gate_pre * sig_gate
         hidden = (silu_gate * up_pre).astype(b16)
 
-        grad_down = jnp.einsum("ctn,te->cne", hidden, cot, preferred_element_type=f32)
-        grad_down = scatter_blocks(split_wide(grad_down.astype(b16), rows))
-        d_hidden = jnp.einsum("te,cne->ctn", cot, down_w, preferred_element_type=f32)
-        d_gate = (d_hidden * up_pre * sig_gate * (1.0 + gate_pre * (1.0 - sig_gate))).astype(b16)
-        d_up = (d_hidden * silu_gate).astype(b16)
-        grad_gate = jnp.einsum("td,ctn->cdn", second, d_gate, preferred_element_type=f32)
-        grad_gate = scatter_blocks(grad_gate.astype(b16))
-        grad_up = jnp.einsum("td,ctn->cdn", second, d_up, preferred_element_type=f32)
-        grad_up = scatter_blocks(grad_up.astype(b16))
+        cot_pair = pair_features(cot, rows)
+        grad_down = weight_grad(cot_pair, pair_tokens(hidden, rows), rows)
+        d_hidden = jnp.einsum("td,cdn->ctn", cot, down_w, preferred_element_type=f32)
+        d_gate = d_hidden * up_pre * sig_gate * (1.0 + gate_pre * (1.0 - sig_gate))
+        d_up = d_hidden * silu_gate
+        d_pre = jnp.concatenate([d_gate.astype(b16), d_up.astype(b16)], axis=2)
+        grad_hid = weight_grad(pair_features(second, rows), pair_tokens(d_pre, rows), rows)
         out_rows = (
-            residual + jnp.einsum("ctn,cne->te", hidden, down_w, preferred_element_type=f32)
+            residual + jnp.einsum("ctn,cdn->td", hidden, down_w, preferred_element_type=f32)
         ).astype(b16)
-        d_second = jnp.einsum(
-            "ctn,cdn->td", d_gate, gate_w, preferred_element_type=f32
-        ) + jnp.einsum("ctn,cdn->td", d_up, up_w, preferred_element_type=f32)
+        d_second = jnp.einsum("ctn,cdn->td", d_pre, late_w_hid, preferred_element_type=f32)
         part_two = jnp.sum(d_second * normed_two, axis=0)
         scaled_two = d_second * gain_two
         mean_two = jnp.mean(scaled_two * normed_two, axis=1, keepdims=True)
         d_resid = cot.astype(f32) + inv_two * (scaled_two - normed_two * mean_two)
         d_low = d_resid.astype(b16)
-        grad_out = jnp.einsum("ctv,te->cve", mixed, d_low, preferred_element_type=f32)
-        grad_out = scatter_blocks(split_wide(grad_out.astype(b16), rows))
-        d_mixed = jnp.einsum("te,cve->ctv", d_low, out_w, preferred_element_type=f32)
+        grad_out = weight_grad(pair_features(d_low, rows), pair_tokens(mixed, rows), rows)
+        d_mixed = jnp.einsum("td,cdv->ctv", d_low, out_w, preferred_element_type=f32)
         gated = d_mixed * silu_out
         part_head = jnp.sum(gated * unit, axis=(0, 1))
         d_gates = d_mixed * unit * gain_head * sig_out * (1.0 + gates * (1.0 - sig_out))
@@ -341,7 +357,6 @@
         scaled_one = d_first * gain_one
         mean_one = jnp.mean(scaled_one * normed_one, axis=1, keepdims=True)
         grad_tokens = d_resid + inv_one * (scaled_one - normed_one * mean_one)
-        grad_first = jnp.einsum("td,ctn->cdn", first, d_proj, preferred_element_type=f32)
         part_rank_in = lax.dot_general(
             first.astype(f32), d_rank, TN, precision=exact_mode, preferred_element_type=f32
         )
@@ -362,17 +377,25 @@
                 jnp.zeros(whole + (128 - 2 * RANK - 4,), f32),
             ],
             axis=3,
-        ).reshape(cols, D, 128)
-        grad_first = jnp.concatenate([grad_first.astype(b16), side_grad.astype(b16)], axis=2)
-        grad_first = scatter_blocks(grad_first)
+        ).astype(b16)
+        me = lax.axis_index("row")
+
+        def side_piece(bit):
+            return lax.dynamic_index_in_dim(side_grad, me ^ bit, 1, False)
+
+        side_other = swap(jnp.stack([side_piece(1), side_piece(3)]), 1, rows).astype(f32)
+        side_keep = side_piece(0).astype(f32) + side_other[0]
+        side_send = (side_piece(2).astype(f32) + side_other[1]).astype(b16)
+        grad_first = weight_grad(
+            pair_features(first, rows), pair_tokens(d_proj, rows), rows, (side_keep, side_send)
+        )
 
         out_rows = exchange(out_rows.reshape(count, rows, feat).transpose(1, 0, 2))
         grad_tokens = exchange(
             grad_tokens.astype(b16).reshape(count, rows, feat).transpose(1, 0, 2)
         )
         grad_down = batch_sum(grad_down, dp)
-        grad_gate = batch_sum(grad_gate, dp)
-        grad_up = batch_sum(grad_up, dp)
+        grad_hid = batch_sum(grad_hid, dp)
         grad_out = batch_sum(grad_out, dp)
         grad_first = batch_sum(grad_first, dp)
         side_sum = grad_first[:, narrow:]
@@ -388,11 +411,11 @@
             side_sum[:HK, RANK + 2 : 2 * RANK + 2].T,
             side_sum[:HK, 2 * RANK + 2],
             side_sum[:, 2 * RANK + 3],
-            grad_out,
+            grad_out.T,
             side_sum[:, RANK + 1],
-            grad_gate,
-            grad_up,
-            grad_down,
+            grad_hid[:, :hid],
+            grad_hid[:, hid:],
+            grad_down.T,
         )
 
     return per_device

time: 838 us -> 656 us (0.78)
  waiting for transfers between devices: 456 us -> 282 us
  blocking collectives: 51.7 us -> 34.6 us
  local copies, waits for them, and re-layouts: 117 us -> 101 us
  other arithmetic: 30.9 us -> 44.9 us
  starting transfers between devices: 28.7 us -> 37.7 us
    reduce_scatter x5 -> x4, waiting for transfers between devices: 198 us -> 0.05 us  [weight_grad(): return lax.psum_scatter(flat, 'col', scatter_dimension=0, tiled=True)]
    ppermute x0 -> x13, waiting for transfers between devices: none -> 103 us  [swap(): return lax.ppermute(part, 'row', [(i, i ^ bit) for i in range(rows)])]
    all_gather x5 -> x2, waiting for transfers between devices: 145 us -> 50.4 us  [gather_blocks(): whole = lax.all_gather(block, GRID, axis=0, tiled=True)]
    reshape x8 -> x3, local copies, waits for them, and re-layouts: 50.3 us -> 7.98 us  [weight_grad(): flat = total.reshape(-1, total.shape[-1])]
    all_gather x0 -> x1, local copies, waits for them, and re-layouts: none -> 25.1 us  [gather_blocks(): whole = lax.all_gather(block, GRID, axis=0, tiled=True)]
    all_to_all x2 -> x1, blocking collectives: 51.7 us -> 34.6 us  [exchange(): return lax.all_to_all(blocks, 'row', 0, 0)]
    ppermute x5 -> x4, waiting for transfers between devices: 12.4 us -> 26.3 us  [batch_sum(): other = lax.ppermute(part, 'dp', [(0, 1), (1, 0)])]
    concatenate x1 -> x0, local copies, waits for them, and re-layouts: 11.4 us -> none  [per_device(): jnp.concatenate([grad_first.astype(b16), side_grad.astype(b16)], axis=2)]
  transfers between devices with their start and end apart: 21 -> 30, of which waited for: 12 -> 15; matrix products, arithmetic and copies ran while one was open for 24% -> 25% of each run, Pallas kernels for 3% -> 4%
where the time goes in v2:
time: 656 us; the launch traced here: 647 us
  waiting for transfers between devices  282 us (43%)
  matrix products  108 us (16%)
  local copies, waits for them, and re-layouts  101 us (15%)
  other arithmetic  44.9 us (7%)
  starting transfers between devices  37.7 us (6%)
  blocking collectives  34.6 us (5%)
  Pallas kernels  23.1 us (4%)
  between operations  15.5 us (2%)
    ppermute x13, waiting for transfers between devices, swap(): return lax.ppermute(part, 'row', [(i, i ^ bit) for i in range(rows)])  103 us
    all_to_all x6, waiting for transfers between devices, exchange(): return lax.all_to_all(blocks, 'row', 0, 0)  101 us
    all_gather x2, waiting for transfers between devices, gather_blocks(): whole = lax.all_gather(block, GRID, axis=0, tiled=True)  50.4 us
    all_to_all x1, blocking collectives, exchange(): return lax.all_to_all(blocks, 'row', 0, 0)  34.6 us
    ppermute x4, waiting for transfers between devices, batch_sum(): other = lax.ppermute(part, 'dp', [(0, 1), (1, 0)])  26.3 us
    all_to_all x6, starting transfers between devices, exchange(): return lax.all_to_all(blocks, 'row', 0, 0)  25.3 us
    all_gather x1, local copies, waits for them, and re-layouts, gather_blocks(): whole = lax.all_gather(block, GRID, axis=0, tiled=True)  25.1 us
    dot_general x4, matrix products, weight_grad(): jnp.einsum('td,ctn->cdn', send, blocks, preferred_element_type=f32)  19.3 us
  transfers between devices with their start and end apart: 30, of which 15 were waited for; matrix products, arithmetic and copies ran while one was open for 25% of the time, Pallas kernels for 4%

profile of v2, /device:TPU:0, one launch (start us, length us, event | category | flops | bytes accessed | tf_op | source)
XLA Modules:
  0.0 647.0 jit_solution(7035578669464480269)
XLA Ops:
  16.4 34.6 %all_to_all.35 = bf16[4,2,512,256]{3,2,1,0:T(8,128)(2,1)S(1)} all-to-all(bf16[4,2,512,256]{3,2,1,0:T(8,128)(2,1)S(1)} %pad_maximum_fusion.18), channel_id=1, replica_groups=mesh['dp'=2,'row'=4,'col'=4] {'row'}, dimensions={0} | all-to-all | bytes 4194304 | tf_op jit(solution)/shard_map/all_to_all | solution.py:31
  54.3 31.4 %all-gather.3.cloned.1.call-done = bf16[4096,896]{1,0:T(8,128)(2,1)} async-done(((bf16[256,896]{1,0:T(8,128)(2,1)}), bf16[4096,896]{1,0:T(8,128)(2,1)}) %all-gather.3.cloned.1.call-update) | async-done | bytes 7340048 | tf_op jit(solution)/shard_map/all_gather | solution.py:181
  88.4 6.1 fusion.29
  106.7 55.0 %all-to-all-done.1 = bf16[4,512,640]{1,2,0:T(8,128)(2,1)} async-done(((bf16[4,512,640]{1,2,0:T(8,128)(2,1)}), bf16[4,512,640]{1,2,0:T(8,128)(2,1)}, u32[]{:S(2)}, u32[]{:S(2)}) %all-to-all-start.1) | async-done | bytes 2621472 | tf_op jit(solution)/shard_map/all_to_all | solution.py:31
  166.1 9.0 %mix_forward.1 = (bf16[2048,256]{1,0:T(8,128)(2,1)}, bf16[32,256,128]{2,1,0:T(8,128)(2,1)}) custom-call(s32[6]{0:T(128)} %bitcast_subtract_fusion.starts_ref, bf16[2048,640]{1,0:T(8,128)(2,1)} %bitcast.243), custom_call_target="tpu_custom_call" | custom-call | flops 368640000 | bytes 5324800 | tf_op jit(solution)/shard_map/mix_forward/pallas_call | solution.py:134
  189.8 17.1 %all-to-all-done.2 = bf16[4,512,256]{1,2,0:T(8,128)(2,1)S(1)} async-done(((bf16[4,512,256]{1,2,0:T(8,128)(2,1)}), bf16[4,512,256]{1,2,0:T(8,128)(2,1)S(1)}, u32[]{:S(2)}, u32[]{:S(2)}) %all-to-all-start.2) | async-done | bytes 1048608 | tf_op jit(solution)/shard_map/all_to_all | solution.py:31
  210.5 19.0 %all-gather.5.cloned.1.call-done = bf16[4096,2368]{0,1:T(8,128)(2,1)} async-done(((bf16[256,2368]{0,1:T(8,128)(2,1)}), bf16[4096,2368]{0,1:T(8,128)(2,1)}) %all-gather.5.cloned.1.call-update) | async-done | bytes 19398672 | tf_op jit(solution)/shard_map/all_gather | solution.py:181
  229.5 25.1 %copy.151 = bf16[4096,2368]{1,0:T(8,128)(2,1)} copy(bf16[4096,2368]{0,1:T(8,128)(2,1)} %all-gather.5.cloned.1.call-done) | data formatting | bytes 38797312 | tf_op jit(solution)/shard_map/all_gather | solution.py:181
  260.6 9.3 %fusion.4 = f32[4,512,1408]{1,2,0:T(8,128)S(1)} fusion(bf16[4,1024,2368]{2,1,0:T(8,128)(2,1)} %bitcast.246, bf16[512,1024]{1,0:T(8,128)(2,1)S(1)} %multiply_convert_fusion.1), kind=kOutput, calls=%fused_computation.5 | convolution fusion | flops 5905580032 | bytes 24117248 | tf_op jit(solution)/shard_map/td,cdn->ctn/dot_general | solution.py:315
  269.9 10.8 %fusion.10 = (bf16[4,512,704]{1,2,0:T(8,128)(2,1)}, bf16[4,512,704]{1,2,0:T(8,128)(2,1)}, bf16[4,512,704]{1,2,0:T(8,128)(2,1)}) fusion(f32[4,512,1408]{1,2,0:T(8,128)S(1)} %fusion.4, bf16[512,1024,1]{1,0,2:T(8,128)(2,1)S(1)} %copy-done.18, bf16[4,1024,2368]{2,1,0:T(8,128)(2,1)} %bitcast.247), kind=kOutput, calls=%fused_computation.15 | convolution fusion | flops 2974416896 | bytes 27525120 | tf_op jit(solution)/shard_map/td,cdn->ctn/dot_general | solution.py:324
  280.7 15.0 %fusion.51 = (f32[1024]{0:T(1024)}, f32[512]{0:T(512)}, f32[512,1024,1]{1,0,2:T(8,128)}) fusion(f32[512,1024]{1,0:T(8,128)} %copy-done, f32[512]{0:T(512)} %copy-done.34, f32[1024]{0:T(1024)S(1)} %get-tuple-element.93, bf16[4,1024,2368]{2,1,0:T(8,128)(2,1)} %bitcast.248, bf16[4,512,704]{1,2,0:T(8,128)(2,1)} %get-tuple-element.97, ...), kind=kOutput, calls=%fused_computation.70 | convolution fusion | flops 5920258560 | bytes 21508096 | tf_op jit(solution)/shard_map/ctn,cdn->td/dot_general | solution.py:332
  300.1 6.6 %fusion.49 = (bf16[256]{0:T(256)(128)(2,1)}, f32[4,512]{1,0:T(4,128)S(1)}, f32[4,512,256]{1,2,0:T(8,128)S(1)}, bf16[4,512,256]{1,2,0:T(8,128)(2,1)}) fusion(bf16[4,512,256]{1,2,0:T(8,128)(2,1)S(1)} %all-to-all-done.2, f32[4,512]{1,0:T(4,128)S(1)} %add_rsqrt_fusion, f32[256]{0:T(256)S(1)} %copy-done.40, f32[4,512,768]{1,2,0:T(8,128)} %copy-done.15, ...), kind=kOutput, calls=%fused_computation.62 | convolution fusion | flops 1084225280 | bytes 9455104 | tf_op jit(solution)/shard_map/td,cdv->ctv/dot_general | solution.py:339
  315.8 11.6 %all-to-all-done.4 = bf16[4,512,256]{1,2,0:T(8,128)(2,1)} async-done(((bf16[4,512,256]{1,2,0:T(8,128)(2,1)}), bf16[4,512,256]{1,2,0:T(8,128)(2,1)}, u32[]{:S(2)}, u32[]{:S(2)}) %all-to-all-start.4) | async-done | bytes 1048608 | tf_op jit(solution)/shard_map/all_to_all | solution.py:31
  329.6 14.0 %mix_backward.1 = bf16[2048,640]{1,0:T(8,128)(2,1)} custom-call(s32[6]{0:T(128)} %bitcast_subtract_fusion.starts_ref, bf16[2048,640]{1,0:T(8,128)(2,1)} %bitcast.244, bf16[2048,256]{1,0:T(8,128)(2,1)} %bitcast.265, bf16[32,256,128]{2,1,0:T(8,128)(2,1)} %get-tuple-element.19.states_ref), custom_call_target="tpu_custom_call" | custom-call | flops 1024000000 | bytes 8601600 | tf_op jit(solution)/shard_map/mix_backward/pallas_call | solution.py:161
  390.4 5.0 multiply_reduce_fusion
  413.3 20.5 %collective-permute-done.16 = bf16[4,256,704]{1,2,0:T(8,128)(2,1)} collective-permute-done((bf16[4,256,704]{1,2,0:T(8,128)(2,1)}, bf16[4,256,704]{1,2,0:T(8,128)(2,1)}, u32[]{:S(2)}, u32[]{:S(2)}) %collective-permute-start.16) | collective-permute-done | bytes 1441824 | tf_op jit(solution)/shard_map/ppermute | solution.py:193
  447.1 6.6 %fusion.27 = bf16[4,256,1408]{2,1,0:T(8,128)(2,1)} fusion(bf16[4,512,1408]{1,2,0:T(8,128)(2,1)} %collective-permute-done.10, bf16[4,512,704]{1,2,0:T(8,128)(2,1)S(1)} %copy-done.14, bf16[4,512,704]{1,2,0:T(8,128)(2,1)S(1)} %copy-done.13, bf16[512,256]{1,0:T(8,128)(2,1)S(1)} %get-tuple-element.131, bf16[512,256]{1,0:T(8,128)(2,1)} %get-tuple-element.111), kind=kOutput, calls=%fused_computation.36 | convolution fusion | flops 2989883392 | bytes 14942208 | tf_op jit(solution)/shard_map/td,ctn->cdn/dot_general | solution.py:215
  458.7 28.6 %collective-permute-done.4 = bf16[4,256,896]{1,2,0:T(8,128)(2,1)S(1)} collective-permute-done((bf16[4,256,896]{1,2,0:T(8,128)(2,1)S(1)}, bf16[4,256,896]{1,2,0:T(8,128)(2,1)S(1)}, u32[]{:S(2)}, u32[]{:S(2)}) %collective-permute-start.4) | collective-permute-done | bytes 1835040 | tf_op jit(solution)/shard_map/ppermute | solution.py:193
  493.0 54.2 %collective-permute-done.12 = bf16[4,256,1408]{2,1,0:T(8,128)(2,1)} collective-permute-done((bf16[4,256,1408]{2,1,0:T(8,128)(2,1)}, bf16[4,256,1408]{2,1,0:T(8,128)(2,1)}, u32[]{:S(2)}, u32[]{:S(2)}) %collective-permute-start.12) | collective-permute-done | bytes 2883616 | tf_op jit(solution)/shard_map/ppermute | solution.py:193
  547.2 8.1 %fusion.7 = bf16[4,256,1408]{2,1,0:T(8,128)(2,1)} fusion(bf16[4,256,1408]{2,1,0:T(8,128)(2,1)} %collective-permute-done.12, bf16[4,512,1408]{1,2,0:T(8,128)(2,1)} %collective-permute-done.10, bf16[4,512,704]{1,2,0:T(8,128)(2,1)} %get-tuple-element.97, bf16[4,512,704]{1,2,0:T(8,128)(2,1)} %get-tuple-element.96, bf16[512,256]{1,0:T(8,128)(2,1)} %get-tuple-element.130, ...), kind=kOutput, calls=%fused_computation.10 | convolution fusion | flops 2992766976 | bytes 17825792 | tf_op jit(solution)/shard_map/td,ctn->cdn/dot_general | solution.py:219
  560.0 7.8 %fusion.52 = bf16[512,1024]{1,0:T(8,128)(2,1)S(1)} fusion(f32[512,1024]{1,0:T(8,128)} %copy-done, bf16[4,512,704]{1,2,0:T(8,128)(2,1)} %get-tuple-element.98, bf16[4,1024,2368]{2,1,0:T(8,128)(2,1)} %bitcast.250), kind=kOutput, calls=%fused_computation.72 | convolution fusion | flops 2953838592 | bytes 12320768 | tf_op jit(solution)/shard_map/ctn,cdn->td/dot_general | solution.py:330
  578.1 9.5 %all-to-all-done.3 = bf16[4,512,256]{2,1,0:T(8,128)(2,1)} async-done(((bf16[4,512,256]{2,1,0:T(8,128)(2,1)}), bf16[4,512,256]{2,1,0:T(8,128)(2,1)}, u32[]{:S(2)}, u32[]{:S(2)}) %all-to-all-start.3) | async-done | bytes 1048608 | tf_op jit(solution)/shard_map/all_to_all | solution.py:31
  611.3 7.5 %collective-permute-done.5 = bf16[256,896]{1,0:T(8,128)(2,1)S(1)} collective-permute-done((bf16[256,896]{1,0:T(8,128)(2,1)}, bf16[256,896]{1,0:T(8,128)(2,1)S(1)}, u32[]{:S(2)}, u32[]{:S(2)}) %collective-permute-start.5) | collective-permute-done | bytes 458784 | tf_op jit(solution)/shard_map/ppermute | solution.py:187
  625.1 11.0 %collective-permute-done.13 = bf16[256,1408]{0,1:T(8,128)(2,1)S(1)} collective-permute-done((bf16[256,1408]{0,1:T(8,128)(2,1)}, bf16[256,1408]{0,1:T(8,128)(2,1)S(1)}, u32[]{:S(2)}, u32[]{:S(2)}) %collective-permute-start.13) | collective-permute-done | bytes 720928 | tf_op jit(solution)/shard_map/ppermute | solution.py:187
  (266 shorter events, 207.8 us)
Async XLA Ops:
  7.2 78.6 %all-gather.3.cloned.1.call-start = ((), (), s32[]{:S(2)}) async-start(), calls=%async_computation.11 | async-start | bytes 7798784 | tf_op jit(solution)/shard_map/all_gather | solution.py:181
  12.4 217.1 %all-gather.5.cloned.1.call-start = ((), (), s32[]{:S(2)}) async-start(), calls=%async_computation.12 | async-start | bytes 20611072 | tf_op jit(solution)/shard_map/all_gather | solution.py:181
  100.6 61.1 %all-to-all-start.1 = ((bf16[4,512,640]{1,2,0:T(8,128)(2,1)}), bf16[4,512,640]{1,2,0:T(8,128)(2,1)}, u32[]{:S(2)}, u32[]{:S(2)}) async-start(bf16[4,512,640]{1,2,0:T(8,128)(2,1)} %pad_maximum_fusion.15), calls=%async_computation.1 | async-start | bytes 5242880 | tf_op jit(solution)/shard_map/all_to_all | solution.py:31
  177.4 29.5 %all-to-all-start.2 = ((bf16[4,512,256]{1,2,0:T(8,128)(2,1)}), bf16[4,512,256]{1,2,0:T(8,128)(2,1)S(1)}, u32[]{:S(2)}, u32[]{:S(2)}) async-start(bf16[4,512,256]{1,2,0:T(8,128)(2,1)} %copy.150), calls=%async_computation.2 | async-start | bytes 2097152 | tf_op jit(solution)/shard_map/all_to_all | solution.py:31
  308.3 19.0 %all-to-all-start.4 = ((bf16[4,512,256]{1,2,0:T(8,128)(2,1)}), bf16[4,512,256]{1,2,0:T(8,128)(2,1)}, u32[]{:S(2)}, u32[]{:S(2)}) async-start(bf16[4,512,256]{1,2,0:T(8,128)(2,1)} %fusion.44), calls=%async_computation.4 | async-start | bytes 2097152 | tf_op jit(solution)/shard_map/all_to_all | solution.py:31
  314.7 33.6 %collective-permute-start.15 = (bf16[2,512,256]{2,1,0:T(8,128)(2,1)}, bf16[2,512,256]{2,1,0:T(8,128)(2,1)}, u32[]{:S(2)}, u32[]{:S(2)}) collective-permute-start(bf16[2,512,256]{2,1,0:T(8,128)(2,1)} %pad_maximum_fusion.48), channel_id=1, source_target_pairs={{0,4},{4,0},{8,12},{12,8},{1,5},{5,1},{9,13},{13,9},{2,6},{6,2},{1... | collective-permute-start | bytes 1572872 | tf_op jit(solution)/shard_map/ppermute | solution.py:193
  343.7 36.5 %all-to-all-start.5 = ((bf16[4,512,640]{2,1,0:T(8,128)(2,1)}), bf16[4,512,640]{2,1,0:T(8,128)(2,1)}, u32[]{:S(2)}, u32[]{:S(2)}) async-start(bf16[4,512,640]{2,1,0:T(8,128)(2,1)} %bitcast.256), calls=%async_computation.5 | async-start | bytes 5242880 | tf_op jit(solution)/shard_map/all_to_all | solution.py:31
  348.3 242.9 %reduce-scatter.7.cloned.1.call-start = ((), (), s32[]{:S(2)}) async-start(), calls=%async_computation.14 | async-start | bytes 655360 | tf_op jit(solution)/shard_map/reduce_scatter | solution.py:224
  357.0 14.8 %collective-permute-start.6 = (bf16[4,512,256]{1,2,0:T(8,128)(2,1)}, bf16[4,512,256]{1,2,0:T(8,128)(2,1)}, u32[]{:S(2)}, u32[]{:S(2)}) collective-permute-start(bf16[4,512,256]{1,2,0:T(8,128)(2,1)} %fusion.40), channel_id=1, source_target_pairs={{0,4},{4,0},{8,12},{12,8},{1,5},{5,1},{9,13},{13,9},{2,6},{6,2},{1... | collective-permute-start | bytes 3145736 | tf_op jit(solution)/shard_map/ppermute | solution.py:193
  362.5 33.0 %collective-permute-start.14 = (bf16[4,512,704]{1,2,0:T(8,128)(2,1)}, bf16[4,512,704]{1,2,0:T(8,128)(2,1)}, u32[]{:S(2)}, u32[]{:S(2)}) collective-permute-start(bf16[4,512,704]{1,2,0:T(8,128)(2,1)} %get-tuple-element.98), channel_id=1, source_target_pairs={{0,4},{4,0},{8,12},{12,8},{1,5},{5,1},{9,13},{13,9},{2,6},{6,2},{1... | collective-permute-start | bytes 8650760 | tf_op jit(solution)/shard_map/ppermute | solution.py:193
  367.3 79.8 %collective-permute-start.10 = (bf16[4,512,1408]{1,2,0:T(8,128)(2,1)}, bf16[4,512,1408]{1,2,0:T(8,128)(2,1)}, u32[]{:S(2)}, u32[]{:S(2)}) collective-permute-start(bf16[4,512,1408]{1,2,0:T(8,128)(2,1)} %pad_maximum_fusion.2), channel_id=1, source_target_pairs={{0,4},{4,0},{8,12},{12,8},{1,5},{5,1},{9,13},{13,9},{2,6},{6,2},{1... | collective-permute-start | bytes 17301512 | tf_op jit(solution)/shard_map/ppermute | solution.py:193
  374.9 27.6 %collective-permute-start.8 = (bf16[4,256,256]{2,1,0:T(8,128)(2,1)}, bf16[4,256,256]{2,1,0:T(8,128)(2,1)}, u32[]{:S(2)}, u32[]{:S(2)}) collective-permute-start(bf16[4,256,256]{2,1,0:T(8,128)(2,1)} %fusion.76), channel_id=1, source_target_pairs={{0,8},{4,12},{8,0},{12,4},{1,9},{5,13},{9,1},{13,5},{2,10},{6,14},... | collective-permute-start | bytes 1572872 | tf_op jit(solution)/shard_map/ppermute | solution.py:193
  384.0 55.3 %collective-permute-start.1 = (bf16[4,512,768]{2,1,0:T(8,128)(2,1)}, bf16[4,512,768]{2,1,0:T(8,128)(2,1)}, u32[]{:S(2)}, u32[]{:S(2)}) collective-permute-start(bf16[4,512,768]{2,1,0:T(8,128)(2,1)} %pad_maximum_fusion.14), channel_id=1, source_target_pairs={{0,4},{4,0},{8,12},{12,8},{1,5},{5,1},{9,13},{13,9},{2,6},{6,2},{1... | collective-permute-start | bytes 9437192 | tf_op jit(solution)/shard_map/ppermute | solution.py:193
  400.2 33.7 %collective-permute-start.16 = (bf16[4,256,704]{1,2,0:T(8,128)(2,1)}, bf16[4,256,704]{1,2,0:T(8,128)(2,1)}, u32[]{:S(2)}, u32[]{:S(2)}) collective-permute-start(bf16[4,256,704]{1,2,0:T(8,128)(2,1)} %fusion.68), channel_id=1, source_target_pairs={{0,8},{4,12},{8,0},{12,4},{1,9},{5,13},{9,1},{13,5},{2,10},{6,14},... | collective-permute-start | bytes 4325384 | tf_op jit(solution)/shard_map/ppermute | solution.py:193
  407.5 191.3 %reduce-scatter.11.cloned.1.call-start = ((), (), s32[]{:S(2)}) async-start(), calls=%async_computation.16 | async-start | bytes 1802240 | tf_op jit(solution)/shard_map/reduce_scatter | solution.py:224
  410.8 34.1 %collective-permute-start.11 = (bf16[2,512,256]{2,1,0:T(8,128)(2,1)}, bf16[2,512,256]{2,1,0:T(8,128)(2,1)}, u32[]{:S(2)}, u32[]{:S(2)}) collective-permute-start(bf16[2,512,256]{2,1,0:T(8,128)(2,1)} %pad_maximum_fusion.47), channel_id=1, source_target_pairs={{0,4},{4,0},{8,12},{12,8},{1,5},{5,1},{9,13},{13,9},{2,6},{6,2},{1... | collective-permute-start | bytes 1572872 | tf_op jit(solution)/shard_map/ppermute | solution.py:193
  439.2 161.1 %reduce-scatter.5.cloned.1.call-start = ((), (), s32[]{:S(2)}) async-start(), calls=%async_computation.13 | async-start | bytes 2293760 | tf_op jit(solution)/shard_map/reduce_scatter | solution.py:224
  444.3 42.9 %collective-permute-start.4 = (bf16[4,256,896]{1,2,0:T(8,128)(2,1)S(1)}, bf16[4,256,896]{1,2,0:T(8,128)(2,1)S(1)}, u32[]{:S(2)}, u32[]{:S(2)}) collective-permute-start(bf16[4,256,896]{1,2,0:T(8,128)(2,1)S(1)} %pad_maximum_fusion.22), channel_id=1, source_target_pairs={{0,8},{4,12},{8,0},{12,4},{1,9},{5,13},{9,1},{13,5},{2,10},{6,14},... | collective-permute-start | bytes 5505032 | tf_op jit(solution)/shard_map/ppermute | solution.py:193
  453.7 93.5 %collective-permute-start.12 = (bf16[4,256,1408]{2,1,0:T(8,128)(2,1)}, bf16[4,256,1408]{2,1,0:T(8,128)(2,1)}, u32[]{:S(2)}, u32[]{:S(2)}) collective-permute-start(bf16[4,256,1408]{2,1,0:T(8,128)(2,1)} %fusion.27), channel_id=1, source_target_pairs={{0,8},{4,12},{8,0},{12,4},{1,9},{5,13},{9,1},{13,5},{2,10},{6,14},... | collective-permute-start | bytes 8650760 | tf_op jit(solution)/shard_map/ppermute | solution.py:193
  492.7 126.3 %reduce-scatter.9.cloned.1.call-start = ((), (), s32[]{:S(2)}) async-start(), calls=%async_computation.15 | async-start | bytes 3604480 | tf_op jit(solution)/shard_map/reduce_scatter | solution.py:224
  568.8 18.8 %all-to-all-start.3 = ((bf16[4,512,256]{2,1,0:T(8,128)(2,1)}), bf16[4,512,256]{2,1,0:T(8,128)(2,1)}, u32[]{:S(2)}, u32[]{:S(2)}) async-start(bf16[4,512,256]{2,1,0:T(8,128)(2,1)} %bitcast.267), calls=%async_computation.3 | async-start | bytes 2097152 | tf_op jit(solution)/shard_map/all_to_all | solution.py:31
  587.6 17.9 %all-to-all-start.6 = ((bf16[4,512,256]{2,1,0:T(8,128)(2,1)}), bf16[4,512,256]{2,1,0:T(8,128)(2,1)S(1)}, u32[]{:S(2)}, u32[]{:S(2)}) async-start(bf16[4,512,256]{2,1,0:T(8,128)(2,1)} %bitcast.235), calls=%async_computation.6 | async-start | bytes 2097152 | tf_op jit(solution)/shard_map/all_to_all | solution.py:31
  600.3 18.5 %collective-permute-start.5 = (bf16[256,896]{1,0:T(8,128)(2,1)}, bf16[256,896]{1,0:T(8,128)(2,1)S(1)}, u32[]{:S(2)}, u32[]{:S(2)}) collective-permute-start(bf16[256,896]{1,0:T(8,128)(2,1)} %reduce-scatter.5.cloned.1.call-done), channel_id=1, source_target_pairs={{0,16},{16,0},{1,17},{17,1},{2,18},{18,2},{3,19},{19,3},{4,20},{20... | collective-permute-start | bytes 1376264 | tf_op jit(solution)/shard_map/ppermute | solution.py:187
  619.0 17.1 %collective-permute-start.13 = (bf16[256,1408]{0,1:T(8,128)(2,1)}, bf16[256,1408]{0,1:T(8,128)(2,1)S(1)}, u32[]{:S(2)}, u32[]{:S(2)}) collective-permute-start(bf16[256,1408]{0,1:T(8,128)(2,1)} %reduce-scatter.9.cloned.1.call-done), channel_id=1, source_target_pairs={{0,16},{16,0},{1,17},{17,1},{2,18},{18,2},{3,19},{19,3},{4,20},{20... | collective-permute-start | bytes 2162696 | tf_op jit(solution)/shard_map/ppermute | solution.py:187
  (56 other events, 491.6 us)
Sparse Core Ops, SparseCore 0:
  12.5 73.1 all-gather.2
  87.2 142.2 all-gather.4
  407.7 23.3 reduce-scatter.6
  439.3 33.4 reduce-scatter.10
  492.8 39.5 reduce-scatter.4
  560.1 56.9 reduce-scatter.8

commit v3 on v2

--- a/solution.py
+++ b/solution.py
@@ -5,8 +5,8 @@
 from jax.experimental.pallas import tpu as pltpu
 from jax.sharding import PartitionSpec as P
 
+
 D = 1024
-SEQ_LEN = 2048
 SPAN = 64
 HK = 128
 HV = 256
@@ -18,7 +18,6 @@
 f32 = jnp.float32
 b16 = jnp.bfloat16
 GRID = ("col", "row")
-PACK = 2 * HK + HV + HK
 NT = (((1,), (1,)), ((), ()))
 TN = (((0,), (0,)), ((), ()))
 
@@ -32,7 +31,7 @@
 
 
 def span_parts(starts_ref, base, x):
-    docs = starts_ref.shape[0]
+    docs = starts_ref.shape[0] - 2
     rows = lax.broadcasted_iota(jnp.int32, (SPAN, HK), 0) + base
     first = jnp.zeros((SPAN, HK), jnp.int32)
     last_first = jnp.int32(0)
@@ -65,18 +64,37 @@
     return v, lam, e_pos, e_neg, e_end, qs, ks, ke, qr, fade, scores, allowed, reads, tail, i, j
 
 
-def mix_forward(starts_ref, x_ref, o_ref, states_ref, carry_ref):
-    step = pl.program_id(0)
-
-    @pl.when(step == 0)
+def span_base(info_ref, block, n):
+    docs = info_ref.shape[0] - 2
+    return info_ref[docs] * (2 * BLOCK) + block * BLOCK + n * SPAN
+
+
+def mix_state(info_ref, x_ref, end_ref, carry_ref):
+    block = pl.program_id(1)
+
+    @pl.when(block == 0)
     def _():
         carry_ref[...] = jnp.zeros_like(carry_ref)
 
-    rows = x_ref.shape[0]
     state = carry_ref[...]
-    for n in range(rows // SPAN):
+    for n in range(BLOCK // SPAN):
+        part = span_parts(info_ref, span_base(info_ref, block, n), x_ref[pl.ds(n * SPAN, SPAN), :])
+        state = state * part[9] + dot(part[0], part[7], TN)
+    carry_ref[...] = state
+    end_ref[...] = state
+
+
+def mix_forward(info_ref, x_ref, start_ref, o_ref, states_ref, carry_ref):
+    block = pl.program_id(1)
+
+    @pl.when(block == 0)
+    def _():
+        carry_ref[...] = start_ref[...]
+
+    state = carry_ref[...]
+    for n in range(BLOCK // SPAN):
         at = pl.ds(n * SPAN, SPAN)
-        part = span_parts(starts_ref, step * rows + n * SPAN, x_ref[at, :])
+        part = span_parts(info_ref, span_base(info_ref, block, n), x_ref[at, :])
         v, ke, qr, fade, scores = part[0], part[7], part[8], part[9], part[10]
         low = state.astype(b16)
         states_ref[n] = low
@@ -85,20 +103,34 @@
     carry_ref[...] = state
 
 
-def mix_backward(starts_ref, x_ref, do_ref, states_ref, out_ref, carry_ref):
-    step = pl.program_id(0)
-    steps = pl.num_programs(0)
+def mix_grad_state(info_ref, x_ref, do_ref, end_ref, carry_ref):
+    step = pl.program_id(1)
 
     @pl.when(step == 0)
     def _():
         carry_ref[...] = jnp.zeros_like(carry_ref)
 
-    rows = x_ref.shape[0]
     grad = carry_ref[...]
-    for n in reversed(range(rows // SPAN)):
+    for n in reversed(range(BLOCK // SPAN)):
+        at = pl.ds(n * SPAN, SPAN)
+        part = span_parts(info_ref, span_base(info_ref, 1 - step, n), x_ref[at, :])
+        grad = grad * part[9] + dot(do_ref[at, :], part[8], TN)
+    carry_ref[...] = grad
+    end_ref[...] = grad
+
+
+def mix_backward(info_ref, x_ref, do_ref, states_ref, start_ref, out_ref, carry_ref):
+    step = pl.program_id(1)
+
+    @pl.when(step == 0)
+    def _():
+        carry_ref[...] = start_ref[...]
+
+    grad = carry_ref[...]
+    for n in reversed(range(BLOCK // SPAN)):
         at = pl.ds(n * SPAN, SPAN)
         (v, lam, e_pos, e_neg, e_end, qs, ks, ke, qr, fade, scores, allowed, reads, tail, i, j) = (
-            span_parts(starts_ref, (steps - 1 - step) * rows + n * SPAN, x_ref[at, :])
+            span_parts(info_ref, span_base(info_ref, 1 - step, n), x_ref[at, :])
         )
         do = do_ref[at, :]
         low = grad.astype(b16)
@@ -128,53 +160,57 @@
 BLOCK = 512
 
 
-def run_forward(starts, packed):
-    rows = packed.shape[0]
-    spans = BLOCK // SPAN
+def run_mix(kernel, reverse, work, info, operands, results):
+    heads = operands[0].shape[1]
+
+    def order(step):
+        return 1 - step if reverse else step
+
+    def spec(array):
+        if len(array.shape) == 4:
+            return pl.BlockSpec(
+                (None, None) + array.shape[2:],
+                lambda h, s, info_ref: (order(s) ^ info_ref[info_ref.shape[0] - 1], h, 0, 0),
+            )
+        if len(array.shape) == 5:
+            return pl.BlockSpec(
+                (None, None) + array.shape[2:], lambda h, s, info_ref: (order(s), h, 0, 0, 0)
+            )
+        return pl.BlockSpec((None,) + array.shape[1:], lambda h, s, info_ref: (h, 0, 0))
+
     return pl.pallas_call(
-        mix_forward,
-        out_shape=(
-            jax.ShapeDtypeStruct((rows, HV), b16),
-            jax.ShapeDtypeStruct((rows // SPAN, HV, HK), b16),
+        kernel,
+        out_shape=results,
+        grid_spec=pltpu.PrefetchScalarGridSpec(
+            num_scalar_prefetch=1,
+            grid=(heads, 2),
+            in_specs=[spec(array) for array in operands],
+            out_specs=tuple(spec(array) for array in results),
+            scratch_shapes=[pltpu.VMEM((HV, HK), f32)],
         ),
-        grid=(rows // BLOCK,),
-        in_specs=[
-            pl.BlockSpec(memory_space=pltpu.SMEM),
-            pl.BlockSpec((BLOCK, PACK), lambda s: (s, 0)),
-        ],
-        out_specs=(
-            pl.BlockSpec((BLOCK, HV), lambda s: (s, 0)),
-            pl.BlockSpec((spans, HV, HK), lambda s: (s, 0, 0)),
+        cost_estimate=pl.CostEstimate(
+            flops=work * 200000000, bytes_accessed=work * 4000000, transcendentals=work * 800000
         ),
-        scratch_shapes=[pltpu.VMEM((HV, HK), f32)],
-        cost_estimate=pl.CostEstimate(
-            flops=rows * 180000, bytes_accessed=rows * 2600, transcendentals=rows * 400
-        ),
-        name="mix_forward",
-    )(starts, packed)
-
-
-def run_backward(starts, packed, d_out, states):
-    rows = packed.shape[0]
-    spans = BLOCK // SPAN
-    steps = rows // BLOCK
-    return pl.pallas_call(
-        mix_backward,
-        out_shape=jax.ShapeDtypeStruct((rows, PACK), b16),
-        grid=(steps,),
-        in_specs=[
-            pl.BlockSpec(memory_space=pltpu.SMEM),
-            pl.BlockSpec((BLOCK, PACK), lambda s: (steps - 1 - s, 0)),
-            pl.BlockSpec((BLOCK, HV), lambda s: (steps - 1 - s, 0)),
-            pl.BlockSpec((spans, HV, HK), lambda s: (steps - 1 - s, 0, 0)),
-        ],
-        out_specs=pl.BlockSpec((BLOCK, PACK), lambda s: (steps - 1 - s, 0)),
-        scratch_shapes=[pltpu.VMEM((HV, HK), f32)],
-        cost_estimate=pl.CostEstimate(
-            flops=rows * 500000, bytes_accessed=rows * 4200, transcendentals=rows * 600
-        ),
-        name="mix_backward",
-    )(starts, packed, d_out, states)
+    )(info, *operands)
+
+
+def run_forward(info, packed, rows):
+    pairs, heads, count = packed.shape[:3]
+    state = jax.ShapeDtypeStruct((heads, HV, HK), f32)
+    (end,) = run_mix(mix_state, False, 1, info, (packed,), (state,))
+    begin = lax.ppermute(end, "row", [(0, 2), (1, 3)]) if rows else jnp.zeros_like(end)
+    out = jax.ShapeDtypeStruct((pairs, heads, count, HV), b16)
+    kept = jax.ShapeDtypeStruct((pairs, heads, count // SPAN, HV, HK), b16)
+    return run_mix(mix_forward, False, 2, info, (packed, begin), (out, kept))
+
+
+def run_backward(info, packed, d_out, states, rows):
+    _, heads, _ = packed.shape[:3]
+    state = jax.ShapeDtypeStruct((heads, HV, HK), f32)
+    (end,) = run_mix(mix_grad_state, True, 1, info, (packed, d_out), (state,))
+    begin = lax.ppermute(end, "row", [(2, 0), (3, 1)]) if rows else jnp.zeros_like(end)
+    out = jax.ShapeDtypeStruct(packed.shape, b16)
+    return run_mix(mix_backward, True, 4, info, (packed, d_out, states, begin), (out,))[0]
 
 
 def gather_blocks(block, rows, cols):
@@ -210,18 +246,34 @@
     return jnp.concatenate([blocks, swap(blocks, 1, rows)], axis=1)
 
 
-def weight_grad(features, blocks, rows, side=None):
-    keep, send = features
-    away = jnp.einsum("td,ctn->cdn", send, blocks, preferred_element_type=f32).astype(b16)
-    if side is not None:
-        away = jnp.concatenate([away, side[1]], axis=2)
-    came = swap(away, 2, rows)
-    held = jnp.einsum("td,ctn->cdn", keep, blocks, preferred_element_type=f32)
-    if side is not None:
-        held = jnp.concatenate([held, side[0]], axis=2)
-    total = (held + came.astype(f32)).astype(b16)
+def to_heads(blocks, rows):
+    parts = blocks.reshape((2, -1) + blocks.shape[1:])
+    core = lax.axis_index("row") % 2
+    mine = lax.dynamic_index_in_dim(parts, core, 0, False)
+    away = lax.dynamic_index_in_dim(parts, 1 - core, 0, False)
+    return jnp.stack([mine, swap(away, 1, rows)])
+
+
+def to_tokens(parts, rows):
+    other = swap(parts[1], 1, rows)
+    core = lax.axis_index("row") % 2
+    both = jnp.where(
+        core == 0, jnp.stack([parts[0], other]), jnp.stack([other, parts[0]])
+    )
+    return both.reshape((-1,) + both.shape[2:])
+
+
+def grad_part(features, blocks):
+    return jnp.einsum("td,ctn->cdn", features, blocks, preferred_element_type=f32)
+
+
+def col_sum(total):
     flat = total.reshape(-1, total.shape[-1])
     return lax.psum_scatter(flat, "col", scatter_dimension=0, tiled=True)
+
+
+def after(value, *firsts):
+    return lax.optimization_barrier((value,) + firsts)[0]
 
 
 def make_body(dp, rows, cols):
@@ -246,10 +298,12 @@
     ):
         feat = tokens_in.shape[1]
         count = tokens_in.shape[0] // rows
-        narrow = 2 * HK + 2 * HV
+        narrow = 2 * HK + HV
         cross = [(a * cols + b, b * cols + a) for a in range(rows) for b in range(cols)]
         lengths = lax.ppermute(doc_lengths, ("row", "col"), cross)[0]
         starts = jnp.cumsum(lengths, dtype=jnp.int32) - lengths
+        me = lax.axis_index("row")
+        info = jnp.concatenate([starts, jnp.stack([me // 2, me % 2]).astype(jnp.int32)])
         key_side = jnp.concatenate([w_rank_out.T, decay_bias[:, None]], axis=1)
         side = jnp.concatenate(
             [
@@ -262,10 +316,22 @@
             axis=1,
         )
         first_w = gather_blocks(
-            jnp.concatenate([w_query, w_key, w_value, w_outgate, side], axis=1), rows, cols
+            jnp.concatenate([w_query, w_key, w_value, side], axis=1), rows, cols
         )
         late_w = gather_blocks(
-            jnp.concatenate([w_gate, w_up, w_output.T, w_down.T], axis=1), rows, cols
+            jnp.concatenate(
+                [
+                    w_gate,
+                    w_up,
+                    w_output.T,
+                    w_outgate,
+                    w_down.T,
+                    jnp.zeros((feat, -(3 * w_gate.shape[1]) % 128), b16),
+                ],
+                axis=1,
+            ),
+            rows,
+            cols,
         )
         extra = first_w[0, :, :, narrow:].reshape(D, 128)
         rank_in = extra[:, :RANK]
@@ -279,14 +345,14 @@
         hid = w_gate.shape[1]
         late_w_hid = late_w[:, :, : 2 * hid]
         out_w = late_w[:, :, 2 * hid : 2 * hid + HV]
-        down_w = late_w[:, :, 2 * hid + HV :]
-
-        both = jnp.stack(
-            [tokens_in.reshape(rows, count, feat), cotangent.reshape(rows, count, feat)], axis=1
-        )
-        both = exchange(both).transpose(1, 2, 0, 3).reshape(2, count, D)
-        inputs = both[0].astype(f32)
-        cot = both[1]
+        outgate_w = late_w[:, :, 2 * hid + HV : 2 * hid + 2 * HV]
+        down_w = late_w[:, :, 2 * hid + 2 * HV : 3 * hid + 2 * HV]
+
+        def features_whole(block):
+            split = exchange(block.reshape(rows, count, feat))
+            return split.transpose(1, 0, 2).reshape(count, D)
+
+        inputs = features_whole(tokens_in).astype(f32)
         inv_one = lax.rsqrt(jnp.mean(inputs * inputs, axis=1, keepdims=True) + norm_eps)
         normed_one = inputs * inv_one
         first = (normed_one * gain_one).astype(b16)
@@ -297,11 +363,14 @@
             + bias[:, None, :]
         )
         lam = jax.nn.log_sigmoid(zeta) / 16.0
-        gates = proj[:, :, 2 * HK + HV :]
-        packed = jnp.concatenate([proj[:, :, : 2 * HK + HV], lam], axis=2).astype(b16)
-        packed = exchange(packed).reshape(SEQ_LEN, PACK)
-        attended, states = run_forward(starts, packed)
-        heads = exchange(attended.reshape(rows, count, HV)).astype(f32)
+        packed = jnp.concatenate([proj, lam], axis=2).astype(b16)
+        packed = to_heads(packed, rows)
+        attended, states = run_forward(info, packed, rows)
+        heads = to_tokens(attended, rows).astype(f32)
+        cot = features_whole(after(cotangent, packed))
+        cot_keep, cot_send = pair_features(cot, rows)
+        first_keep, first_send = pair_features(first, rows)
+        gates = jnp.einsum("td,cdn->ctn", first, outgate_w, preferred_element_type=f32)
         gain_head = head_gain.astype(f32)
         inv_head = lax.rsqrt(jnp.mean(heads * heads, axis=-1, keepdims=True) + head_eps)
         unit = heads * inv_head
@@ -319,39 +388,58 @@
         silu_gate = gate_pre * sig_gate
         hidden = (silu_gate * up_pre).astype(b16)
 
-        cot_pair = pair_features(cot, rows)
-        grad_down = weight_grad(cot_pair, pair_tokens(hidden, rows), rows)
+        hidden_pair = pair_tokens(hidden, rows)
+        away_down = grad_part(cot_send, hidden_pair).astype(b16)
+        came_down = swap(away_down, 2, rows)
         d_hidden = jnp.einsum("td,cdn->ctn", cot, down_w, preferred_element_type=f32)
         d_gate = d_hidden * up_pre * sig_gate * (1.0 + gate_pre * (1.0 - sig_gate))
         d_up = d_hidden * silu_gate
         d_pre = jnp.concatenate([d_gate.astype(b16), d_up.astype(b16)], axis=2)
-        grad_hid = weight_grad(pair_features(second, rows), pair_tokens(d_pre, rows), rows)
+        second_keep, second_send = pair_features(second, rows)
+        pre_pair = pair_tokens(d_pre, rows)
+        away_hid = grad_part(second_send, pre_pair).astype(b16)
+        came_hid = swap(away_hid, 2, rows)
         out_rows = (
             residual + jnp.einsum("ctn,cdn->td", hidden, down_w, preferred_element_type=f32)
         ).astype(b16)
-        d_second = jnp.einsum("ctn,cdn->td", d_pre, late_w_hid, preferred_element_type=f32)
+        d_second = jnp.einsum(
+            "ctn,cdn->td", after(d_pre, away_down), late_w_hid, preferred_element_type=f32
+        )
         part_two = jnp.sum(d_second * normed_two, axis=0)
         scaled_two = d_second * gain_two
         mean_two = jnp.mean(scaled_two * normed_two, axis=1, keepdims=True)
         d_resid = cot.astype(f32) + inv_two * (scaled_two - normed_two * mean_two)
         d_low = d_resid.astype(b16)
-        grad_out = weight_grad(pair_features(d_low, rows), pair_tokens(mixed, rows), rows)
+        d_low = after(d_low, away_hid)
         d_mixed = jnp.einsum("td,cdv->ctv", d_low, out_w, preferred_element_type=f32)
         gated = d_mixed * silu_out
         part_head = jnp.sum(gated * unit, axis=(0, 1))
         d_gates = d_mixed * unit * gain_head * sig_out * (1.0 + gates * (1.0 - sig_out))
         d_unit = gated * gain_head
         d_heads = inv_head * (d_unit - unit * jnp.mean(d_unit * unit, axis=-1, keepdims=True))
-        d_attended = exchange(d_heads.astype(b16)).reshape(SEQ_LEN, HV)
-        d_packed = run_backward(starts, packed, d_attended, states)
-        d_packed = exchange(d_packed.reshape(rows, count, PACK))
-        d_zeta = d_packed[:, :, 2 * HK + HV :].astype(f32)
-        d_proj = jnp.concatenate([d_packed[:, :, : 2 * HK + HV], d_gates.astype(b16)], axis=2)
+        d_gates = d_gates.astype(b16)
+        total_down = (grad_part(cot_keep, hidden_pair) + came_down.astype(f32)).astype(b16)
+        d_attended = to_heads(d_heads.astype(b16), rows)
+        low_keep, low_send = pair_features(d_low, rows)
+        mixed_pair = pair_tokens(mixed, rows)
+        gates_pair = pair_tokens(d_gates, rows)
+        away_out = jnp.concatenate(
+            [grad_part(low_send, mixed_pair), grad_part(first_send, gates_pair)], axis=2
+        ).astype(b16)
+        came_out = swap(away_out, 2, rows)
+        d_attended = after(d_attended, total_down, away_out)
+        d_packed = run_backward(info, packed, d_attended, states, rows)
+        grad_down = col_sum(total_down)
+        d_packed = to_tokens(d_packed, rows)
+        d_zeta = d_packed[:, :, narrow:].astype(f32)
+        d_proj = d_packed[:, :, :narrow]
         d_rank = jnp.einsum("ctk,cks->ts", d_zeta, rank_out, precision=exact_mode)
-        d_first = jnp.einsum(
-            "ctn,cdn->td", d_proj, first_w, preferred_element_type=f32
-        ) + lax.dot_general(
-            d_rank, rank_in.astype(f32), NT, precision=exact_mode, preferred_element_type=f32
+        d_first = (
+            jnp.einsum("ctn,cdn->td", d_proj, first_w, preferred_element_type=f32)
+            + jnp.einsum("ctn,cdn->td", d_gates, outgate_w, preferred_element_type=f32)
+            + lax.dot_general(
+                d_rank, rank_in.astype(f32), NT, precision=exact_mode, preferred_element_type=f32
+            )
         )
         part_one = jnp.sum(d_first * normed_one, axis=0)
         scaled_one = d_first * gain_one
@@ -378,7 +466,6 @@
             ],
             axis=3,
         ).astype(b16)
-        me = lax.axis_index("row")
 
         def side_piece(bit):
             return lax.dynamic_index_in_dim(side_grad, me ^ bit, 1, False)
@@ -386,9 +473,19 @@
         side_other = swap(jnp.stack([side_piece(1), side_piece(3)]), 1, rows).astype(f32)
         side_keep = side_piece(0).astype(f32) + side_other[0]
         side_send = (side_piece(2).astype(f32) + side_other[1]).astype(b16)
-        grad_first = weight_grad(
-            pair_features(first, rows), pair_tokens(d_proj, rows), rows, (side_keep, side_send)
-        )
+        proj_pair = pair_tokens(d_proj, rows)
+        away_first = grad_part(first_send, proj_pair).astype(b16)
+        away_first = jnp.concatenate([away_first, side_send], axis=2)
+        total_hid = (grad_part(second_keep, pre_pair) + came_hid.astype(f32)).astype(b16)
+        grad_hid = col_sum(total_hid)
+        held_out = jnp.concatenate(
+            [grad_part(low_keep, mixed_pair), grad_part(first_keep, gates_pair)], axis=2
+        )
+        total_out = (held_out + came_out.astype(f32)).astype(b16)
+        grad_out = col_sum(total_out)
+        came_first = swap(after(away_first, total_hid), 2, rows)
+        held_first = jnp.concatenate([grad_part(first_keep, proj_pair), side_keep], axis=2)
+        grad_first = col_sum((held_first + came_first.astype(f32)).astype(b16))
 
         out_rows = exchange(out_rows.reshape(count, rows, feat).transpose(1, 0, 2))
         grad_tokens = exchange(
@@ -405,13 +502,13 @@
             side_sum[:, RANK],
             grad_first[:, :HK],
             grad_first[:, HK : 2 * HK],
-            grad_first[:, 2 * HK : 2 * HK + HV],
-            grad_first[:, 2 * HK + HV : narrow],
+            grad_first[:, 2 * HK : narrow],
+            grad_out[:, HV:],
             side_sum[:, :RANK],
             side_sum[:HK, RANK + 2 : 2 * RANK + 2].T,
             side_sum[:HK, 2 * RANK + 2],
             side_sum[:, 2 * RANK + 3],
-            grad_out.T,
+            grad_out[:, :HV].T,
             side_sum[:, RANK + 1],
             grad_hid[:, :hid],
             grad_hid[:, hid:],
@@ -463,6 +560,5 @@
         flipped,
     )
     body = make_body(mesh.shape["dp"], mesh.shape["row"], mesh.shape["col"])
-    return jax.shard_map(
-        body, mesh=mesh, in_specs=in_specs, out_specs=out_specs, check_vma=False
-    )
+
+    return jax.shard_map(body, mesh=mesh, in_specs=in_specs, out_specs=out_specs, check_vma=False)

time: 656 us -> 594 us (0.905)
  blocking collectives: 34.6 us -> 0 us
  waiting for transfers between devices: 282 us -> 248 us
  local copies, waits for them, and re-layouts: 101 us -> 80.4 us
  Pallas kernels: 23.1 us -> 37.4 us
  matrix products: 108 us -> 117 us
    all_to_all x6 -> x4, waiting for transfers between devices: 101 us -> 37.4 us  [exchange(): return lax.all_to_all(blocks, 'row', 0, 0)]
    all_to_all x1 -> x0, blocking collectives: 34.6 us -> none  [exchange(): return lax.all_to_all(blocks, 'row', 0, 0)]
    ppermute x13 -> x18, waiting for transfers between devices: 103 us -> 72.4 us  [swap(): return lax.ppermute(part, 'row', [(i, i ^ bit) for i in range(rows)])]
    reduce_scatter x4, waiting for transfers between devices: 0.05 us -> 28.5 us  [col_sum(): return lax.psum_scatter(flat, 'col', scatter_dimension=0, tiled=True)]
    all_gather x1 -> x0, local copies, waits for them, and re-layouts: 25.1 us -> none  [gather_blocks(): whole = lax.all_gather(block, GRID, axis=0, tiled=True)]
    all_gather x2, waiting for transfers between devices: 50.4 us -> 69.8 us  [gather_blocks(): whole = lax.all_gather(block, GRID, axis=0, tiled=True)]
    pallas_call x2 -> x4, Pallas kernels: 23.1 us -> 37.4 us  [run_mix(): pl.pallas_call(kernel, out_shape=results, grid_spec=pltpu.PrefetchScalarG...]
    ppermute x0 -> x2, waiting for transfers between devices: none -> 14.1 us  [the longest x1 7.36 us: run_forward(): lax.ppermute(end, 'row', [(0, 2), (1, 3)])]
  transfers between devices with their start and end apart: 30 -> 35, of which waited for: 15 -> 15; matrix products, arithmetic and copies ran while one was open for 25% -> 32% of each run, Pallas kernels for 4% -> 6%
where the time goes in v3:
time: 594 us; the launch traced here: 586 us
  waiting for transfers between devices  248 us (42%)
  matrix products  117 us (20%)
  local copies, waits for them, and re-layouts  80.4 us (14%)
  starting transfers between devices  44.2 us (7%)
  other arithmetic  44 us (7%)
  Pallas kernels  37.4 us (6%)
  between operations  15.5 us (3%)
    ppermute x18, waiting for transfers between devices, swap(): return lax.ppermute(part, 'row', [(i, i ^ bit) for i in range(rows)])  72.4 us
    all_gather x2, waiting for transfers between devices, gather_blocks(): whole = lax.all_gather(block, GRID, axis=0, tiled=True)  69.8 us
    dot_general x10, matrix products, grad_part(): jnp.einsum('td,ctn->cdn', features, blocks, preferred_element_type=f32)  38.5 us
    pallas_call x4, Pallas kernels, run_mix(): pl.pallas_call(kernel, out_shape=results, grid_spec=pltpu.PrefetchScalarG...  37.4 us
    all_to_all x4, waiting for transfers between devices, exchange(): return lax.all_to_all(blocks, 'row', 0, 0)  37.4 us
    reduce_scatter x4, waiting for transfers between devices, col_sum(): return lax.psum_scatter(flat, 'col', scatter_dimension=0, tiled=True)  28.5 us
    ppermute x4, waiting for transfers between devices, batch_sum(): other = lax.ppermute(part, 'dp', [(0, 1), (1, 0)])  25.6 us
    unnamed x124, local copies, waits for them, and re-layouts  16.8 us
  transfers between devices with their start and end apart: 35, of which 15 were waited for; matrix products, arithmetic and copies ran while one was open for 32% of the time, Pallas kernels for 6%

profile of v3, /device:TPU:0, one launch (start us, length us, event | category | flops | bytes accessed | tf_op | source)
XLA Modules:
  0.0 586.2 jit_solution(4579953824351336584)
XLA Ops:
  20.6 17.9 %all-to-all-done = bf16[4,512,256]{2,1,0:T(8,128)(2,1)S(1)} async-done(((bf16[4,512,256]{2,1,0:T(8,128)(2,1)}), bf16[4,512,256]{2,1,0:T(8,128)(2,1)S(1)}, u32[]{:S(2)}, u32[]{:S(2)}) %all-to-all-start) | async-done | bytes 1048608 | tf_op jit(solution)/shard_map/all_to_all | solution.py:30
  39.3 34.6 %all-gather.3.cloned.1.call-done = bf16[4096,640]{1,0:T(8,128)(2,1)} async-done(((bf16[256,640]{1,0:T(8,128)(2,1)}), bf16[4096,640]{1,0:T(8,128)(2,1)}) %all-gather.3.cloned.1.call-update) | async-done | bytes 5242896 | tf_op jit(solution)/shard_map/all_gather | solution.py:217
  81.7 5.9 %convert_bitcast_fusion.1 = bf16[4,512,512]{1,2,0:T(8,128)(2,1)} fusion(bf16[4,1024,640]{2,1,0:T(8,128)(2,1)} %bitcast.341, bf16[512,1024]{1,0:T(8,128)(2,1)S(1)} %multiply_convert_fusion.4), kind=kOutput, calls=%fused_computation.87 | convolution fusion | flops 2148532224 | bytes 7340032 | tf_op jit(solution)/shard_map/td,cdn->ctn/dot_general | solution.py:359
  102.8 6.4 %shard_map.288 = f32[2,256,128]{2,1,0:T(8,128)} custom-call(s32[8]{0:T(128)} %pad_add_fusion.info_ref, bf16[2,2,512,640]{3,2,1,0:T(8,128)(2,1)} %pad_maximum_fusion.16.x_ref), custom_call_target="tpu_custom_call" | custom-call | flops 200000000 | bytes 4000000 | tf_op jit(solution)/shard_map/pallas_call | solution.py:181
  109.1 8.0 %collective-permute-start.2 = (f32[2,256,128]{2,1,0:T(8,128)}, f32[2,256,128]{2,1,0:T(8,128)}, u32[]{:S(2)}, u32[]{:S(2)}) collective-permute-start(f32[2,256,128]{2,1,0:T(8,128)} %shard_map.288), channel_id=1, source_target_pairs={{0,8},{4,12},{1,9},{5,13},{2,10},{6,14},{3,11},{7,15},{16,24},{20,... | collective-permute-start | bytes 786440 | tf_op jit(solution)/shard_map/ppermute | solution.py:201
  121.7 7.4 %collective-permute-done.2.start_ref = f32[2,256,128]{2,1,0:T(8,128)} collective-permute-done((f32[2,256,128]{2,1,0:T(8,128)}, f32[2,256,128]{2,1,0:T(8,128)}, u32[]{:S(2)}, u32[]{:S(2)}) %collective-permute-start.2) | collective-permute-done | bytes 262176 | tf_op jit(solution)/shard_map/ppermute | solution.py:201
  129.0 9.7 %shard_map.289 = (bf16[2,2,512,256]{3,2,1,0:T(8,128)(2,1)}, bf16[2,2,8,256,128]{4,3,2,1,0:T(8,128)(2,1)}) custom-call(s32[8]{0:T(128)} %pad_add_fusion.info_ref, bf16[2,2,512,640]{3,2,1,0:T(8,128)(2,1)} %pad_maximum_fusion.16.x_ref, f32[2,256,128]{2,1,0:T(8,128)} %collective-permute-done.2.start_ref), custom_call_target="tpu_custom_call" | custom-call | flops 400000000 | bytes 8000000 | tf_op jit(solution)/shard_map/pallas_call | solution.py:181
  141.6 9.9 %all-to-all-done.2 = bf16[4,512,256]{2,1,0:T(8,128)(2,1)} async-done(((bf16[4,512,256]{2,1,0:T(8,128)(2,1)}), bf16[4,512,256]{2,1,0:T(8,128)(2,1)}, u32[]{:S(2)}, u32[]{:S(2)}) %all-to-all-start.2) | async-done | bytes 1048608 | tf_op jit(solution)/shard_map/all_to_all | solution.py:30
  165.7 35.1 %all-gather.5.cloned.1.call-done = bf16[4096,2688]{1,0:T(8,128)(2,1)} async-done(((bf16[256,2688]{1,0:T(8,128)(2,1)}), bf16[4096,2688]{1,0:T(8,128)(2,1)}) %all-gather.5.cloned.1.call-update) | async-done | bytes 22020112 | tf_op jit(solution)/shard_map/all_gather | solution.py:217
  211.2 13.7 %fusion.4 = f32[4,512,1408]{1,2,0:T(8,128)} fusion(bf16[4,1024,2688]{2,1,0:T(8,128)(2,1)} %bitcast.353, bf16[512,1024]{1,0:T(8,128)(2,1)S(1)} %multiply_convert_fusion.2), kind=kOutput, calls=%fused_computation.5 | convolution fusion | flops 5905580032 | bytes 24117248 | tf_op jit(solution)/shard_map/td,cdn->ctn/dot_general | solution.py:384
  224.9 12.1 %fusion.10 = (bf16[4,512,704]{1,2,0:T(8,128)(2,1)S(1)}, bf16[4,512,704]{1,2,0:T(8,128)(2,1)S(1)}, bf16[4,512,704]{1,2,0:T(8,128)(2,1)}) fusion(f32[4,512,1408]{1,2,0:T(8,128)} %fusion.4, bf16[512,1024,1]{1,0,2:T(8,128)(2,1)S(1)} %copy-done.16, bf16[4,1024,2688]{2,1,0:T(8,128)(2,1)} %bitcast.354), kind=kOutput, calls=%fused_computation.14 | convolution fusion | flops 2974416896 | bytes 27525120 | tf_op jit(solution)/shard_map/td,cdn->ctn/dot_general | solution.py:394
  263.6 11.7 %fusion.38 = (f32[1024]{0:T(1024)}, f32[512]{0:T(512)S(1)}, f32[512,1024,1]{1,0,2:T(8,128)S(1)}) fusion(f32[512,1024]{1,0:T(8,128)S(1)} %copy-done.1, f32[512]{0:T(512)S(1)} %add_rsqrt_fusion.1, f32[1024]{0:T(1024)S(1)} %get-tuple-element.103, bf16[4,512,1408]{1,2,0:T(8,128)(2,1)} %pad_maximum_fusion.1, bf16[4,1024,2688]{2,1,0:T(8,128)(2,1)} %bitcast.355), kind=kOutput, calls=%fused_computation.64 | convolution fusion | flops 5908724224 | bytes 21508096 | tf_op jit(solution)/shard_map/ctn,cdn->td/dot_general | solution.py:405
  278.7 6.6 %fusion.26 = bf16[4,256,1408]{1,2,0:T(8,128)(2,1)} fusion(bf16[4,512,1408]{1,2,0:T(8,128)(2,1)} %collective-permute-done.6, bf16[4,512,704]{1,2,0:T(8,128)(2,1)S(1)} %copy-done.13, bf16[4,512,704]{1,2,0:T(8,128)(2,1)S(1)} %copy-done.10, bf16[512,256]{1,0:T(8,128)(2,1)S(1)} %get-tuple-element.147, bf16[512,256]{1,0:T(8,128)(2,1)S(1)} %get-tuple-element.125), kind=kOutput, calls=%fused_computation.35 | convolution fusion | flops 2989883392 | bytes 14942208 | tf_op jit(solution)/shard_map/td,ctn->cdn/dot_general | solution.py:267
  317.1 6.5 %shard_map.290 = f32[2,256,128]{2,1,0:T(8,128)} custom-call(s32[8]{0:T(128)} %pad_add_fusion.info_ref, bf16[2,2,512,640]{3,2,1,0:T(8,128)(2,1)} %pad_maximum_fusion.16.x_ref, bf16[2,2,512,256]{3,2,1,0:T(8,128)(2,1)} %pad_maximum_fusion.44.do_ref), custom_call_target="tpu_custom_call" | custom-call | flops 200000000 | bytes 4000000 | tf_op jit(solution)/shard_map/pallas_call | solution.py:181
  328.2 6.8 %collective-permute-done.14.start_ref = f32[2,256,128]{2,1,0:T(8,128)} collective-permute-done((f32[2,256,128]{2,1,0:T(8,128)}, f32[2,256,128]{2,1,0:T(8,128)}, u32[]{:S(2)}, u32[]{:S(2)}) %collective-permute-start.14) | collective-permute-done | bytes 262176 | tf_op jit(solution)/shard_map/ppermute | solution.py:211
  334.9 14.8 %shard_map.291 = bf16[2,2,512,640]{3,2,1,0:T(8,128)(2,1)} custom-call(s32[8]{0:T(128)} %pad_add_fusion.info_ref, bf16[2,2,512,640]{3,2,1,0:T(8,128)(2,1)} %pad_maximum_fusion.16.x_ref, bf16[2,2,512,256]{3,2,1,0:T(8,128)(2,1)} %pad_maximum_fusion.44.do_ref, bf16[2,2,8,256,128]{4,3,2,1,0:T(8,128)(2,1)} %get-tuple-element.28.states_ref, ...), custom_call_target="tpu_custom_call" | custom-call | flops 800000000 | bytes 16000000 | tf_op jit(solution)/shard_map/pallas_call | solution.py:181
  383.1 39.4 %collective-permute-done.18 = bf16[4,256,1408]{1,2,0:T(8,128)(2,1)} collective-permute-done((bf16[4,256,1408]{1,2,0:T(8,128)(2,1)}, bf16[4,256,1408]{1,2,0:T(8,128)(2,1)}, u32[]{:S(2)}, u32[]{:S(2)}) %collective-permute-start.18) | collective-permute-done | bytes 2883616 | tf_op jit(solution)/shard_map/ppermute | solution.py:229
  422.5 6.7 %fusion.7 = bf16[4,256,1408]{1,2,0:T(8,128)(2,1)} fusion(bf16[4,256,1408]{1,2,0:T(8,128)(2,1)} %collective-permute-done.18, bf16[4,512,1408]{1,2,0:T(8,128)(2,1)} %collective-permute-done.6, bf16[4,512,704]{1,2,0:T(8,128)(2,1)S(1)} %copy-done.14, bf16[4,512,704]{1,2,0:T(8,128)(2,1)S(1)} %copy-done.11, bf16[512,256]{1,0:T(8,128)(2,1)S(1)} %copy-done.30, ...), kind=kOutput, calls=%fused_computation.9 | convolution fusion | flops 2992766976 | bytes 17825792 | tf_op jit(solution)/shard_map/td,ctn->cdn/dot_general | solution.py:267
  437.0 26.6 %collective-permute-done.19 = bf16[4,256,640]{1,2,0:T(8,128)(2,1)S(1)} collective-permute-done((bf16[4,256,640]{1,2,0:T(8,128)(2,1)S(1)}, bf16[4,256,640]{1,2,0:T(8,128)(2,1)S(1)}, u32[]{:S(2)}, u32[]{:S(2)}) %collective-permute-start.19) | collective-permute-done | bytes 1310752 | tf_op jit(solution)/shard_map/ppermute | solution.py:229
  472.4 8.0 %fusion.39 = bf16[512,1024]{1,0:T(8,128)(2,1)S(1)} fusion(f32[512,1024]{1,0:T(8,128)} %copy-done, bf16[4,512,704]{1,2,0:T(8,128)(2,1)} %get-tuple-element.107, bf16[4,1024,2688]{2,1,0:T(8,128)(2,1)} %bitcast.358), kind=kOutput, calls=%fused_computation.66 | convolution fusion | flops 2953838592 | bytes 12320768 | tf_op jit(solution)/shard_map/ctn,cdn->td/dot_general | solution.py:403
  490.7 9.6 %all-to-all-done.1 = bf16[4,512,256]{2,1,0:T(8,128)(2,1)} async-done(((bf16[4,512,256]{2,1,0:T(8,128)(2,1)}), bf16[4,512,256]{2,1,0:T(8,128)(2,1)}, u32[]{:S(2)}, u32[]{:S(2)}) %all-to-all-start.1) | async-done | bytes 1048608 | tf_op jit(solution)/shard_map/all_to_all | solution.py:30
  505.5 9.2 %collective-permute-done.24 = bf16[256,704]{0,1:T(8,128)(2,1)S(1)} collective-permute-done((bf16[256,704]{0,1:T(8,128)(2,1)}, bf16[256,704]{0,1:T(8,128)(2,1)S(1)}, u32[]{:S(2)}, u32[]{:S(2)}) %collective-permute-start.24) | collective-permute-done | bytes 360480 | tf_op jit(solution)/shard_map/ppermute | solution.py:223
  527.7 28.5 %reduce-scatter.9.cloned.1.call-done = bf16[256,1408]{1,0:T(8,128)(2,1)} async-done(((bf16[1024,1408]{1,0:T(8,128)(2,1)}), bf16[256,1408]{1,0:T(8,128)(2,1)}) %reduce-scatter.9.cloned.1.call-update) | async-done | bytes 720912 | tf_op jit(solution)/shard_map/reduce_scatter | solution.py:272
  562.3 11.7 %collective-permute-done.23 = bf16[256,1408]{1,0:T(8,128)(2,1)S(1)} collective-permute-done((bf16[256,1408]{1,0:T(8,128)(2,1)}, bf16[256,1408]{1,0:T(8,128)(2,1)S(1)}, u32[]{:S(2)}, u32[]{:S(2)}) %collective-permute-start.23) | collective-permute-done | bytes 720928 | tf_op jit(solution)/shard_map/ppermute | solution.py:223
  (307 shorter events, 224.0 us)
Async XLA Ops:
  7.2 66.7 %all-gather.3.cloned.1.call-start = ((), (), s32[]{:S(2)}) async-start(), calls=%async_computation.8 | async-start | bytes 5570560 | tf_op jit(solution)/shard_map/all_gather | solution.py:217
  12.5 188.3 %all-gather.5.cloned.1.call-start = ((), (), s32[]{:S(2)}) async-start(), calls=%async_computation.9 | async-start | bytes 23396352 | tf_op jit(solution)/shard_map/all_gather | solution.py:217
  16.3 22.2 %all-to-all-start = ((bf16[4,512,256]{2,1,0:T(8,128)(2,1)}), bf16[4,512,256]{2,1,0:T(8,128)(2,1)S(1)}, u32[]{:S(2)}, u32[]{:S(2)}) async-start(bf16[4,512,256]{2,1,0:T(8,128)(2,1)} %bitcast.332), calls=%async_computation | async-start | bytes 2097152 | tf_op jit(solution)/shard_map/all_to_all | solution.py:30
  109.1 19.9 %collective-permute-start.2 = (f32[2,256,128]{2,1,0:T(8,128)}, f32[2,256,128]{2,1,0:T(8,128)}, u32[]{:S(2)}, u32[]{:S(2)}) collective-permute-start(f32[2,256,128]{2,1,0:T(8,128)} %shard_map.288), channel_id=1, source_target_pairs={{0,8},{4,12},{1,9},{5,13},{2,10},{6,14},{3,11},{7,15},{16,24},{20,... | collective-permute-start | bytes 786440 | tf_op jit(solution)/shard_map/ppermute | solution.py:201
  117.1 34.3 %all-to-all-start.2 = ((bf16[4,512,256]{2,1,0:T(8,128)(2,1)}), bf16[4,512,256]{2,1,0:T(8,128)(2,1)}, u32[]{:S(2)}, u32[]{:S(2)}) async-start(bf16[4,512,256]{2,1,0:T(8,128)(2,1)} %bitcast.333), calls=%async_computation.2 | async-start | bytes 2097152 | tf_op jit(solution)/shard_map/all_to_all | solution.py:30
  121.4 382.4 %reduce-scatter.11.cloned.1.call-start = ((), (), s32[]{:S(2)}) async-start(), calls=%async_computation.13 | async-start | bytes 1802240 | tf_op jit(solution)/shard_map/reduce_scatter | solution.py:272
  241.6 35.0 %collective-permute-start.6 = (bf16[4,512,1408]{1,2,0:T(8,128)(2,1)}, bf16[4,512,1408]{1,2,0:T(8,128)(2,1)}, u32[]{:S(2)}, u32[]{:S(2)}) collective-permute-start(bf16[4,512,1408]{1,2,0:T(8,128)(2,1)} %pad_maximum_fusion.1), channel_id=1, source_target_pairs={{0,4},{4,0},{8,12},{12,8},{1,5},{5,1},{9,13},{13,9},{2,6},{6,2},{1... | collective-permute-start | bytes 17301512 | tf_op jit(solution)/shard_map/ppermute | solution.py:229
  247.5 57.9 %collective-permute-start.13 = (bf16[2,512,256]{2,1,0:T(8,128)(2,1)}, bf16[2,512,256]{2,1,0:T(8,128)(2,1)}, u32[]{:S(2)}, u32[]{:S(2)}) collective-permute-start(bf16[2,512,256]{2,1,0:T(8,128)(2,1)} %pad_maximum_fusion.49), channel_id=1, source_target_pairs={{0,4},{4,0},{8,12},{12,8},{1,5},{5,1},{9,13},{13,9},{2,6},{6,2},{1... | collective-permute-start | bytes 1572872 | tf_op jit(solution)/shard_map/ppermute | solution.py:229
  252.7 58.7 %collective-permute-start.10 = (bf16[4,512,256]{1,2,0:T(8,128)(2,1)}, bf16[4,512,256]{1,2,0:T(8,128)(2,1)}, u32[]{:S(2)}, u32[]{:S(2)}) collective-permute-start(bf16[4,512,256]{1,2,0:T(8,128)(2,1)} %get-tuple-element.152), channel_id=1, source_target_pairs={{0,4},{4,0},{8,12},{12,8},{1,5},{5,1},{9,13},{13,9},{2,6},{6,2},{1... | collective-permute-start | bytes 3145736 | tf_op jit(solution)/shard_map/ppermute | solution.py:229
  259.2 40.1 %collective-permute-start.9 = (bf16[4,256,704]{1,2,0:T(8,128)(2,1)}, bf16[4,256,704]{1,2,0:T(8,128)(2,1)}, u32[]{:S(2)}, u32[]{:S(2)}) collective-permute-start(bf16[4,256,704]{1,2,0:T(8,128)(2,1)} %fusion.63), channel_id=1, source_target_pairs={{0,8},{4,12},{8,0},{12,4},{1,9},{5,13},{9,1},{13,5},{2,10},{6,14},... | collective-permute-start | bytes 4325384 | tf_op jit(solution)/shard_map/ppermute | solution.py:229
  287.1 22.5 %collective-permute-start.11 = (bf16[2,512,256]{2,1,0:T(8,128)(2,1)}, bf16[2,512,256]{2,1,0:T(8,128)(2,1)}, u32[]{:S(2)}, u32[]{:S(2)}) collective-permute-start(bf16[2,512,256]{2,1,0:T(8,128)(2,1)} %pad_maximum_fusion.48), channel_id=1, source_target_pairs={{0,4},{4,0},{8,12},{12,8},{1,5},{5,1},{9,13},{13,9},{2,6},{6,2},{1... | collective-permute-start | bytes 1572872 | tf_op jit(solution)/shard_map/ppermute | solution.py:229
  305.4 211.3 %reduce-scatter.7.cloned.1.call-start = ((), (), s32[]{:S(2)}) async-start(), calls=%async_computation.11 | async-start | bytes 1310720 | tf_op jit(solution)/shard_map/reduce_scatter | solution.py:272
  324.9 41.6 %collective-permute-start.21 = (bf16[4,256,512]{1,2,0:T(8,128)(2,1)}, bf16[4,256,512]{1,2,0:T(8,128)(2,1)}, u32[]{:S(2)}, u32[]{:S(2)}) collective-permute-start(bf16[4,256,512]{1,2,0:T(8,128)(2,1)} %pad_maximum_fusion.45), channel_id=1, source_target_pairs={{0,8},{4,12},{8,0},{12,4},{1,9},{5,13},{9,1},{13,5},{2,10},{6,14},... | collective-permute-start | bytes 3145736 | tf_op jit(solution)/shard_map/ppermute | solution.py:229
  353.1 18.2 %collective-permute-start.15 = (bf16[2,512,640]{2,1,0:T(8,128)(2,1)}, bf16[2,512,640]{2,1,0:T(8,128)(2,1)}, u32[]{:S(2)}, u32[]{:S(2)}) collective-permute-start(bf16[2,512,640]{2,1,0:T(8,128)(2,1)} %get-tuple-element.111), channel_id=1, source_target_pairs={{0,4},{4,0},{8,12},{12,8},{1,5},{5,1},{9,13},{13,9},{2,6},{6,2},{1... | collective-permute-start | bytes 3932168 | tf_op jit(solution)/shard_map/ppermute | solution.py:229
  357.2 65.2 %collective-permute-start.18 = (bf16[4,256,1408]{1,2,0:T(8,128)(2,1)}, bf16[4,256,1408]{1,2,0:T(8,128)(2,1)}, u32[]{:S(2)}, u32[]{:S(2)}) collective-permute-start(bf16[4,256,1408]{1,2,0:T(8,128)(2,1)} %fusion.26), channel_id=1, source_target_pairs={{0,8},{4,12},{8,0},{12,4},{1,9},{5,13},{9,1},{13,5},{2,10},{6,14},... | collective-permute-start | bytes 8650760 | tf_op jit(solution)/shard_map/ppermute | solution.py:229
  371.3 148.7 %reduce-scatter.5.cloned.1.call-start = ((), (), s32[]{:S(2)}) async-start(), calls=%async_computation.10 | async-start | bytes 1638400 | tf_op jit(solution)/shard_map/reduce_scatter | solution.py:272
  374.7 54.7 %collective-permute-start.16 = (bf16[4,512,512]{2,1,0:T(8,128)(2,1)S(1)}, bf16[4,512,512]{2,1,0:T(8,128)(2,1)}, u32[]{:S(2)}, u32[]{:S(2)}) collective-permute-start(bf16[4,512,512]{2,1,0:T(8,128)(2,1)S(1)} %slice.202), channel_id=1, source_target_pairs={{0,4},{4,0},{8,12},{12,8},{1,5},{5,1},{9,13},{13,9},{2,6},{6,2},{1... | collective-permute-start | bytes 6291464 | tf_op jit(solution)/shard_map/ppermute | solution.py:229
  382.6 46.5 %collective-permute-start.17 = (bf16[2,4,256,128]{2,3,1,0:T(8,128)(2,1)S(1)}, bf16[2,4,256,128]{2,3,1,0:T(8,128)(2,1)S(1)}, u32[]{:S(2)}, u32[]{:S(2)}) collective-permute-start(bf16[2,4,256,128]{2,3,1,0:T(8,128)(2,1)S(1)} %pad_maximum_fusion.50), channel_id=1, source_target_pairs={{0,4},{4,0},{8,12},{12,8},{1,5},{5,1},{9,13},{13,9},{2,6},{6,2},{1... | collective-permute-start | bytes 1572872 | tf_op jit(solution)/shard_map/ppermute | solution.py:229
  433.2 30.4 %collective-permute-start.19 = (bf16[4,256,640]{1,2,0:T(8,128)(2,1)S(1)}, bf16[4,256,640]{1,2,0:T(8,128)(2,1)S(1)}, u32[]{:S(2)}, u32[]{:S(2)}) collective-permute-start(bf16[4,256,640]{1,2,0:T(8,128)(2,1)S(1)} %pad_maximum_fusion.35), channel_id=1, source_target_pairs={{0,8},{4,12},{8,0},{12,4},{1,9},{5,13},{9,1},{13,5},{2,10},{6,14},... | collective-permute-start | bytes 3932168 | tf_op jit(solution)/shard_map/ppermute | solution.py:229
  467.5 88.7 %reduce-scatter.9.cloned.1.call-start = ((), (), s32[]{:S(2)}) async-start(), calls=%async_computation.12 | async-start | bytes 3604480 | tf_op jit(solution)/shard_map/reduce_scatter | solution.py:272
  481.5 18.8 %all-to-all-start.1 = ((bf16[4,512,256]{2,1,0:T(8,128)(2,1)}), bf16[4,512,256]{2,1,0:T(8,128)(2,1)}, u32[]{:S(2)}, u32[]{:S(2)}) async-start(bf16[4,512,256]{2,1,0:T(8,128)(2,1)} %bitcast.327), calls=%async_computation.1 | async-start | bytes 2097152 | tf_op jit(solution)/shard_map/all_to_all | solution.py:30
  500.2 18.1 %all-to-all-start.3 = ((bf16[4,512,256]{2,1,0:T(8,128)(2,1)}), bf16[4,512,256]{2,1,0:T(8,128)(2,1)S(1)}, u32[]{:S(2)}, u32[]{:S(2)}) async-start(bf16[4,512,256]{2,1,0:T(8,128)(2,1)} %bitcast.300), calls=%async_computation.3 | async-start | bytes 2097152 | tf_op jit(solution)/shard_map/all_to_all | solution.py:30
  519.9 37.8 %collective-permute-start.20 = (bf16[256,640]{1,0:T(8,128)(2,1)}, bf16[256,640]{1,0:T(8,128)(2,1)S(1)}, u32[]{:S(2)}, u32[]{:S(2)}) collective-permute-start(bf16[256,640]{1,0:T(8,128)(2,1)} %reduce-scatter.5.cloned.1.call-done), channel_id=1, source_target_pairs={{0,16},{16,0},{1,17},{17,1},{2,18},{18,2},{3,19},{19,3},{4,20},{20... | collective-permute-start | bytes 983048 | tf_op jit(solution)/shard_map/ppermute | solution.py:223
  556.2 17.7 %collective-permute-start.23 = (bf16[256,1408]{1,0:T(8,128)(2,1)}, bf16[256,1408]{1,0:T(8,128)(2,1)S(1)}, u32[]{:S(2)}, u32[]{:S(2)}) collective-permute-start(bf16[256,1408]{1,0:T(8,128)(2,1)} %reduce-scatter.9.cloned.1.call-done), channel_id=1, source_target_pairs={{0,16},{16,0},{1,17},{17,1},{2,18},{18,2},{3,19},{19,3},{4,20},{20... | collective-permute-start | bytes 2162696 | tf_op jit(solution)/shard_map/ppermute | solution.py:223
  (67 other events, 734.3 us)
Sparse Core Ops, SparseCore 0:
  12.6 61.2 all-gather.2
  75.5 125.2 all-gather.4
  305.5 33.4 reduce-scatter.10
  371.4 28.7 reduce-scatter.6
  467.6 31.4 reduce-scatter.4
  501.2 54.9 reduce-scatter.8

commit v4 on v3

--- a/solution.py
+++ b/solution.py
@@ -194,21 +194,22 @@
     )(info, *operands)
 
 
-def run_forward(info, packed, rows):
+def run_forward(info, packed):
     pairs, heads, count = packed.shape[:3]
     state = jax.ShapeDtypeStruct((heads, HV, HK), f32)
     (end,) = run_mix(mix_state, False, 1, info, (packed,), (state,))
-    begin = lax.ppermute(end, "row", [(0, 2), (1, 3)]) if rows else jnp.zeros_like(end)
+    begin = lax.ppermute(end, "row", [(0, 2), (1, 3)])
     out = jax.ShapeDtypeStruct((pairs, heads, count, HV), b16)
     kept = jax.ShapeDtypeStruct((pairs, heads, count // SPAN, HV, HK), b16)
     return run_mix(mix_forward, False, 2, info, (packed, begin), (out, kept))
 
 
-def run_backward(info, packed, d_out, states, rows):
+def run_backward(info, packed, d_out, states, firsts):
     _, heads, _ = packed.shape[:3]
     state = jax.ShapeDtypeStruct((heads, HV, HK), f32)
     (end,) = run_mix(mix_grad_state, True, 1, info, (packed, d_out), (state,))
-    begin = lax.ppermute(end, "row", [(2, 0), (3, 1)]) if rows else jnp.zeros_like(end)
+    begin = lax.ppermute(end, "row", [(2, 0), (3, 1)])
+    begin = after(begin, *firsts)
     out = jax.ShapeDtypeStruct(packed.shape, b16)
     return run_mix(mix_backward, True, 4, info, (packed, d_out, states, begin), (out,))[0]
 
@@ -267,9 +268,13 @@
     return jnp.einsum("td,ctn->cdn", features, blocks, preferred_element_type=f32)
 
 
+def joined(held, came):
+    total = (held + came.astype(f32)).astype(b16)
+    return total.reshape(-1, total.shape[-1])
+
+
 def col_sum(total):
-    flat = total.reshape(-1, total.shape[-1])
-    return lax.psum_scatter(flat, "col", scatter_dimension=0, tiled=True)
+    return lax.psum_scatter(total, "col", scatter_dimension=0, tiled=True)
 
 
 def after(value, *firsts):
@@ -341,12 +346,6 @@
         rank_out = keys_extra[:, :, RANK + 2 : 2 * RANK + 2].astype(f32)
         bias = keys_extra[:, :, 2 * RANK + 2].astype(f32)
         first_w = first_w.reshape(cols, D, narrow + 128)[:, :, :narrow]
-        late_w = late_w.reshape(cols, D, -1)
-        hid = w_gate.shape[1]
-        late_w_hid = late_w[:, :, : 2 * hid]
-        out_w = late_w[:, :, 2 * hid : 2 * hid + HV]
-        outgate_w = late_w[:, :, 2 * hid + HV : 2 * hid + 2 * HV]
-        down_w = late_w[:, :, 2 * hid + 2 * HV : 3 * hid + 2 * HV]
 
         def features_whole(block):
             split = exchange(block.reshape(rows, count, feat))
@@ -365,11 +364,18 @@
         lam = jax.nn.log_sigmoid(zeta) / 16.0
         packed = jnp.concatenate([proj, lam], axis=2).astype(b16)
         packed = to_heads(packed, rows)
-        attended, states = run_forward(info, packed, rows)
+        attended, states = run_forward(info, packed)
         heads = to_tokens(attended, rows).astype(f32)
         cot = features_whole(after(cotangent, packed))
         cot_keep, cot_send = pair_features(cot, rows)
         first_keep, first_send = pair_features(first, rows)
+        late_w = after(late_w, cot_keep, cot_send, first_keep, first_send)
+        late_w = late_w.reshape(cols, D, -1)
+        hid = w_gate.shape[1]
+        late_w_hid = late_w[:, :, : 2 * hid]
+        out_w = late_w[:, :, 2 * hid : 2 * hid + HV]
+        outgate_w = late_w[:, :, 2 * hid + HV : 2 * hid + 2 * HV]
+        down_w = late_w[:, :, 2 * hid + 2 * HV : 3 * hid + 2 * HV]
         gates = jnp.einsum("td,cdn->ctn", first, outgate_w, preferred_element_type=f32)
         gain_head = head_gain.astype(f32)
         inv_head = lax.rsqrt(jnp.mean(heads * heads, axis=-1, keepdims=True) + head_eps)
@@ -394,23 +400,27 @@
         d_hidden = jnp.einsum("td,cdn->ctn", cot, down_w, preferred_element_type=f32)
         d_gate = d_hidden * up_pre * sig_gate * (1.0 + gate_pre * (1.0 - sig_gate))
         d_up = d_hidden * silu_gate
-        d_pre = jnp.concatenate([d_gate.astype(b16), d_up.astype(b16)], axis=2)
+        d_gate = d_gate.astype(b16)
+        d_up = d_up.astype(b16)
+        d_pre = jnp.concatenate([d_gate, d_up], axis=2)
         second_keep, second_send = pair_features(second, rows)
-        pre_pair = pair_tokens(d_pre, rows)
-        away_hid = grad_part(second_send, pre_pair).astype(b16)
-        came_hid = swap(away_hid, 2, rows)
+        gate_pair = pair_tokens(d_gate, rows)
+        up_pair = pair_tokens(d_up, rows)
+        away_gate = grad_part(second_send, gate_pair).astype(b16)
+        came_gate = swap(away_gate, 2, rows)
+        away_up = grad_part(second_send, up_pair).astype(b16)
+        came_up = swap(away_up, 2, rows)
         out_rows = (
             residual + jnp.einsum("ctn,cdn->td", hidden, down_w, preferred_element_type=f32)
         ).astype(b16)
-        d_second = jnp.einsum(
-            "ctn,cdn->td", after(d_pre, away_down), late_w_hid, preferred_element_type=f32
-        )
+        d_pre = after(d_pre, away_down)
+        d_second = jnp.einsum("ctn,cdn->td", d_pre, late_w_hid, preferred_element_type=f32)
         part_two = jnp.sum(d_second * normed_two, axis=0)
         scaled_two = d_second * gain_two
         mean_two = jnp.mean(scaled_two * normed_two, axis=1, keepdims=True)
         d_resid = cot.astype(f32) + inv_two * (scaled_two - normed_two * mean_two)
         d_low = d_resid.astype(b16)
-        d_low = after(d_low, away_hid)
+        d_low = after(d_low, away_gate)
         d_mixed = jnp.einsum("td,cdv->ctv", d_low, out_w, preferred_element_type=f32)
         gated = d_mixed * silu_out
         part_head = jnp.sum(gated * unit, axis=(0, 1))
@@ -418,7 +428,7 @@
         d_unit = gated * gain_head
         d_heads = inv_head * (d_unit - unit * jnp.mean(d_unit * unit, axis=-1, keepdims=True))
         d_gates = d_gates.astype(b16)
-        total_down = (grad_part(cot_keep, hidden_pair) + came_down.astype(f32)).astype(b16)
+        total_down = joined(grad_part(cot_keep, hidden_pair), came_down)
         d_attended = to_heads(d_heads.astype(b16), rows)
         low_keep, low_send = pair_features(d_low, rows)
         mixed_pair = pair_tokens(mixed, rows)
@@ -427,9 +437,11 @@
             [grad_part(low_send, mixed_pair), grad_part(first_send, gates_pair)], axis=2
         ).astype(b16)
         came_out = swap(away_out, 2, rows)
-        d_attended = after(d_attended, total_down, away_out)
-        d_packed = run_backward(info, packed, d_attended, states, rows)
+        d_attended = after(d_attended, total_down, away_up, away_out)
         grad_down = col_sum(total_down)
+        total_gate = joined(grad_part(second_keep, gate_pair), came_gate)
+        d_packed = run_backward(info, packed, d_attended, states, (total_gate,))
+        grad_gate = col_sum(total_gate)
         d_packed = to_tokens(d_packed, rows)
         d_zeta = d_packed[:, :, narrow:].astype(f32)
         d_proj = d_packed[:, :, :narrow]
@@ -476,23 +488,24 @@
         proj_pair = pair_tokens(d_proj, rows)
         away_first = grad_part(first_send, proj_pair).astype(b16)
         away_first = jnp.concatenate([away_first, side_send], axis=2)
-        total_hid = (grad_part(second_keep, pre_pair) + came_hid.astype(f32)).astype(b16)
-        grad_hid = col_sum(total_hid)
+        total_up = joined(grad_part(second_keep, up_pair), came_up)
+        grad_up = col_sum(total_up)
         held_out = jnp.concatenate(
             [grad_part(low_keep, mixed_pair), grad_part(first_keep, gates_pair)], axis=2
         )
-        total_out = (held_out + came_out.astype(f32)).astype(b16)
+        total_out = joined(held_out, came_out)
         grad_out = col_sum(total_out)
-        came_first = swap(after(away_first, total_hid), 2, rows)
+        came_first = swap(after(away_first, total_up, total_out), 2, rows)
         held_first = jnp.concatenate([grad_part(first_keep, proj_pair), side_keep], axis=2)
-        grad_first = col_sum((held_first + came_first.astype(f32)).astype(b16))
+        grad_first = col_sum(joined(held_first, came_first))
 
         out_rows = exchange(out_rows.reshape(count, rows, feat).transpose(1, 0, 2))
         grad_tokens = exchange(
             grad_tokens.astype(b16).reshape(count, rows, feat).transpose(1, 0, 2)
         )
         grad_down = batch_sum(grad_down, dp)
-        grad_hid = batch_sum(grad_hid, dp)
+        grad_gate = batch_sum(grad_gate, dp)
+        grad_up = batch_sum(grad_up, dp)
         grad_out = batch_sum(grad_out, dp)
         grad_first = batch_sum(grad_first, dp)
         side_sum = grad_first[:, narrow:]
@@ -510,8 +523,8 @@
             side_sum[:, 2 * RANK + 3],
             grad_out[:, :HV].T,
             side_sum[:, RANK + 1],
-            grad_hid[:, :hid],
-            grad_hid[:, hid:],
+            grad_gate,
+            grad_up,
             grad_down.T,
         )
 

time: 594 us -> 693 us (1.17)
  local copies, waits for them, and re-layouts: 80.4 us -> 156 us
  waiting for transfers between devices: 248 us -> 261 us
  matrix products: 117 us -> 124 us
    reshape x1 -> x5, local copies, waits for them, and re-layouts: 1.31 us -> 72.5 us  [the longest x1 36.3 us: gather_blocks(): return whole.reshape(cols, rows, block.shape[0], block.shape[1])]
    reduce_scatter x4 -> x5, waiting for transfers between devices: 28.5 us -> 0.03 us  [col_sum(): return lax.psum_scatter(total, 'col', scatter_dimension=0, tiled=True)]
    slice x1 -> x3, local copies, waits for them, and re-layouts: 0.27 us -> 18.6 us  [the longest x1 9.62 us: per_device(): late_w_hid = late_w[:, :, :2 * hid]]
    ppermute x2, waiting for transfers between devices: 14.1 us -> 29 us  [the longest x1 21.3 us: run_backward(): begin = lax.ppermute(end, 'row', [(2, 0), (3, 1)])]
    ppermute x18 -> x20, waiting for transfers between devices: 72.4 us -> 87 us  [swap(): return lax.ppermute(part, 'row', [(i, i ^ bit) for i in range(rows)])]
    all_gather x2, waiting for transfers between devices: 69.8 us -> 81.1 us  [gather_blocks(): whole = lax.all_gather(block, GRID, axis=0, tiled=True)]
    dot_general x10 -> x12, matrix products: 38.5 us -> 43.2 us  [grad_part(): jnp.einsum('td,ctn->cdn', features, blocks, preferred_element_type=f32)]
    unnamed x124 -> x142, local copies, waits for them, and re-layouts: 16.8 us -> 13.2 us
  transfers between devices with their start and end apart: 35 -> 39, of which waited for: 15 -> 20; matrix products, arithmetic and copies ran while one was open for 32% -> 28% of each run, Pallas kernels for 6% -> 5%
where the time goes in v4:
time: 693 us; the launch traced here: 684 us
  waiting for transfers between devices  261 us (38%)
  local copies, waits for them, and re-layouts  156 us (23%)
  matrix products  124 us (18%)
  other arithmetic  48.5 us (7%)
  starting transfers between devices  41.8 us (6%)
  Pallas kernels  37.3 us (5%)
  between operations  15.5 us (2%)
    ppermute x20, waiting for transfers between devices, swap(): return lax.ppermute(part, 'row', [(i, i ^ bit) for i in range(rows)])  87 us
    all_gather x2, waiting for transfers between devices, gather_blocks(): whole = lax.all_gather(block, GRID, axis=0, tiled=True)  81.1 us
    dot_general x12, matrix products, grad_part(): jnp.einsum('td,ctn->cdn', features, blocks, preferred_element_type=f32)  43.2 us
    all_to_all x4, waiting for transfers between devices, exchange(): return lax.all_to_all(blocks, 'row', 0, 0)  40.7 us
    pallas_call x4, Pallas kernels, run_mix(): pl.pallas_call(kernel, out_shape=results, grid_spec=pltpu.PrefetchScalarG...  37.3 us
    reshape x1, local copies, waits for them, and re-layouts, gather_blocks(): return whole.reshape(cols, rows, block.shape[0], block.shape[1])  36.3 us
    reshape x1, local copies, waits for them, and re-layouts, per_device(): late_w = late_w.reshape(cols, D, -1)  32.3 us
    ppermute x5, waiting for transfers between devices, batch_sum(): other = lax.ppermute(part, 'dp', [(0, 1), (1, 0)])  23.1 us
  transfers between devices with their start and end apart: 39, of which 20 were waited for; matrix products, arithmetic and copies ran while one was open for 28% of the time, Pallas kernels for 5%

profile of v4, /device:TPU:0, one launch (start us, length us, event | category | flops | bytes accessed | tf_op | source)
XLA Modules:
  0.0 683.5 jit_solution(7650289555609359376)
XLA Ops:
  19.1 17.9 %all-to-all-done = bf16[4,512,256]{2,1,0:T(8,128)(2,1)S(1)} async-done(((bf16[4,512,256]{2,1,0:T(8,128)(2,1)}), bf16[4,512,256]{2,1,0:T(8,128)(2,1)S(1)}, u32[]{:S(2)}, u32[]{:S(2)}) %all-to-all-start) | async-done | bytes 1048608 | tf_op jit(solution)/shard_map/all_to_all | solution.py:30
  37.8 36.1 %all-gather.3.cloned.1.call-done = bf16[4096,640]{1,0:T(8,128)(2,1)} async-done(((bf16[256,640]{1,0:T(8,128)(2,1)}), bf16[4096,640]{1,0:T(8,128)(2,1)}) %all-gather.3.cloned.1.call-update) | async-done | bytes 5242896 | tf_op jit(solution)/shard_map/all_gather | solution.py:218
  102.9 6.4 shard_map.288
  109.3 6.7 collective-permute-start.2
  120.8 7.7 %collective-permute-done.2.start_ref = f32[2,256,128]{2,1,0:T(8,128)S(1)} collective-permute-done((f32[2,256,128]{2,1,0:T(8,128)}, f32[2,256,128]{2,1,0:T(8,128)S(1)}, u32[]{:S(2)}, u32[]{:S(2)}) %collective-permute-start.2) | collective-permute-done | bytes 262176 | tf_op jit(solution)/shard_map/ppermute | solution.py:201
  129.3 9.7 %shard_map.289 = (bf16[2,2,512,256]{3,2,1,0:T(8,128)(2,1)}, bf16[2,2,8,256,128]{4,3,2,1,0:T(8,128)(2,1)}) custom-call(s32[8]{0:T(128)} %pad_add_fusion.info_ref, bf16[2,2,512,640]{3,2,1,0:T(8,128)(2,1)} %pad_maximum_fusion.13.x_ref, f32[2,256,128]{2,1,0:T(8,128)} %copy-done.56), custom_call_target="tpu_custom_call" | custom-call | flops 400000000 | bytes 8000000 | tf_op jit(solution)/shard_map/pallas_call | solution.py:181
  141.3 9.7 %all-to-all-done.1 = bf16[4,512,256]{2,1,0:T(8,128)(2,1)} async-done(((bf16[4,512,256]{2,1,0:T(8,128)(2,1)}), bf16[4,512,256]{2,1,0:T(8,128)(2,1)}, u32[]{:S(2)}, u32[]{:S(2)}) %all-to-all-start.1) | async-done | bytes 1048608 | tf_op jit(solution)/shard_map/all_to_all | solution.py:30
  164.6 45.0 %all-gather.5.cloned.1.call-done = bf16[4096,2688]{0,1:T(8,128)(2,1)} async-done(((bf16[256,2688]{0,1:T(8,128)(2,1)}), bf16[4096,2688]{0,1:T(8,128)(2,1)}) %all-gather.5.cloned.1.call-update) | async-done | bytes 22020112 | tf_op jit(solution)/shard_map/all_gather | solution.py:218
  209.7 36.3 %reshape.221 = bf16[4,4,256,2688]{2,1,0,3:T(4,128)(2,1)} reshape(bf16[4096,2688]{0,1:T(8,128)(2,1)} %all-gather.5.cloned.1.call-done) | data formatting | bytes 44040192 | tf_op jit(solution)/shard_map/reshape | solution.py:219
  246.0 32.3 %reshape.264 = bf16[4,1024,2688]{1,0,2:T(4,128)(2,1)} reshape(bf16[4,4,256,2688]{2,1,0,3:T(4,128)(2,1)} %reshape.221) | data formatting | bytes 44040192 | tf_op jit(solution)/shard_map/reshape | solution.py:373
  287.3 9.6 %slice.186 = bf16[4,1024,1408]{1,0,2:T(4,128)(2,1)S(1)} slice(bf16[4,1024,2688]{1,0,2:T(4,128)(2,1)} %reshape.264), slice={[0:4], [0:1024], [0:1408]} | slice | bytes 23068672 | tf_op jit(solution)/shard_map/slice | solution.py:375
  305.8 13.0 %fusion.4 = f32[4,512,1408]{1,2,0:T(8,128)} fusion(bf16[4,1024,1408]{1,0,2:T(4,128)(2,1)S(1)} %slice.186, bf16[512,1024]{1,0:T(8,128)(2,1)S(1)} %multiply_convert_fusion.2), kind=kOutput, calls=%fused_computation.4 | convolution fusion | flops 5905580032 | bytes 24117248 | tf_op jit(solution)/shard_map/td,cdn->ctn/dot_general | solution.py:390
  318.8 11.8 %fusion.9 = (bf16[4,512,704]{1,2,0:T(8,128)(2,1)}, bf16[4,512,704]{1,2,0:T(8,128)(2,1)}, bf16[4,512,704]{1,2,0:T(8,128)(2,1)}) fusion(f32[4,512,1408]{1,2,0:T(8,128)} %fusion.4, bf16[512,1024,1]{1,0,2:T(8,128)(2,1)S(1)} %copy-done.25, bf16[4,1024,704]{1,0,2:T(4,128)(2,1)S(1)} %slice.190), kind=kOutput, calls=%fused_computation.13 | convolution fusion | flops 2974416896 | bytes 27000832 | tf_op jit(solution)/shard_map/td,cdn->ctn/dot_general | solution.py:400
  349.6 17.8 %fusion.39 = (f32[1024]{0:T(1024)S(1)}, f32[512]{0:T(512)S(1)}, f32[512,1024,1]{1,0,2:T(8,128)S(1)}) fusion(f32[512,1024]{1,0:T(8,128)S(1)} %copy-done.1, f32[512]{0:T(512)S(1)} %add_rsqrt_fusion.1, f32[1024]{0:T(1024)S(1)} %get-tuple-element.107, bf16[4,512,1408]{1,2,0:T(8,128)(2,1)} %pad_maximum_fusion, bf16[4,1024,1408]{1,0,2:T(4,128)(2,1)S(1)} %bitcast.344), kind=kOutput, calls=%fused_computation.67 | convolution fusion | flops 5908724224 | bytes 21508096 | tf_op jit(solution)/shard_map/ctn,cdn->td/dot_general | solution.py:417
  389.7 20.5 %collective-permute-done.21 = bf16[4,256,512]{1,2,0:T(8,128)(2,1)S(1)} collective-permute-done((bf16[4,256,512]{1,2,0:T(8,128)(2,1)S(1)}, bf16[4,256,512]{1,2,0:T(8,128)(2,1)S(1)}, u32[]{:S(2)}, u32[]{:S(2)}) %collective-permute-start.21) | collective-permute-done | bytes 1048608 | tf_op jit(solution)/shard_map/ppermute | solution.py:230
  420.6 28.2 %collective-permute-done.16 = bf16[4,256,704]{1,2,0:T(8,128)(2,1)} collective-permute-done((bf16[4,256,704]{1,2,0:T(8,128)(2,1)}, bf16[4,256,704]{1,2,0:T(8,128)(2,1)}, u32[]{:S(2)}, u32[]{:S(2)}) %collective-permute-start.16) | collective-permute-done | bytes 1441824 | tf_op jit(solution)/shard_map/ppermute | solution.py:230
  464.4 15.2 %collective-permute-done.10 = bf16[4,256,704]{1,2,0:T(8,128)(2,1)} collective-permute-done((bf16[4,256,704]{1,2,0:T(8,128)(2,1)}, bf16[4,256,704]{1,2,0:T(8,128)(2,1)}, u32[]{:S(2)}, u32[]{:S(2)}) %collective-permute-start.10) | collective-permute-done | bytes 1441824 | tf_op jit(solution)/shard_map/ppermute | solution.py:230
  485.7 6.5 shard_map.290
  493.4 21.3 %collective-permute-done.15.start_ref = f32[2,256,128]{2,1,0:T(8,128)} collective-permute-done((f32[2,256,128]{2,1,0:T(8,128)}, f32[2,256,128]{2,1,0:T(8,128)}, u32[]{:S(2)}, u32[]{:S(2)}) %collective-permute-start.15) | collective-permute-done | bytes 262176 | tf_op jit(solution)/shard_map/ppermute | solution.py:211
  514.7 14.8 %shard_map.291 = bf16[2,2,512,640]{3,2,1,0:T(8,128)(2,1)} custom-call(s32[8]{0:T(128)} %pad_add_fusion.info_ref, bf16[2,2,512,640]{3,2,1,0:T(8,128)(2,1)} %pad_maximum_fusion.13.x_ref, bf16[2,2,512,256]{3,2,1,0:T(8,128)(2,1)} %pad_maximum_fusion.59.do_ref, bf16[2,2,8,256,128]{4,3,2,1,0:T(8,128)(2,1)} %get-tuple-element.31.states_ref, ...), custom_call_target="tpu_custom_call" | custom-call | flops 800000000 | bytes 16000000 | tf_op jit(solution)/shard_map/pallas_call | solution.py:181
  590.8 16.4 %collective-permute-done.22 = bf16[4,256,640]{1,2,0:T(8,128)(2,1)} collective-permute-done((bf16[4,256,640]{1,2,0:T(8,128)(2,1)}, bf16[4,256,640]{1,2,0:T(8,128)(2,1)}, u32[]{:S(2)}, u32[]{:S(2)}) %collective-permute-start.22) | collective-permute-done | bytes 1310752 | tf_op jit(solution)/shard_map/ppermute | solution.py:230
  622.6 12.8 %all-to-all-done.3 = bf16[4,512,256]{2,1,0:T(8,128)(2,1)S(1)} async-done(((bf16[4,512,256]{2,1,0:T(8,128)(2,1)}), bf16[4,512,256]{2,1,0:T(8,128)(2,1)S(1)}, u32[]{:S(2)}, u32[]{:S(2)}) %all-to-all-start.3) | async-done | bytes 1048608 | tf_op jit(solution)/shard_map/all_to_all | solution.py:30
  642.2 6.3 collective-permute-done.25
  657.1 6.8 collective-permute-done.27
  (342 shorter events, 259.2 us)
Async XLA Ops:
  7.2 66.7 %all-gather.3.cloned.1.call-start = ((), (), s32[]{:S(2)}) async-start(), calls=%async_computation.9 | async-start | bytes 5570560 | tf_op jit(solution)/shard_map/all_gather | solution.py:218
  12.5 197.2 %all-gather.5.cloned.1.call-start = ((), (), s32[]{:S(2)}) async-start(), calls=%async_computation.10 | async-start | bytes 23396352 | tf_op jit(solution)/shard_map/all_gather | solution.py:218
  14.9 22.2 %all-to-all-start = ((bf16[4,512,256]{2,1,0:T(8,128)(2,1)}), bf16[4,512,256]{2,1,0:T(8,128)(2,1)S(1)}, u32[]{:S(2)}, u32[]{:S(2)}) async-start(bf16[4,512,256]{2,1,0:T(8,128)(2,1)} %bitcast.362), calls=%async_computation | async-start | bytes 2097152 | tf_op jit(solution)/shard_map/all_to_all | solution.py:30
  116.0 34.9 %all-to-all-start.1 = ((bf16[4,512,256]{2,1,0:T(8,128)(2,1)}), bf16[4,512,256]{2,1,0:T(8,128)(2,1)}, u32[]{:S(2)}, u32[]{:S(2)}) async-start(bf16[4,512,256]{2,1,0:T(8,128)(2,1)} %bitcast.363), calls=%async_computation.1 | async-start | bytes 2097152 | tf_op jit(solution)/shard_map/all_to_all | solution.py:30
  120.3 500.8 %reduce-scatter.8.cloned.1.call-start = ((), (), s32[]{:S(2)}) async-start(), calls=%async_computation.12 | async-start | bytes 1310720 | tf_op jit(solution)/shard_map/reduce_scatter | solution.py:277
  334.6 44.4 %collective-permute-start.5 = (bf16[2,512,256]{2,1,0:T(8,128)(2,1)}, bf16[2,512,256]{2,1,0:T(8,128)(2,1)}, u32[]{:S(2)}, u32[]{:S(2)}) collective-permute-start(bf16[2,512,256]{2,1,0:T(8,128)(2,1)} %pad_maximum_fusion.64), channel_id=1, source_target_pairs={{0,4},{4,0},{8,12},{12,8},{1,5},{5,1},{9,13},{13,9},{2,6},{6,2},{1... | collective-permute-start | bytes 1572872 | tf_op jit(solution)/shard_map/ppermute | solution.py:230
  337.5 44.1 %collective-permute-start.12 = (bf16[4,512,256]{1,2,0:T(8,128)(2,1)}, bf16[4,512,256]{1,2,0:T(8,128)(2,1)}, u32[]{:S(2)}, u32[]{:S(2)}) collective-permute-start(bf16[4,512,256]{1,2,0:T(8,128)(2,1)} %get-tuple-element.156), channel_id=1, source_target_pairs={{0,4},{4,0},{8,12},{12,8},{1,5},{5,1},{9,13},{13,9},{2,6},{6,2},{1... | collective-permute-start | bytes 3145736 | tf_op jit(solution)/shard_map/ppermute | solution.py:230
  337.8 30.9 %collective-permute-start.7 = (bf16[4,512,704]{1,2,0:T(8,128)(2,1)S(1)}, bf16[4,512,704]{1,2,0:T(8,128)(2,1)}, u32[]{:S(2)}, u32[]{:S(2)}) collective-permute-start(bf16[4,512,704]{1,2,0:T(8,128)(2,1)S(1)} %copy-done.16), channel_id=1, source_target_pairs={{0,4},{4,0},{8,12},{12,8},{1,5},{5,1},{9,13},{13,9},{2,6},{6,2},{1... | collective-permute-start | bytes 8650760 | tf_op jit(solution)/shard_map/ppermute | solution.py:230
  384.7 25.5 %collective-permute-start.21 = (bf16[4,256,512]{1,2,0:T(8,128)(2,1)S(1)}, bf16[4,256,512]{1,2,0:T(8,128)(2,1)S(1)}, u32[]{:S(2)}, u32[]{:S(2)}) collective-permute-start(bf16[4,256,512]{1,2,0:T(8,128)(2,1)S(1)} %pad_maximum_fusion.60), channel_id=1, source_target_pairs={{0,8},{4,12},{8,0},{12,4},{1,9},{5,13},{9,1},{13,5},{2,10},{6,14},... | collective-permute-start | bytes 3145736 | tf_op jit(solution)/shard_map/ppermute | solution.py:230
  386.7 68.3 %collective-permute-start.11 = (bf16[4,512,704]{1,2,0:T(8,128)(2,1)}, bf16[4,512,704]{1,2,0:T(8,128)(2,1)}, u32[]{:S(2)}, u32[]{:S(2)}) collective-permute-start(bf16[4,512,704]{1,2,0:T(8,128)(2,1)} %get-tuple-element.112), channel_id=1, source_target_pairs={{0,4},{4,0},{8,12},{12,8},{1,5},{5,1},{9,13},{13,9},{2,6},{6,2},{1... | collective-permute-start | bytes 8650760 | tf_op jit(solution)/shard_map/ppermute | solution.py:230
  413.8 223.2 %reduce-scatter.10.cloned.1.call-start = ((), (), s32[]{:S(2)}) async-start(), calls=%async_computation.13 | async-start | bytes 1802240 | tf_op jit(solution)/shard_map/reduce_scatter | solution.py:277
  413.9 34.8 %collective-permute-start.16 = (bf16[4,256,704]{1,2,0:T(8,128)(2,1)}, bf16[4,256,704]{1,2,0:T(8,128)(2,1)}, u32[]{:S(2)}, u32[]{:S(2)}) collective-permute-start(bf16[4,256,704]{1,2,0:T(8,128)(2,1)} %fusion.67), channel_id=1, source_target_pairs={{0,8},{4,12},{8,0},{12,4},{1,9},{5,13},{9,1},{13,5},{2,10},{6,14},... | collective-permute-start | bytes 4325384 | tf_op jit(solution)/shard_map/ppermute | solution.py:230
  415.7 63.9 %collective-permute-start.10 = (bf16[4,256,704]{1,2,0:T(8,128)(2,1)}, bf16[4,256,704]{1,2,0:T(8,128)(2,1)}, u32[]{:S(2)}, u32[]{:S(2)}) collective-permute-start(bf16[4,256,704]{1,2,0:T(8,128)(2,1)} %fusion.68), channel_id=1, source_target_pairs={{0,8},{4,12},{8,0},{12,4},{1,9},{5,13},{9,1},{13,5},{2,10},{6,14},... | collective-permute-start | bytes 4325384 | tf_op jit(solution)/shard_map/ppermute | solution.py:230
  420.6 41.8 %collective-permute-start.9 = (bf16[2,512,256]{2,1,0:T(8,128)(2,1)}, bf16[2,512,256]{2,1,0:T(8,128)(2,1)}, u32[]{:S(2)}, u32[]{:S(2)}) collective-permute-start(bf16[2,512,256]{2,1,0:T(8,128)(2,1)} %get-tuple-element.141), channel_id=1, source_target_pairs={{0,4},{4,0},{8,12},{12,8},{1,5},{5,1},{9,13},{13,9},{2,6},{6,2},{1... | collective-permute-start | bytes 1572872 | tf_op jit(solution)/shard_map/ppermute | solution.py:230
  454.8 183.7 %reduce-scatter.12.cloned.1.call-start = ((), (), s32[]{:S(2)}) async-start(), calls=%async_computation.14 | async-start | bytes 1802240 | tf_op jit(solution)/shard_map/reduce_scatter | solution.py:277
  460.6 80.8 %collective-permute-start.20 = (bf16[4,256,704]{1,2,0:T(8,128)(2,1)}, bf16[4,256,704]{1,2,0:T(8,128)(2,1)}, u32[]{:S(2)}, u32[]{:S(2)}) collective-permute-start(bf16[4,256,704]{1,2,0:T(8,128)(2,1)} %fusion.66), channel_id=1, source_target_pairs={{0,8},{4,12},{8,0},{12,4},{1,9},{5,13},{9,1},{13,5},{2,10},{6,14},... | collective-permute-start | bytes 4325384 | tf_op jit(solution)/shard_map/ppermute | solution.py:230
  492.1 22.6 %collective-permute-start.15 = (f32[2,256,128]{2,1,0:T(8,128)}, f32[2,256,128]{2,1,0:T(8,128)}, u32[]{:S(2)}, u32[]{:S(2)}) collective-permute-start(f32[2,256,128]{2,1,0:T(8,128)} %shard_map.290), channel_id=1, source_target_pairs={{8,0},{12,4},{9,1},{13,5},{10,2},{14,6},{11,3},{15,7},{24,16},{28,... | collective-permute-start | bytes 786440 | tf_op jit(solution)/shard_map/ppermute | solution.py:211
  547.4 91.6 %reduce-scatter.14.cloned.1.call-start = ((), (), s32[]{:S(2)}) async-start(), calls=%async_computation.15 | async-start | bytes 1802240 | tf_op jit(solution)/shard_map/reduce_scatter | solution.py:277
  575.2 32.0 %collective-permute-start.22 = (bf16[4,256,640]{1,2,0:T(8,128)(2,1)}, bf16[4,256,640]{1,2,0:T(8,128)(2,1)}, u32[]{:S(2)}, u32[]{:S(2)}) collective-permute-start(bf16[4,256,640]{1,2,0:T(8,128)(2,1)} %pad_maximum_fusion.50), channel_id=1, source_target_pairs={{0,8},{4,12},{8,0},{12,4},{1,9},{5,13},{9,1},{13,5},{2,10},{6,14},... | collective-permute-start | bytes 3932168 | tf_op jit(solution)/shard_map/ppermute | solution.py:230
  582.6 34.9 %all-to-all-start.2 = ((bf16[4,512,256]{2,1,0:T(8,128)(2,1)}), bf16[4,512,256]{2,1,0:T(8,128)(2,1)}, u32[]{:S(2)}, u32[]{:S(2)}) async-start(bf16[4,512,256]{2,1,0:T(8,128)(2,1)} %bitcast.359), calls=%async_computation.2 | async-start | bytes 2097152 | tf_op jit(solution)/shard_map/all_to_all | solution.py:30
  586.9 62.6 %reduce-scatter.6.cloned.1.call-start = ((), (), s32[]{:S(2)}) async-start(), calls=%async_computation.11 | async-start | bytes 1638400 | tf_op jit(solution)/shard_map/reduce_scatter | solution.py:277
  621.1 19.4 %collective-permute-start.24 = (bf16[256,512]{1,0:T(8,128)(2,1)}, bf16[256,512]{1,0:T(8,128)(2,1)S(1)}, u32[]{:S(2)}, u32[]{:S(2)}) collective-permute-start(bf16[256,512]{1,0:T(8,128)(2,1)} %reduce-scatter.8.cloned.1.call-done), channel_id=1, source_target_pairs={{0,16},{16,0},{1,17},{17,1},{2,18},{18,2},{3,19},{19,3},{4,20},{20... | collective-permute-start | bytes 786440 | tf_op jit(solution)/shard_map/ppermute | solution.py:224
  639.0 24.9 %collective-permute-start.27 = (bf16[256,704]{0,1:T(8,128)(2,1)}, bf16[256,704]{0,1:T(8,128)(2,1)S(1)}, u32[]{:S(2)}, u32[]{:S(2)}) collective-permute-start(bf16[256,704]{0,1:T(8,128)(2,1)} %reduce-scatter.14.cloned.1.call-done), channel_id=1, source_target_pairs={{0,16},{16,0},{1,17},{17,1},{2,18},{18,2},{3,19},{19,3},{4,20},{20... | collective-permute-start | bytes 1081352 | tf_op jit(solution)/shard_map/ppermute | solution.py:224
  649.4 20.2 %collective-permute-start.23 = (bf16[256,640]{1,0:T(8,128)(2,1)}, bf16[256,640]{1,0:T(8,128)(2,1)S(1)}, u32[]{:S(2)}, u32[]{:S(2)}) collective-permute-start(bf16[256,640]{1,0:T(8,128)(2,1)} %reduce-scatter.6.cloned.1.call-done), channel_id=1, source_target_pairs={{0,16},{16,0},{1,17},{17,1},{2,18},{18,2},{3,19},{19,3},{4,20},{20... | collective-permute-start | bytes 983048 | tf_op jit(solution)/shard_map/ppermute | solution.py:224
  (80 other events, 996.3 us)
Sparse Core Ops, SparseCore 0:
  12.6 61.2 all-gather.2
  75.4 134.2 all-gather.4
  414.0 26.8 reduce-scatter.7
  454.9 32.9 reduce-scatter.9
  547.5 32.0 reduce-scatter.11
  581.8 32.0 reduce-scatter.13
  616.2 30.1 reduce-scatter.5
